TPU v7x, 128 devices: a whole 4x4x4 slice. The times are simulated.
128 devices in a mesh: comp: 4 (over x), blk: 32 (over y, z, core).
Axes of the slice: x: 4, y: 4, z: 4, core: 2. Of those that a mesh axis runs over, the one named last changes fastest.
Arguments:
- psi_start: float32 [4, 6, 256, 128, 128], P('comp', None, 'blk'), may hold values from -6 to 6
- adj_source: float32 [4, 6, 256, 128, 128], P('comp', None, 'blk'), may hold values from -6 to 6
- vol_inverse: float32 [4, 256, 128, 128], P('comp', 'blk'), may hold values from 0.5 to 2
- coupling: float32 [4, 6, 6, 6], P('comp'), may hold values from -0.6 to 0.65
- send_tile: int32 [128, 128, 8], P(('comp', 'blk')), may hold values from 0 to 1023
- send_count: int32 [128, 128], P(('comp', 'blk')), may hold values from 0 to 8, as said below
- send_weight: float32 [128, 128, 8], P(('comp', 'blk')), may hold values from 0.2 to 1
- recv_slot: int32 [128, 128, 8], P(('comp', 'blk')), may hold values from 0 to 63
- fringe_row: int32 [128, 64], P(('comp', 'blk')), may hold values from 0 to 1023, as said below
Outputs:
- psi_end: float32 [4, 6, 256, 128, 128], P('comp', None, 'blk')
Inputs may be any that keep to these rules, and one draw needn't show every extreme that they name: `send_count`: no tiles travel between devices of the same component; between devices of different components the count is 4 or more. In every draw one receiver gets 8 live entries from every device of the other components. `fringe_row`: the rows of one device's fringe slots are distinct.
All inputs are finite; a program needn't handle non-finite values.
Results may differ from a plain program's by a relative error of at most 0.0003.
Values sent between devices are 32-bit elements; how exact they have to be, the bound alone decides.
No kernel may reach another device: no remote copies, remote signals or barrier semaphores. Data moves between devices by JAX's collectives and lax.ppermute only.
A program may use at most 128 MiB of HBM per device.

v0:
```python
import jax
import jax.numpy as jnp
from jax import lax
from jax.sharding import PartitionSpec as P

PENALTY = 4.0
TIME_STEP = 0.08


def padded(cells, sides, width):
    for axis, dim in sides:
        count = lax.axis_size(axis)
        ends = count - 1
        head = lax.slice_in_dim(cells, 0, width, axis=dim)
        tail = lax.slice_in_dim(cells, cells.shape[dim] - width, cells.shape[dim], axis=dim)
        cells = jnp.concatenate(
            [
                lax.ppermute(tail, axis, [(i, (i + 1) % count) for i in range(ends)]),
                cells,
                lax.ppermute(head, axis, [((i + 1) % count, i) for i in range(ends)]),
            ],
            axis=dim,
        )
    return cells


def fringe_values(field, send_tile, send_count, send_weight, recv_slot, count_slots):
    nvar, depth, width, length = field.shape
    flat = field.reshape(nvar, depth * width, length)
    peers, capacity = send_tile.shape
    picked = jnp.take(flat, send_tile.reshape(-1), axis=1)
    live = lax.broadcasted_iota(jnp.int32, (peers, capacity), 1) < send_count.reshape(peers, 1)
    scale = jnp.where(live, send_weight, 0.0).reshape(-1)
    outgoing = (picked * scale[None, :, None]).reshape(nvar, peers, capacity, length)
    arrived = lax.all_to_all(outgoing, ("comp", "blk"), split_axis=1, concat_axis=1, tiled=True)
    arrived = arrived.reshape(nvar, peers * capacity, length)
    slot_ids = lax.broadcasted_iota(jnp.int32, (count_slots, 1), 0)
    onehot = (recv_slot.reshape(1, -1) == slot_ids).astype(jnp.float32)
    return jnp.einsum("sk,vkz->vsz", onehot, arrived, precision=lax.Precision.HIGHEST)


def apply_block(matrix, values):
    return jnp.einsum("vu,vxyz->uxyz", matrix, values, precision=lax.Precision.HIGHEST)


def residual_of(field, volume, source, matrices, interp, rows):
    nvar, depth, width, length = field.shape
    extended = padded(field, (("blk", 1),), 1)
    zero_y = jnp.zeros((nvar, depth, 1, length), jnp.float32)
    zero_z = jnp.zeros((nvar, depth, width, 1), jnp.float32)
    flux = apply_block(-jnp.sum(matrices, axis=0), field)
    flux = flux + apply_block(matrices[0], extended[:, 2:])
    flux = flux + apply_block(matrices[1], extended[:, :-2])
    flux = flux + apply_block(matrices[2], jnp.concatenate([field[:, :, 1:], zero_y], axis=2))
    flux = flux + apply_block(matrices[3], jnp.concatenate([zero_y, field[:, :, :-1]], axis=2))
    flux = flux + apply_block(matrices[4], jnp.concatenate([field[:, :, :, 1:], zero_z], axis=3))
    flux = flux + apply_block(matrices[5], jnp.concatenate([zero_z, field[:, :, :, :-1]], axis=3))
    rate = volume[None] * flux + source
    rate_flat = rate.reshape(nvar, depth * width, length)
    field_flat = field.reshape(nvar, depth * width, length)
    rate_flat = rate_flat.at[:, rows, :].add(PENALTY * (interp - field_flat[:, rows, :]))
    return rate_flat.reshape(nvar, depth, width, length)


def shards(
    psi_start,
    adj_source,
    vol_inverse,
    coupling,
    send_tile,
    send_count,
    send_weight,
    recv_slot,
    fringe_row,
):
    start = psi_start[0]
    source = adj_source[0]
    volume = vol_inverse[0]
    matrices = coupling[0]
    rows = fringe_row[0]

    def rate_of(field):
        interp = fringe_values(
            field, send_tile[0], send_count[0], send_weight[0], recv_slot[0], rows.shape[0]
        )
        return residual_of(field, volume, source, matrices, interp, rows)

    first = rate_of(start)
    middle = start + TIME_STEP * first
    second = rate_of(middle)
    result = start + 0.5 * TIME_STEP * (first + second)
    return result[None]


def solution(mesh):
    in_specs = (
        P("comp", None, "blk", None, None),
        P("comp", None, "blk", None, None),
        P("comp", "blk", None, None),
        P("comp", None, None, None),
        P(("comp", "blk"), None, None),
        P(("comp", "blk"), None),
        P(("comp", "blk"), None, None),
        P(("comp", "blk"), None, None),
        P(("comp", "blk"), None),
    )
    out_specs = P("comp", None, "blk", None, None)
    return jax.shard_map(shards, mesh=mesh, in_specs=in_specs, out_specs=out_specs, check_vma=False)
```

profile of v0, /device:TPU:1, one launch (start us, length us, event | category | flops | bytes accessed | tf_op | source)
XLA Modules:
  0.0 279.5 jit_solution(5447209523548036402)
XLA Ops:
  0.0 3.7 %copy.188 = f32[1,6,8,128,128]{4,1,3,2,0:T(8,128)S(1)} copy(f32[1,6,8,128,128]{4,3,2,1,0:T(8,128)} %param.11) | data formatting | bytes 6291456 | tf_op args[0]
  6.8 3.3 %collective-permute-start = (f32[6,1,128,128]{3,0,2,1:T(8,128)}, f32[6,1,128,128]{3,0,2,1:T(8,128)}, u32[]{:S(2)}, u32[]{:S(2)}) collective-permute-start(f32[6,1,128,128]{3,0,2,1:T(8,128)} %get-tuple-element.13), channel_id=1, source_target_pairs={{1,0},{2,1},{3,2},{4,3},{5,4},{6,5},{7,6},{8,7},{9,8},{10,9},{11,1... | collective-permute-start | bytes 1179656 | tf_op jit(solution)/shard_map/ppermute | solution.py:20
  10.1 3.5 %collective-permute-start.1 = (f32[6,1,128,128]{3,0,2,1:T(8,128)}, f32[6,1,128,128]{3,0,2,1:T(8,128)}, u32[]{:S(2)}, u32[]{:S(2)}) collective-permute-start(f32[6,1,128,128]{3,0,2,1:T(8,128)} %get-tuple-element.12), channel_id=1, source_target_pairs={{0,1},{1,2},{2,3},{3,4},{4,5},{5,6},{6,7},{7,8},{8,9},{9,10},{10,1... | collective-permute-start | bytes 1179656 | tf_op jit(solution)/shard_map/ppermute | solution.py:18
  14.3 10.4 %gather_fusion.2 = f32[1024,6,128]{2,1,0:T(8,128)} fusion(f32[6,1024,128]{2,0,1:T(8,128)} %bitcast.179, s32[1024]{0:T(1024)S(1)} %fusion.81), kind=kCustom, calls=%fused_computation.clone | custom fusion | bytes 6295552 | tf_op jit(solution)/shard_map/jit(_take)/gather | solution.py:31
  24.7 7.3 %bitcast_multiply_fusion.1 = f32[6,1024,128]{2,0,1:T(8,128)S(1)} fusion(f32[1024,6,128]{2,1,0:T(8,128)} %gather_fusion.2, f32[1024]{0:T(1024)S(1)} %broadcast_select_fusion, pred[1024]{0:T(1024)(128)(4,1)S(1)} %compare_and_fusion), kind=kLoop, calls=%fused_computation.32 | loop fusion | flops 1572864 | bytes 6296576 | tf_op jit(solution)/shard_map/mul | solution.py:34
  34.4 12.5 %all-to-all-start = ((f32[6,128,8,128]{3,2,0,1:T(8,128)}), f32[6,128,8,128]{3,2,0,1:T(8,128)}, u32[]{:S(2)}, u32[]{:S(2)}) async-start(f32[6,128,8,128]{3,2,0,1:T(8,128)} %copy.85), calls=%async_computation | async-start | bytes 6291456 | tf_op jit(solution)/shard_map/all_to_all | solution.py:35
  46.9 7.0 %fusion.94 = (f32[6,8,128,127]{3,0,2,1:T(8,128)}, f32[6,8,128,127]{3,0,2,1:T(8,128)S(1)}) fusion(f32[6,8,128,128]{3,0,2,1:T(8,128)} %bitcast.180), kind=kLoop, calls=%fused_computation.112 | loop fusion | bytes 12484608 | tf_op jit(solution)/shard_map/slice | solution.py:56
  53.9 5.2 %fusion.31 = f32[8,128,128,6]{2,3,1,0:T(8,128)} fusion(f32[6,8,128,128]{3,0,2,1:T(8,128)S(1)} %bitcast.184, f32[1,1,6,6]{3,0,2,1:T(1,128)S(1)} %get-tuple-element.20), kind=kOutput, calls=%fused_computation.53 | convolution fusion | flops 56180736 | bytes 7310336 | tf_op jit(solution)/shard_map/vu,vxyz->uxyz/dot_general | solution.py:43
  59.1 5.7 %fusion.23 = f32[8,128,128,6]{2,3,1,0:T(8,128)} fusion(f32[6,8,128,127]{3,0,2,1:T(8,128)S(1)} %get-tuple-element.15, f32[1,1,6,6]{3,0,2,1:T(1,128)S(1)} %get-tuple-element.23), kind=kOutput, calls=%fused_computation.45 | convolution fusion | flops 56623104 | bytes 6267024 | tf_op jit(solution)/shard_map/vu,vxyz->uxyz/dot_general | solution.py:43
  64.9 8.0 %fusion.33 = f32[8,128,128,6]{2,3,1,0:T(8,128)} fusion(f32[6,8,128,128]{3,0,2,1:T(8,128)} %bitcast.181, f32[1,1,6,6]{3,0,2,1:T(1,128)S(1)} %get-tuple-element.21), kind=kOutput, calls=%fused_computation.55 | convolution fusion | flops 56180736 | bytes 7307408 | tf_op jit(solution)/shard_map/vu,vxyz->uxyz/dot_general | solution.py:43
  72.9 7.4 %fusion.70 = f32[6,8,128,128]{3,0,2,1:T(8,128)} fusion(f32[1,6,8,128,128]{4,3,2,1,0:T(8,128)S(1)} %copy-done.4, f32[6,6]{1,0:T(8,128)S(1)} %reduce_sum.8), kind=kOutput, calls=%fused_computation.76 | convolution fusion | flops 56623140 | bytes 6291600 | tf_op jit(solution)/shard_map/vu,vxyz->uxyz/dot_general | solution.py:43
  80.3 5.3 %fusion.25 = f32[8,128,128,6]{2,3,1,0:T(8,128)} fusion(f32[6,8,128,127]{3,0,2,1:T(8,128)S(1)} %copy-done.6, f32[1,1,6,6]{3,0,2,1:T(1,128)S(1)} %get-tuple-element.19), kind=kOutput, calls=%fused_computation.47 | convolution fusion | flops 56623104 | bytes 6267024 | tf_op jit(solution)/shard_map/vu,vxyz->uxyz/dot_general | solution.py:43
  88.7 8.2 %fusion = f32[8,128,128,6]{2,3,1,0:T(8,128)} fusion(f32[6,1,128,128]{3,0,2,1:T(8,128)} %collective-permute-done, f32[6,8,128,128]{3,0,2,1:T(8,128)} %bitcast.183, f32[1,1,6,6]{3,0,2,1:T(1,128)S(1)} %get-tuple-element.22), kind=kOutput, calls=%fused_computation.6 | convolution fusion | flops 57507840 | bytes 6684816 | tf_op jit(solution)/shard_map/vu,vxyz->uxyz/dot_general | solution.py:43
  96.8 15.9 %bitcast_add_fusion.7 = f32[6,8,128,128]{3,0,2,1:T(8,128)} fusion(f32[1,6,8,128,128]{4,3,2,1,0:T(8,128)S(1)} %copy-done.5, f32[8,128,128,6]{2,3,1,0:T(8,128)} %fusion.23, f32[8,128,128,6]{2,3,1,0:T(8,128)} %fusion.25, f32[8,128,128,6]{2,3,1,0:T(8,128)} %fusion.31, f32[8,128,128,6]{2,3,1,0:T(8,128)} %fusion.33, f32[6,8,128,128]{3,0,2,1:T(8,128)} %fusion.70, ...), kind=kOutput, calls=%fused_computation.33 | convolution fusion | flops 63799296 | bytes 29229200 | tf_op jit(solution)/shard_map/vu,vxyz->uxyz/dot_general | solution.py:43
  112.8 3.2 %fusion.66 = f32[64,6,128]{2,0,1:T(8,128)S(1)} fusion(f32[6,128,8,128]{3,2,0,1:T(8,128)} %all-to-all-done, f32[64,6,128]{2,1,0:T(8,128)S(1)} %gather_fusion, s32[1024]{0:T(1024)S(1)} %eq.8), kind=kOutput, calls=%fused_computation.73 | convolution fusion | flops 604143616 | bytes 3543040 | tf_op jit(solution)/shard_map/sk,vkz->vsz/dot_general | solution.py:39
  116.1 6.8 %scatter_fusion = f32[6,1024,128]{2,0,1:T(8,128)} fusion(f32[6,1024,128]{2,0,1:T(8,128)} %bitcast.186, s32[64]{0:T(128)S(1)} %fusion.82, f32[64,6,128]{2,1,0:T(8,128)S(1)} %copy.89), kind=kCustom, calls=%fused_computation.4 | custom fusion | flops 49152 | bytes 590080 | tf_op jit(solution)/shard_map/scatter-add | solution.py:61
  129.1 5.4 %fusion.27 = f32[8,128,128,6]{2,3,1,0:T(8,128)} fusion(f32[6,8,128,128]{3,0,2,1:T(8,128)S(1)} %fusion.69, f32[1,1,6,6]{3,0,2,1:T(1,128)S(1)} %get-tuple-element.20), kind=kOutput, calls=%fused_computation.49 | convolution fusion | flops 56180736 | bytes 7310336 | tf_op jit(solution)/shard_map/vu,vxyz->uxyz/dot_general | solution.py:43
  134.5 5.1 %fusion.29 = f32[8,128,128,6]{2,3,1,0:T(8,128)} fusion(f32[6,8,128,128]{3,0,2,1:T(8,128)S(1)} %fusion.69, f32[1,1,6,6]{3,0,2,1:T(1,128)S(1)} %get-tuple-element.21), kind=kOutput, calls=%fused_computation.51 | convolution fusion | flops 56180736 | bytes 7310336 | tf_op jit(solution)/shard_map/vu,vxyz->uxyz/dot_general | solution.py:43
  139.6 5.8 %fusion.76 = f32[6,8,128,128]{3,0,2,1:T(8,128)} fusion(f32[6,8,128,128]{3,0,2,1:T(8,128)S(1)} %fusion.69, f32[6,6]{1,0:T(8,128)S(1)} %reduce_sum.8), kind=kOutput, calls=%fused_computation.90 | convolution fusion | flops 56623140 | bytes 6291600 | tf_op jit(solution)/shard_map/vu,vxyz->uxyz/dot_general | solution.py:43
  145.4 2.8 %collective-permute-start.2 = (f32[6,1,128,128]{3,0,2,1:T(8,128)S(1)}, f32[6,1,128,128]{3,0,2,1:T(8,128)S(1)}, u32[]{:S(2)}, u32[]{:S(2)}) collective-permute-start(f32[6,1,128,128]{3,0,2,1:T(8,128)S(1)} %get-tuple-element.9), channel_id=1, source_target_pairs={{1,0},{2,1},{3,2},{4,3},{5,4},{6,5},{7,6},{8,7},{9,8},{10,9},{11,1... | collective-permute-start | bytes 1179656 | tf_op jit(solution)/shard_map/ppermute | solution.py:20
  148.2 5.3 %fusion.21 = f32[8,128,128,6]{2,3,1,0:T(8,128)} fusion(f32[6,8,128,127]{3,0,2,1:T(8,128)S(1)} %get-tuple-element.10, f32[1,1,6,6]{3,0,2,1:T(1,128)S(1)} %get-tuple-element.19), kind=kOutput, calls=%fused_computation.43 | convolution fusion | flops 56623104 | bytes 6267024 | tf_op jit(solution)/shard_map/vu,vxyz->uxyz/dot_general | solution.py:43
  156.3 5.9 %fusion.19 = f32[8,128,128,6]{2,3,1,0:T(8,128)} fusion(f32[6,8,128,127]{3,0,2,1:T(8,128)S(1)} %get-tuple-element.11, f32[1,1,6,6]{3,0,2,1:T(1,128)S(1)} %get-tuple-element.23), kind=kOutput, calls=%fused_computation.41 | convolution fusion | flops 56623104 | bytes 6267024 | tf_op jit(solution)/shard_map/vu,vxyz->uxyz/dot_general | solution.py:43
  162.2 5.8 %fusion.8 = f32[8,128,128,6]{2,3,1,0:T(8,128)} fusion(f32[6,1,128,128]{3,0,2,1:T(8,128)S(1)} %collective-permute-done.2, f32[6,8,128,128]{3,0,2,1:T(8,128)S(1)} %fusion.69, f32[1,1,6,6]{3,0,2,1:T(1,128)S(1)} %get-tuple-element.22), kind=kOutput, calls=%fused_computation.14 | convolution fusion | flops 57507840 | bytes 6684816 | tf_op jit(solution)/shard_map/vu,vxyz->uxyz/dot_general | solution.py:43
  168.1 14.1 %fusion.17 = f32[6,8,128,128]{3,0,2,1:T(8,128)} fusion(f32[8,128,128,6]{2,3,1,0:T(8,128)} %fusion.19, f32[8,128,128,6]{2,3,1,0:T(8,128)} %fusion.21, f32[8,128,128,6]{2,3,1,0:T(8,128)} %fusion.27, f32[8,128,128,6]{2,3,1,0:T(8,128)} %fusion.29, f32[6,8,128,128]{3,0,2,1:T(8,128)} %fusion.76, f32[8,128,128,6]{2,3,1,0:T(8,128)} %fusion.8, ...), kind=kOutput, calls=%fused_computation.26 | convolution fusion | flops 63799296 | bytes 29229200 | tf_op jit(solution)/shard_map/vu,vxyz->uxyz/dot_general | solution.py:43
  182.2 7.9 %bitcast_add_fusion.14 = (f32[6,1024,128]{2,0,1:T(8,128)}, f32[6,1024,128]{2,0,1:T(8,128)}) fusion(f32[1,6,8,128,128]{4,1,3,2,0:T(8,128)S(1)} %copy-done.3, f32[6,1024,128]{2,0,1:T(8,128)} %scatter_fusion, f32[6,8,128,128]{3,0,2,1:T(8,128)} %fusion.17), kind=kLoop, calls=%fused_computation.104 | loop fusion | flops 2359296 | bytes 15728640 | tf_op jit(solution)/shard_map/add | solution.py:89
  190.1 10.4 %gather_fusion.3 = f32[1024,6,128]{2,1,0:T(8,128)} fusion(f32[6,1024,128]{2,0,1:T(8,128)} %get-tuple-element.6, s32[1024]{0:T(1024)S(1)} %fusion.81), kind=kCustom, calls=%fused_computation.1.clone | custom fusion | bytes 6295552 | tf_op jit(solution)/shard_map/jit(_take)/gather | solution.py:31
  200.5 7.3 %bitcast_multiply_fusion = f32[6,1024,128]{2,0,1:T(8,128)S(1)} fusion(f32[1024,6,128]{2,1,0:T(8,128)} %gather_fusion.3, f32[1024]{0:T(1024)S(1)} %broadcast_select_fusion, pred[1024]{0:T(1024)(128)(4,1)S(1)} %compare_and_fusion), kind=kLoop, calls=%fused_computation.22 | loop fusion | flops 1572864 | bytes 6296576 | tf_op jit(solution)/shard_map/mul | solution.py:34
  210.2 12.4 %all-to-all-start.1 = ((f32[6,128,8,128]{3,2,0,1:T(8,128)}), f32[6,128,8,128]{3,2,0,1:T(8,128)}, u32[]{:S(2)}, u32[]{:S(2)}) async-start(f32[6,128,8,128]{3,2,0,1:T(8,128)} %copy.97), calls=%async_computation.1 | async-start | bytes 6291456 | tf_op jit(solution)/shard_map/all_to_all | solution.py:35
  222.7 2.8 gather_fusion.1
  225.5 38.6 %all-to-all-done.1 = f32[6,128,8,128]{3,2,0,1:T(8,128)} async-done(((f32[6,128,8,128]{3,2,0,1:T(8,128)}), f32[6,128,8,128]{3,2,0,1:T(8,128)}, u32[]{:S(2)}, u32[]{:S(2)}) %all-to-all-start.1) | async-done | bytes 3145760 | tf_op jit(solution)/shard_map/all_to_all | solution.py:35
  264.1 3.2 %fusion.57 = f32[64,6,128]{2,0,1:T(8,128)S(1)} fusion(f32[6,128,8,128]{3,2,0,1:T(8,128)} %all-to-all-done.1, f32[64,6,128]{2,1,0:T(8,128)S(1)} %gather_fusion.1, s32[1024]{0:T(1024)S(1)} %eq.8), kind=kOutput, calls=%fused_computation.70 | convolution fusion | flops 604143616 | bytes 3543040 | tf_op jit(solution)/shard_map/sk,vkz->vsz/dot_general | solution.py:39
  267.4 6.8 %scatter_fusion.1 = f32[6,1024,128]{2,0,1:T(8,128)} fusion(f32[6,1024,128]{2,0,1:T(8,128)} %get-tuple-element.7, s32[64]{0:T(128)S(1)} %fusion.82, f32[64,6,128]{2,1,0:T(8,128)S(1)} %copy.100), kind=kCustom, calls=%fused_computation.5 | custom fusion | flops 49152 | bytes 590080 | tf_op jit(solution)/shard_map/scatter-add | solution.py:61
  (63 shorter events, 25.8 us)
Async XLA Ops:
  0.0 13.6 %copy-start.10 = (s32[1,128,8]{1,2,0:T(8,128)S(1)}, s32[1,128,8]{1,2,0:T(8,128)}, u32[]{:S(2)}) copy-start(s32[1,128,8]{1,2,0:T(8,128)} %param.15) | copy-start | bytes 12292
  0.0 13.9 %copy-start.11 = (f32[1,128,8]{1,2,0:T(8,128)S(1)}, f32[1,128,8]{1,2,0:T(8,128)}, u32[]{:S(2)}) copy-start(f32[1,128,8]{1,2,0:T(8,128)} %param.17) | copy-start | bytes 12292
  0.0 14.1 %copy-start.13 = (s32[1,128]{1,0:T(1,128)S(1)}, s32[1,128]{1,0:T(1,128)}, u32[]{:S(2)}) copy-start(s32[1,128]{1,0:T(1,128)} %param.16) | copy-start | bytes 1540
  3.7 1.9 copy-start
  6.8 81.8 %collective-permute-start = (f32[6,1,128,128]{3,0,2,1:T(8,128)}, f32[6,1,128,128]{3,0,2,1:T(8,128)}, u32[]{:S(2)}, u32[]{:S(2)}) collective-permute-start(f32[6,1,128,128]{3,0,2,1:T(8,128)} %get-tuple-element.13), channel_id=1, source_target_pairs={{1,0},{2,1},{3,2},{4,3},{5,4},{6,5},{7,6},{8,7},{9,8},{10,9},{11,1... | collective-permute-start | bytes 1179656 | tf_op jit(solution)/shard_map/ppermute | solution.py:20
  10.1 86.7 %collective-permute-start.1 = (f32[6,1,128,128]{3,0,2,1:T(8,128)}, f32[6,1,128,128]{3,0,2,1:T(8,128)}, u32[]{:S(2)}, u32[]{:S(2)}) collective-permute-start(f32[6,1,128,128]{3,0,2,1:T(8,128)} %get-tuple-element.12), channel_id=1, source_target_pairs={{0,1},{1,2},{2,3},{3,4},{4,5},{5,6},{6,7},{7,8},{8,9},{9,10},{10,1... | collective-permute-start | bytes 1179656 | tf_op jit(solution)/shard_map/ppermute | solution.py:18
  34.4 78.4 %all-to-all-start = ((f32[6,128,8,128]{3,2,0,1:T(8,128)}), f32[6,128,8,128]{3,2,0,1:T(8,128)}, u32[]{:S(2)}, u32[]{:S(2)}) async-start(f32[6,128,8,128]{3,2,0,1:T(8,128)} %copy.85), calls=%async_computation | async-start | bytes 6291456 | tf_op jit(solution)/shard_map/all_to_all | solution.py:35
  46.9 7.0 %copy-start.9 = (f32[1,6,6,6]{3,0,2,1:T(1,128)S(1)}, f32[1,6,6,6]{3,0,2,1:T(1,128)}, u32[]{:S(2)}) copy-start(f32[1,6,6,6]{3,0,2,1:T(1,128)} %param.14) | copy-start | bytes 2596
  46.9 7.0 %copy-start.1 = (f32[1,6,8,128,128]{4,1,3,2,0:T(8,128)S(1)}, f32[1,6,8,128,128]{4,1,3,2,0:T(8,128)}, u32[]{:S(2)}) copy-start(f32[1,6,8,128,128]{4,1,3,2,0:T(8,128)} %copy-done) | copy-start | bytes 9437188
  59.1 5.7 %copy-start.14 = (s32[1,64]{1,0:T(1,128)S(1)}, s32[1,64]{1,0:T(1,128)}, u32[]{:S(2)}) copy-start(s32[1,64]{1,0:T(1,128)} %param.19) | copy-start | bytes 772
  64.8 8.0 %copy-start.4 = (f32[1,6,8,128,128]{4,3,2,1,0:T(8,128)S(1)}, f32[1,6,8,128,128]{4,3,2,1,0:T(8,128)}, u32[]{:S(2)}) copy-start(f32[1,6,8,128,128]{4,3,2,1,0:T(8,128)} %param.11) | copy-start | bytes 9437188
  72.9 7.4 %copy-start.6 = (f32[6,8,128,127]{3,0,2,1:T(8,128)S(1)}, f32[6,8,128,127]{3,0,2,1:T(8,128)}, u32[]{:S(2)}) copy-start(f32[6,8,128,127]{3,0,2,1:T(8,128)} %get-tuple-element.14) | copy-start | bytes 9363460
  80.3 8.1 %copy-start.12 = (s32[1,128,8]{1,2,0:T(8,128)S(1)}, s32[1,128,8]{1,2,0:T(8,128)}, u32[]{:S(2)}) copy-start(s32[1,128,8]{1,2,0:T(8,128)} %param.18) | copy-start | bytes 12292
  88.6 8.2 %copy-start.2 = (f32[1,6,8,128,128]{4,1,3,2,0:T(8,128)S(1)}, f32[1,6,8,128,128]{4,1,3,2,0:T(8,128)}, u32[]{:S(2)}) copy-start(f32[1,6,8,128,128]{4,1,3,2,0:T(8,128)} %copy-done) | copy-start | bytes 9437188
  88.6 8.2 %copy-start.5 = (f32[1,6,8,128,128]{4,3,2,1,0:T(8,128)S(1)}, f32[1,6,8,128,128]{4,3,2,1,0:T(8,128)}, u32[]{:S(2)}) copy-start(f32[1,6,8,128,128]{4,3,2,1,0:T(8,128)} %param.12) | copy-start | bytes 9437188
  88.6 8.2 %copy-start.7 = (f32[1,8,128,128]{3,2,1,0:T(8,128)S(1)}, f32[1,8,128,128]{3,2,1,0:T(8,128)}, u32[]{:S(2)}) copy-start(f32[1,8,128,128]{3,2,1,0:T(8,128)} %param.13) | copy-start | bytes 1572868
  145.4 16.8 %collective-permute-start.2 = (f32[6,1,128,128]{3,0,2,1:T(8,128)S(1)}, f32[6,1,128,128]{3,0,2,1:T(8,128)S(1)}, u32[]{:S(2)}, u32[]{:S(2)}) collective-permute-start(f32[6,1,128,128]{3,0,2,1:T(8,128)S(1)} %get-tuple-element.9), channel_id=1, source_target_pairs={{1,0},{2,1},{3,2},{4,3},{5,4},{6,5},{7,6},{8,7},{9,8},{10,9},{11,1... | collective-permute-start | bytes 1179656 | tf_op jit(solution)/shard_map/ppermute | solution.py:20
  153.6 14.5 %collective-permute-start.3 = (f32[6,1,128,128]{3,0,2,1:T(8,128)S(1)}, f32[6,1,128,128]{3,0,2,1:T(8,128)S(1)}, u32[]{:S(2)}, u32[]{:S(2)}) collective-permute-start(f32[6,1,128,128]{3,0,2,1:T(8,128)S(1)} %get-tuple-element.8), channel_id=1, source_target_pairs={{0,1},{1,2},{2,3},{3,4},{4,5},{5,6},{6,7},{7,8},{8,9},{9,10},{10,1... | collective-permute-start | bytes 1179656 | tf_op jit(solution)/shard_map/ppermute | solution.py:18
  162.2 5.8 %copy-start.8 = (f32[1,8,128,128]{3,2,1,0:T(8,128)S(1)}, f32[1,8,128,128]{3,2,1,0:T(8,128)}, u32[]{:S(2)}) copy-start(f32[1,8,128,128]{3,2,1,0:T(8,128)} %param.13) | copy-start | bytes 1572868
  168.1 14.1 %copy-start.3 = (f32[1,6,8,128,128]{4,1,3,2,0:T(8,128)S(1)}, f32[1,6,8,128,128]{4,1,3,2,0:T(8,128)}, u32[]{:S(2)}) copy-start(f32[1,6,8,128,128]{4,1,3,2,0:T(8,128)} %copy-done) | copy-start | bytes 9437188
  210.2 53.8 %all-to-all-start.1 = ((f32[6,128,8,128]{3,2,0,1:T(8,128)}), f32[6,128,8,128]{3,2,0,1:T(8,128)}, u32[]{:S(2)}, u32[]{:S(2)}) async-start(f32[6,128,8,128]{3,2,0,1:T(8,128)} %copy.97), calls=%async_computation.1 | async-start | bytes 6291456 | tf_op jit(solution)/shard_map/all_to_all | solution.py:35
where the time goes:
time: 284 us; the launch traced here: 279 us
  matrix products  110 us (39%)
  local copies, waits for them, and re-layouts  47.3 us (17%)
  other arithmetic  46.2 us (16%)
  waiting for transfers between devices  38.6 us (14%)
  starting transfers between devices  37.3 us (13%)
    dot_general x14, matrix products, apply_block(): jnp.einsum('vu,vxyz->uxyz', matrix, values, precision=lax.Precision.HIGHEST)  103 us
    all_to_all x2, waiting for transfers between devices, fringe_values(): lax.all_to_all(outgoing, ('comp', 'blk'), split_axis=1, concat_axis=1, ti...  38.6 us
    all_to_all x2, starting transfers between devices, fringe_values(): lax.all_to_all(outgoing, ('comp', 'blk'), split_axis=1, concat_axis=1, ti...  24.9 us
    gather x2, local copies, waits for them, and re-layouts, fringe_values(): picked = jnp.take(flat, send_tile.reshape(-1), axis=1)  20.8 us
    mul x2, other arithmetic, fringe_values(): picked * scale[None, :, None]  14.6 us
    scatter-add x2, other arithmetic, residual_of(): rate_flat.at[:, rows, :].add(PENALTY * (interp - field_flat[:, rows, :]))  13.6 us
    add x2, other arithmetic, shards(): middle = start + TIME_STEP * first  10 us
    slice x2, local copies, waits for them, and re-layouts, residual_of(): field[:, :, :, 1:]  8.32 us
  transfers between devices with their start and end apart: 6, of which 1 were waited for; matrix products, arithmetic and copies ran while one was open for 38% of the time, Pallas kernels for 0%

commit v1 on v0

v1 whole, which is shorter than its diff:
```python
import functools

import jax
import jax.numpy as jnp
from jax import lax
from jax.experimental import pallas as pl
from jax.experimental.pallas import tpu as pltpu
from jax.sharding import PartitionSpec as P

PENALTY = 4.0
TIME_STEP = 0.08
NVAR, CX, CY, CZ = 6, 8, 128, 128
ROWS = CX * CY
CAP = 8
SLOTS = 64
PEERS = 128
STEPS = 8
PB = PEERS // STEPS
BAND = 32
MEM = pltpu.MemorySpace


def gather_rows(field, tile, count, weight, out, first):
    def peer_rows(p, carry):
        peer = first + p
        live = count[0, peer]
        for e in range(CAP):
            t = tile[e, peer]
            w = jnp.where(e < live, weight[e, peer], 0.0)
            for v in range(NVAR):
                out[p, pl.ds(v * CAP + e, 1), :] = field[v, pl.ds(t, 1), :] * w
        return carry

    lax.fori_loop(0, PB, peer_rows, 0)


def reduce_rows(slots, arrived, total):
    slot_ids = lax.broadcasted_iota(jnp.int32, (SLOTS, PB * CAP), 0)
    onehot = (slots[...] == slot_ids).astype(jnp.bfloat16)
    for v in range(NVAR):
        part = arrived[:, v * CAP : (v + 1) * CAP, :].reshape(PB * CAP, CZ)
        high = part.astype(jnp.bfloat16)
        low = (part - high.astype(jnp.float32)).astype(jnp.bfloat16)
        both = jnp.dot(onehot, jnp.concatenate([high, low], axis=1), preferred_element_type=jnp.float32)
        total[v] += both[:, :CZ] + both[:, CZ:]


def send_kernel(tile, count, weight, field, out):
    gather_rows(field, tile, count, weight, out, pl.program_id(0) * PB)


def middle_kernel(tile, count, weight, rows, slots, arrived, start_mid, sent, mid, field, total, sems):
    step = pl.program_id(0)
    load = pltpu.make_async_copy(start_mid, field, sems.at[0])
    store = pltpu.make_async_copy(field, mid, sems.at[1])

    @pl.when(step == 0)
    def _():
        load.start()
        total[...] = jnp.zeros_like(total)

    @pl.when(step < STEPS)
    def _():
        reduce_rows(slots, arrived, total)

    @pl.when(step == STEPS - 1)
    def _():
        load.wait()

        def patch(s, carry):
            t = rows[0, s]
            for v in range(NVAR):
                field[v, pl.ds(t, 1), :] += (TIME_STEP * PENALTY) * total[v, pl.ds(s, 1), :]
            return carry

        lax.fori_loop(0, SLOTS, patch, 0)
        store.start()

    @pl.when(step >= STEPS)
    def _():
        gather_rows(field, tile, count, weight, sent, (step - STEPS) * PB)

    @pl.when(step == 2 * STEPS - 1)
    def _():
        store.wait()


def last_kernel(rows, slots, arrived, start_end, end, field, total, sems):
    step = pl.program_id(0)
    load = pltpu.make_async_copy(start_end, field, sems.at[0])
    store = pltpu.make_async_copy(field, end, sems.at[1])

    @pl.when(step == 0)
    def _():
        load.start()
        total[...] = jnp.zeros_like(total)

    reduce_rows(slots, arrived, total)

    @pl.when(step == STEPS - 1)
    def _():
        load.wait()

        def patch(s, carry):
            t = rows[0, s]
            for v in range(NVAR):
                field[v, pl.ds(t, 1), :] += (0.5 * TIME_STEP * PENALTY) * total[v, pl.ds(s, 1), :]
            return carry

        lax.fori_loop(0, SLOTS, patch, 0)
        store.start()
        store.wait()


def flux_kernel(second, coupling, rows, below, above, *refs):
    if second:
        field, base, source, volume, out, ext, sems = refs
    else:
        field, source, volume, out, ext, sems = refs
    x = pl.program_id(0)
    body = pltpu.make_async_copy(field, ext.at[:, pl.ds(1, CX), pl.ds(8, CY), :], sems.at[0])
    low = pltpu.make_async_copy(below, ext.at[:, 0, pl.ds(8, CY), :], sems.at[1])
    high = pltpu.make_async_copy(above, ext.at[:, CX + 1, pl.ds(8, CY), :], sems.at[2])

    @pl.when(x == 0)
    def _():
        body.start()
        low.start()
        high.start()
        edge = jnp.zeros((NVAR, CX + 2, 8, CZ), jnp.float32)
        ext[:, :, 0:8, :] = edge
        ext[:, :, 8 + CY : 16 + CY, :] = edge
        body.wait()
        low.wait()
        high.wait()

    lane = lax.broadcasted_iota(jnp.int32, (BAND, CZ), 1)

    def band(i, carry):
        y = pl.multiple_of(i * BAND, BAND)
        flux = [jnp.zeros((BAND, CZ), jnp.float32) for _ in range(NVAR)]
        for w in range(NVAR):
            center = ext[w, x + 1, pl.ds(y + 8, BAND), :]
            for d in range(6):
                if d == 0:
                    near = ext[w, x + 2, pl.ds(y + 8, BAND), :]
                elif d == 1:
                    near = ext[w, x, pl.ds(y + 8, BAND), :]
                elif d == 2:
                    near = ext[w, x + 1, pl.ds(y + 9, BAND), :]
                elif d == 3:
                    near = ext[w, x + 1, pl.ds(y + 7, BAND), :]
                elif d == 4:
                    near = jnp.where(lane == CZ - 1, 0.0, pltpu.roll(center, CZ - 1, 1))
                else:
                    near = jnp.where(lane == 0, 0.0, pltpu.roll(center, 1, 1))
                diff = near - center
                for u in range(NVAR):
                    flux[u] = flux[u] + coupling[d, w * NVAR + u] * diff
        vol = volume[0, pl.ds(y, BAND), :]
        for u in range(NVAR):
            rate = vol * flux[u] + source[u, 0, pl.ds(y, BAND), :]
            center = ext[u, x + 1, pl.ds(y + 8, BAND), :]
            if second:
                value = 0.5 * (base[u, 0, pl.ds(y, BAND), :] + center) + (0.5 * TIME_STEP) * rate
            else:
                value = center + TIME_STEP * rate
            out[u, x, pl.ds(y, BAND), :] = value
        return carry

    lax.fori_loop(0, CY // BAND, band, 0)

    @pl.when(x == CX - 1)
    def _():
        scale = PENALTY * TIME_STEP * (0.5 if second else 1.0)

        def patch(s, carry):
            t = rows[0, s]
            a, b = t // CY, t % CY
            for v in range(NVAR):
                out[v, a, pl.ds(b, 1), :] -= scale * ext[v, a + 1, pl.ds(b + 8, 1), :]
            return carry

        lax.fori_loop(0, SLOTS, patch, 0)


SMEM = pl.BlockSpec(memory_space=MEM.SMEM)
ANY = pl.BlockSpec(memory_space=pl.ANY)
FIELD = jax.ShapeDtypeStruct((NVAR, CX, CY, CZ), jnp.float32)
FLAT = jax.ShapeDtypeStruct((NVAR, ROWS, CZ), jnp.float32)
SENT = jax.ShapeDtypeStruct((PEERS, NVAR * CAP, CZ), jnp.float32)


def params(mib):
    return pltpu.CompilerParams(dimension_semantics=("arbitrary",), vmem_limit_bytes=mib << 20)


def pack(field, tile, count, weight):
    return pl.pallas_call(
        send_kernel,
        grid=(STEPS,),
        in_specs=[SMEM, SMEM, SMEM, pl.BlockSpec((NVAR, ROWS, CZ), lambda i: (0, 0, 0))],
        out_specs=pl.BlockSpec((PB, NVAR * CAP, CZ), lambda i: (i, 0, 0)),
        out_shape=SENT,
        compiler_params=params(24),
        cost_estimate=pl.CostEstimate(flops=10**6, bytes_accessed=7 << 20, transcendentals=0),
        name="pack",
    )(tile, count, weight, field)


def middle(arrived, mid, tile, count, weight, rows, slots):
    last = STEPS - 1
    return pl.pallas_call(
        middle_kernel,
        grid=(2 * STEPS,),
        in_specs=[
            SMEM,
            SMEM,
            SMEM,
            SMEM,
            pl.BlockSpec((1, PB * CAP), lambda i: (0, jnp.minimum(i, last))),
            pl.BlockSpec((PB, NVAR * CAP, CZ), lambda i: (jnp.minimum(i, last), 0, 0)),
            ANY,
        ],
        out_specs=[pl.BlockSpec((PB, NVAR * CAP, CZ), lambda i: (jnp.maximum(i - STEPS, 0), 0, 0)), ANY],
        out_shape=[SENT, FLAT],
        scratch_shapes=[
            pltpu.VMEM((NVAR, ROWS, CZ), jnp.float32),
            pltpu.VMEM((NVAR, SLOTS, CZ), jnp.float32),
            pltpu.SemaphoreType.DMA((2,)),
        ],
        compiler_params=params(24),
        cost_estimate=pl.CostEstimate(flops=10**8, bytes_accessed=12 << 20, transcendentals=0),
        name="middle",
    )(tile, count, weight, rows, slots, arrived, mid)


def finish(arrived, end, rows, slots):
    return pl.pallas_call(
        last_kernel,
        grid=(STEPS,),
        in_specs=[
            SMEM,
            pl.BlockSpec((1, PB * CAP), lambda i: (0, i)),
            pl.BlockSpec((PB, NVAR * CAP, CZ), lambda i: (i, 0, 0)),
            ANY,
        ],
        out_specs=ANY,
        out_shape=FLAT,
        scratch_shapes=[
            pltpu.VMEM((NVAR, ROWS, CZ), jnp.float32),
            pltpu.VMEM((NVAR, SLOTS, CZ), jnp.float32),
            pltpu.SemaphoreType.DMA((2,)),
        ],
        compiler_params=params(24),
        cost_estimate=pl.CostEstimate(flops=10**8, bytes_accessed=9 << 20, transcendentals=0),
        name="finish",
    )(rows, slots, arrived, end)


def advance(second, coupling, rows, below, above, field, base, source, volume):
    plane = pl.BlockSpec((NVAR, 1, CY, CZ), lambda i: (0, i, 0, 0))
    fields = [field, base, source] if second else [field, source]
    return pl.pallas_call(
        functools.partial(flux_kernel, second),
        grid=(CX,),
        in_specs=[SMEM, SMEM, ANY, ANY, ANY]
        + [plane] * (len(fields) - 1)
        + [pl.BlockSpec((1, CY, CZ), lambda i: (i, 0, 0))],
        out_specs=pl.BlockSpec((NVAR, CX, CY, CZ), lambda i: (0, 0, 0, 0)),
        out_shape=FIELD,
        scratch_shapes=[
            pltpu.VMEM((NVAR, CX + 2, CY + 16, CZ), jnp.float32),
            pltpu.SemaphoreType.DMA((3,)),
        ],
        compiler_params=params(40),
        cost_estimate=pl.CostEstimate(flops=60 * 10**6, bytes_accessed=12 << 20, transcendentals=0),
        name="advance",
    )(coupling, rows, below, above, *fields, volume)


def halos(field):
    count = lax.axis_size("blk")
    below = lax.ppermute(field[:, -1], "blk", [(i, i + 1) for i in range(count - 1)])
    above = lax.ppermute(field[:, 0], "blk", [(i + 1, i) for i in range(count - 1)])
    return below, above


def exchange(sent):
    return lax.all_to_all(sent, ("comp", "blk"), split_axis=0, concat_axis=0, tiled=True)


def shards(psi_start, adj_source, vol_inverse, coupling, send_tile, send_count, send_weight, recv_slot, fringe_row):
    start = psi_start[0]
    source = adj_source[0]
    volume = vol_inverse[0]
    matrices = coupling[0].reshape(6, NVAR * NVAR)
    tile = send_tile[0].T
    weight = send_weight[0].T
    slots = recv_slot[0].reshape(1, PEERS * CAP)

    sent = pack(start.reshape(NVAR, ROWS, CZ), tile, send_count, weight)
    arrived = exchange(sent)
    below, above = halos(start)
    mid = advance(False, matrices, fringe_row, below, above, start, None, source, volume)
    sent, mid = middle(arrived, mid.reshape(NVAR, ROWS, CZ), tile, send_count, weight, fringe_row, slots)
    arrived = exchange(sent)
    mid = mid.reshape(NVAR, CX, CY, CZ)
    below, above = halos(mid)
    end = advance(True, matrices, fringe_row, below, above, mid, start, source, volume)
    end = finish(arrived, end.reshape(NVAR, ROWS, CZ), fringe_row, slots)
    return end.reshape(1, NVAR, CX, CY, CZ)


def solution(mesh):
    in_specs = (
        P("comp", None, "blk", None, None),
        P("comp", None, "blk", None, None),
        P("comp", "blk", None, None),
        P("comp", None, None, None),
        P(("comp", "blk"), None, None),
        P(("comp", "blk"), None),
        P(("comp", "blk"), None, None),
        P(("comp", "blk"), None, None),
        P(("comp", "blk"), None),
    )
    out_specs = P("comp", None, "blk", None, None)
    return jax.shard_map(shards, mesh=mesh, in_specs=in_specs, out_specs=out_specs, check_vma=False)
```

time: 284 us -> 181 us (0.64)
  matrix products: 110 us -> 0 us
  Pallas kernels: 0 us -> 51 us
  other arithmetic: 46.2 us -> 1.38 us
  waiting for transfers between devices: 38.6 us -> 63.4 us
  local copies, waits for them, and re-layouts: 47.3 us -> 30.4 us
  starting transfers between devices: 37.3 us -> 32.7 us
    dot_general x16 -> x0, matrix products: 110 us -> none  [the longest x14 103 us: apply_block(): jnp.einsum('vu,vxyz->uxyz', matrix, values, precision=lax.Precision.HIGHEST)]
    ppermute x4, waiting for transfers between devices: 0.01 us -> 63.3 us  [the longest x2 63.3 us: halos(): lax.ppermute(field[:, 0], 'blk', [(i + 1, i) for i in range(count - 1)])]
    pallas_call x0 -> x5, Pallas kernels: none -> 51 us  [the longest x2 27.4 us: advance(): pl.pallas_call(functools.partial(flux_kernel, second), grid=(CX,), in_spe...]
    all_to_all x2, waiting for transfers between devices: 38.6 us -> 0.01 us  [exchange(): lax.all_to_all(sent, ('comp', 'blk'), split_axis=0, concat_axis=0, tiled=...]
    gather x4 -> x0, local copies, waits for them, and re-layouts: 26.3 us -> none  [the longest x2 20.8 us: fringe_values(): picked = jnp.take(flat, send_tile.reshape(-1), axis=1)]
    unnamed x34 -> x49, local copies, waits for them, and re-layouts: 6.03 us -> 26.5 us
    mul x4 -> x0, other arithmetic: 20 us -> none  [the longest x2 14.6 us: fringe_values(): picked * scale[None, :, None]]
    scatter-add x2 -> x0, other arithmetic: 13.6 us -> none  [residual_of(): rate_flat.at[:, rows, :].add(PENALTY * (interp - field_flat[:, rows, :]))]
  transfers between devices with their start and end apart: 6 -> 6, of which waited for: 1 -> 2; matrix products, arithmetic and copies ran while one was open for 38% -> 3% of each run, Pallas kernels for 0% -> 15%
where the time goes in v1:
time: 181 us; the launch traced here: 179 us
  waiting for transfers between devices  63.4 us (35%)
  Pallas kernels  51 us (28%)
  starting transfers between devices  32.7 us (18%)
  local copies, waits for them, and re-layouts  30.4 us (17%)
    ppermute x2, waiting for transfers between devices, halos(): lax.ppermute(field[:, 0], 'blk', [(i + 1, i) for i in range(count - 1)])  63.3 us
    pallas_call x2, Pallas kernels, advance(): pl.pallas_call(functools.partial(flux_kernel, second), grid=(CX,), in_spe...  27.4 us
    unnamed x49, local copies, waits for them, and re-layouts  26.5 us
    all_to_all x2, starting transfers between devices, exchange(): lax.all_to_all(sent, ('comp', 'blk'), split_axis=0, concat_axis=0, tiled=...  21.5 us
    pallas_call x1, Pallas kernels, middle(): pl.pallas_call(middle_kernel, grid=(2 * STEPS,), in_specs=[SMEM, SMEM, SM...  11 us
    pallas_call x1, Pallas kernels, finish(): pl.pallas_call(last_kernel, grid=(STEPS,), in_specs=[SMEM, pl.BlockSpec((...  7.76 us
    ppermute x2, starting transfers between devices, halos(): lax.ppermute(field[:, 0], 'blk', [(i + 1, i) for i in range(count - 1)])  6.07 us
    ppermute x2, starting transfers between devices, halos(): lax.ppermute(field[:, -1], 'blk', [(i, i + 1) for i in range(count - 1)])  5.08 us
  transfers between devices with their start and end apart: 6, of which 2 were waited for; matrix products, arithmetic and copies ran while one was open for 3% of the time, Pallas kernels for 15%

profile of v1, /device:TPU:1, one launch (start us, length us, event | category | flops | bytes accessed | tf_op | source)
XLA Modules:
  0.0 178.9 jit_solution(16396458660007061110)
XLA Ops:
  0.0 1.9 %copy-done = f32[1,6,8,128,128]{4,3,2,1,0:T(8,128)S(1)} copy-done((f32[1,6,8,128,128]{4,3,2,1,0:T(8,128)S(1)}, f32[1,6,8,128,128]{4,3,2,1,0:T(8,128)}, u32[]{:S(2)}) %copy-start) | copy-done | bytes 3145752
  3.9 4.9 %pack.1 = f32[128,48,128]{2,1,0:T(8,128)S(1)} custom-call(s32[8,128]{1,0:T(8,128)S(1)} %bitcast.34, s32[1,128]{1,0:T(1,128)S(1)} %copy-done.21, f32[8,128]{1,0:T(8,128)S(1)} %bitcast.36, f32[6,1024,128]{2,1,0:T(8,128)S(1)} %bitcast.22), custom_call_target="tpu_custom_call" | custom-call | flops 1000000 | bytes 7340032 | tf_op jit(solution)/shard_map/pack/pallas_call | solution.py:199
  8.9 1.7 copy-done.2
  10.5 11.9 %all-to-all-start = ((f32[128,48,128]{2,1,0:T(8,128)}), f32[128,48,128]{2,1,0:T(8,128)}, u32[]{:S(2)}, u32[]{:S(2)}) async-start(f32[128,48,128]{2,1,0:T(8,128)} %copy-done.2), calls=%async_computation | async-start | bytes 6291456 | tf_op jit(solution)/shard_map/all_to_all | solution.py:290
  22.4 0.9 slice_bitcast_fusion.2
  23.4 3.0 %collective-permute-start.1 = (f32[6,128,128]{2,1,0:T(8,128)}, f32[6,128,128]{2,1,0:T(8,128)S(1)}, u32[]{:S(2)}, u32[]{:S(2)}) collective-permute-start(f32[6,128,128]{2,1,0:T(8,128)} %get-tuple-element.11), channel_id=1, source_target_pairs={{1,0},{2,1},{3,2},{4,3},{5,4},{6,5},{7,6},{8,7},{9,8},{10,9},{11,1... | collective-permute-start | bytes 1179656 | tf_op jit(solution)/shard_map/ppermute | solution.py:285
  26.4 2.5 %collective-permute-start = (f32[6,128,128]{2,1,0:T(8,128)}, f32[6,128,128]{2,1,0:T(8,128)}, u32[]{:S(2)}, u32[]{:S(2)}) collective-permute-start(f32[6,128,128]{2,1,0:T(8,128)} %get-tuple-element.12), channel_id=1, source_target_pairs={{0,1},{1,2},{2,3},{3,4},{4,5},{5,6},{6,7},{7,8},{8,9},{9,10},{10,1... | collective-permute-start | bytes 1179656 | tf_op jit(solution)/shard_map/ppermute | solution.py:284
  29.0 1.4 reduce
  30.3 0.8 reshape_squeeze.11.coupling
  31.2 0.7 copy.11
  31.9 0.9 reshape_squeeze.9.slots
  32.8 29.9 %collective-permute-done.1.above = f32[6,128,128]{2,1,0:T(8,128)S(1)} collective-permute-done((f32[6,128,128]{2,1,0:T(8,128)}, f32[6,128,128]{2,1,0:T(8,128)S(1)}, u32[]{:S(2)}, u32[]{:S(2)}) %collective-permute-start.1) | collective-permute-done | bytes 393248 | tf_op jit(solution)/shard_map/ppermute | solution.py:285
  62.7 1.9 %copy-done.5 = f32[1,6,8,128,128]{4,3,2,1,0:T(8,128)S(1)} copy-done((f32[1,6,8,128,128]{4,3,2,1,0:T(8,128)S(1)}, f32[1,6,8,128,128]{4,3,2,1,0:T(8,128)}, u32[]{:S(2)}) %copy-start.5) | copy-done | bytes 3145752
  64.6 1.0 copy-done.12
  66.3 13.9 %advance.2 = f32[6,8,128,128]{3,2,1,0:T(8,128)S(1)} custom-call(f32[6,36]{1,0:T(8,128)S(1)} %reshape_squeeze.11.coupling, s32[1,64]{1,0:T(1,128)S(1)} %copy-done.18, f32[6,128,128]{2,1,0:T(8,128)} %collective-permute-done.below, f32[6,128,128]{2,1,0:T(8,128)S(1)} %collective-permute-done.1.above, f32[6,8,128,128]{3,2,1,0:T(8,128)S(1)} %bitcast.24, ...), custom_call_target="tpu_custom_call" | custom-call | flops 60000000 | bytes 12582912 | tf_op jit(solution)/shard_map/advance/pallas_call | solution.py:264
  80.2 1.7 copy-done.3
  81.9 1.9 %copy-done.4 = f32[6,8,128,128]{3,2,1,0:T(8,128)S(1)} copy-done((f32[6,8,128,128]{3,2,1,0:T(8,128)S(1)}, f32[6,8,128,128]{3,2,1,0:T(8,128)}, u32[]{:S(2)}) %copy-start.4) | copy-done | bytes 3145752
  85.1 11.0 %middle.1 = (f32[128,48,128]{2,1,0:T(8,128)S(1)}, f32[6,1024,128]{2,1,0:T(8,128)S(1)}) custom-call(s32[8,128]{1,0:T(8,128)S(1)} %bitcast.35, s32[1,128]{1,0:T(1,128)S(1)} %copy-done.22, f32[8,128]{1,0:T(8,128)S(1)} %bitcast.37, s32[1,64]{1,0:T(1,128)S(1)} %copy-done.19, s32[1,1024]{1,0:T(1,128)S(1)} %reshape_squeeze.9.slots, ...), custom_call_target="tpu_custom_call" | custom-call | flops 100000000 | bytes 12582912 | tf_op jit(solution)/shard_map/middle/pallas_call | solution.py:213
  96.1 1.7 copy-done.9
  97.7 1.7 copy-done.11
  99.4 9.6 %all-to-all-start.1 = ((f32[128,48,128]{2,1,0:T(8,128)}), f32[128,48,128]{2,1,0:T(8,128)}, u32[]{:S(2)}, u32[]{:S(2)}) async-start(f32[128,48,128]{2,1,0:T(8,128)} %copy-done.11), calls=%async_computation.1 | async-start | bytes 6291456 | tf_op jit(solution)/shard_map/all_to_all | solution.py:290
  109.0 1.2 slice_bitcast_fusion
  110.2 3.0 %collective-permute-start.3 = (f32[6,128,128]{2,1,0:T(8,128)S(1)}, f32[6,128,128]{2,1,0:T(8,128)S(1)}, u32[]{:S(2)}, u32[]{:S(2)}) collective-permute-start(f32[6,128,128]{2,1,0:T(8,128)S(1)} %get-tuple-element.9), channel_id=1, source_target_pairs={{1,0},{2,1},{3,2},{4,3},{5,4},{6,5},{7,6},{8,7},{9,8},{10,9},{11,1... | collective-permute-start | bytes 1179656 | tf_op jit(solution)/shard_map/ppermute | solution.py:285
  113.3 2.5 %collective-permute-start.2 = (f32[6,128,128]{2,1,0:T(8,128)S(1)}, f32[6,128,128]{2,1,0:T(8,128)S(1)}, u32[]{:S(2)}, u32[]{:S(2)}) collective-permute-start(f32[6,128,128]{2,1,0:T(8,128)S(1)} %get-tuple-element.10), channel_id=1, source_target_pairs={{0,1},{1,2},{2,3},{3,4},{4,5},{5,6},{6,7},{7,8},{8,9},{9,10},{10,1... | collective-permute-start | bytes 1179656 | tf_op jit(solution)/shard_map/ppermute | solution.py:284
  115.8 33.5 %collective-permute-done.3.above = f32[6,128,128]{2,1,0:T(8,128)S(1)} collective-permute-done((f32[6,128,128]{2,1,0:T(8,128)S(1)}, f32[6,128,128]{2,1,0:T(8,128)S(1)}, u32[]{:S(2)}, u32[]{:S(2)}) %collective-permute-start.3) | collective-permute-done | bytes 393248 | tf_op jit(solution)/shard_map/ppermute | solution.py:285
  149.3 1.9 %copy-done.6 = f32[1,6,8,128,128]{4,3,2,1,0:T(8,128)S(1)} copy-done((f32[1,6,8,128,128]{4,3,2,1,0:T(8,128)S(1)}, f32[1,6,8,128,128]{4,3,2,1,0:T(8,128)}, u32[]{:S(2)}) %copy-start.6) | copy-done | bytes 3145752
  151.2 1.9 %copy-done.10 = f32[6,1024,128]{2,1,0:T(8,128)S(1)} copy-done((f32[6,1024,128]{2,1,0:T(8,128)S(1)}, f32[6,1024,128]{2,1,0:T(8,128)}, u32[]{:S(2)}) %copy-start.10) | copy-done | bytes 3145752
  153.1 1.0 copy-done.13
  154.1 13.5 %advance.3 = f32[6,8,128,128]{3,2,1,0:T(8,128)S(1)} custom-call(f32[6,36]{1,0:T(8,128)S(1)} %reshape_squeeze.11.coupling, s32[1,64]{1,0:T(1,128)S(1)} %copy-done.20, f32[6,128,128]{2,1,0:T(8,128)S(1)} %collective-permute-done.2.below, f32[6,128,128]{2,1,0:T(8,128)S(1)} %collective-permute-done.3.above, f32[6,8,128,128]{3,2,1,0:T(8,128)S(1)} %bitcast.31, ...), custom_call_target="tpu_custom_call" | custom-call | flops 60000000 | bytes 12582912 | tf_op jit(solution)/shard_map/advance/pallas_call | solution.py:264
  167.6 1.7 copy-done.7
  169.3 1.9 %copy-done.8 = f32[6,8,128,128]{3,2,1,0:T(8,128)S(1)} copy-done((f32[6,8,128,128]{3,2,1,0:T(8,128)S(1)}, f32[6,8,128,128]{3,2,1,0:T(8,128)}, u32[]{:S(2)}) %copy-start.8) | copy-done | bytes 3145752
  171.2 7.8 %finish.1 = f32[6,1024,128]{2,1,0:T(8,128)} custom-call(s32[1,64]{1,0:T(1,128)S(1)} %copy-done.20, s32[1,1024]{1,0:T(1,128)S(1)} %reshape_squeeze.9.slots, f32[128,48,128]{2,1,0:T(8,128)} %all-to-all-done.1.arrived, f32[6,1024,128]{2,1,0:T(8,128)S(1)} %bitcast.29), custom_call_target="tpu_custom_call" | custom-call | flops 100000000 | bytes 9437184 | tf_op jit(solution)/shard_map/finish/pallas_call | solution.py:239
  (39 shorter events, 4.0 us)
Async XLA Ops:
  0.0 1.9 %copy-start = (f32[1,6,8,128,128]{4,3,2,1,0:T(8,128)S(1)}, f32[1,6,8,128,128]{4,3,2,1,0:T(8,128)}, u32[]{:S(2)}) copy-start(f32[1,6,8,128,128]{4,3,2,1,0:T(8,128)} %param.9) | copy-start | bytes 9437188
  1.9 0.7 copy-start.14
  2.6 0.7 copy-start.16
  3.3 0.7 copy-start.21
  8.8 1.7 copy-start.2
  10.5 11.9 %copy-start.1 = (f32[1,6,8,128,128]{4,3,2,1,0:T(8,128)S(1)}, f32[1,6,8,128,128]{4,3,2,1,0:T(8,128)}, u32[]{:S(2)}) copy-start(f32[1,6,8,128,128]{4,3,2,1,0:T(8,128)} %param.9) | copy-start | bytes 9437188
  10.5 20.6 %copy-start.23 = (s32[1,128,8]{1,2,0:T(8,128)S(1)}, s32[1,128,8]{1,2,0:T(8,128)}, u32[]{:S(2)}) copy-start(s32[1,128,8]{1,2,0:T(8,128)} %param.16) | copy-start | bytes 12292
  10.5 71.3 %all-to-all-start = ((f32[128,48,128]{2,1,0:T(8,128)}), f32[128,48,128]{2,1,0:T(8,128)}, u32[]{:S(2)}, u32[]{:S(2)}) async-start(f32[128,48,128]{2,1,0:T(8,128)} %copy-done.2), calls=%async_computation | async-start | bytes 6291456 | tf_op jit(solution)/shard_map/all_to_all | solution.py:290
  23.4 39.3 %collective-permute-start.1 = (f32[6,128,128]{2,1,0:T(8,128)}, f32[6,128,128]{2,1,0:T(8,128)S(1)}, u32[]{:S(2)}, u32[]{:S(2)}) collective-permute-start(f32[6,128,128]{2,1,0:T(8,128)} %get-tuple-element.11), channel_id=1, source_target_pairs={{1,0},{2,1},{3,2},{4,3},{5,4},{6,5},{7,6},{8,7},{9,8},{10,9},{11,1... | collective-permute-start | bytes 1179656 | tf_op jit(solution)/shard_map/ppermute | solution.py:285
  26.4 36.3 %collective-permute-start = (f32[6,128,128]{2,1,0:T(8,128)}, f32[6,128,128]{2,1,0:T(8,128)}, u32[]{:S(2)}, u32[]{:S(2)}) collective-permute-start(f32[6,128,128]{2,1,0:T(8,128)} %get-tuple-element.12), channel_id=1, source_target_pairs={{0,1},{1,2},{2,3},{3,4},{4,5},{5,6},{6,7},{7,8},{8,9},{9,10},{10,1... | collective-permute-start | bytes 1179656 | tf_op jit(solution)/shard_map/ppermute | solution.py:284
  62.7 1.9 %copy-start.5 = (f32[1,6,8,128,128]{4,3,2,1,0:T(8,128)S(1)}, f32[1,6,8,128,128]{4,3,2,1,0:T(8,128)}, u32[]{:S(2)}) copy-start(f32[1,6,8,128,128]{4,3,2,1,0:T(8,128)} %param.10) | copy-start | bytes 9437188
  64.6 1.0 copy-start.12
  65.6 0.7 copy-start.18
  66.3 15.6 %copy-start.15 = (s32[1,128,8]{1,2,0:T(8,128)S(1)}, s32[1,128,8]{1,2,0:T(8,128)}, u32[]{:S(2)}) copy-start(s32[1,128,8]{1,2,0:T(8,128)} %param.13) | copy-start | bytes 12292
  66.3 15.6 %copy-start.17 = (f32[1,128,8]{1,2,0:T(8,128)S(1)}, f32[1,128,8]{1,2,0:T(8,128)}, u32[]{:S(2)}) copy-start(f32[1,128,8]{1,2,0:T(8,128)} %param.15) | copy-start | bytes 12292
  80.2 1.7 copy-start.3
  81.9 1.9 %copy-start.4 = (f32[6,8,128,128]{3,2,1,0:T(8,128)S(1)}, f32[6,8,128,128]{3,2,1,0:T(8,128)}, u32[]{:S(2)}) copy-start(f32[6,8,128,128]{3,2,1,0:T(8,128)} %copy-done.3) | copy-start | bytes 9437188
  83.8 0.7 copy-start.19
  84.4 0.7 copy-start.22
  96.1 1.7 copy-start.9
  97.7 1.7 copy-start.11
  99.4 49.9 %copy-start.20 = (s32[1,64]{1,0:T(1,128)S(1)}, s32[1,64]{1,0:T(1,128)}, u32[]{:S(2)}) copy-start(s32[1,64]{1,0:T(1,128)} %rows.7) | copy-start | bytes 772
  99.4 69.9 %all-to-all-start.1 = ((f32[128,48,128]{2,1,0:T(8,128)}), f32[128,48,128]{2,1,0:T(8,128)}, u32[]{:S(2)}, u32[]{:S(2)}) async-start(f32[128,48,128]{2,1,0:T(8,128)} %copy-done.11), calls=%async_computation.1 | async-start | bytes 6291456 | tf_op jit(solution)/shard_map/all_to_all | solution.py:290
  110.2 39.1 %collective-permute-start.3 = (f32[6,128,128]{2,1,0:T(8,128)S(1)}, f32[6,128,128]{2,1,0:T(8,128)S(1)}, u32[]{:S(2)}, u32[]{:S(2)}) collective-permute-start(f32[6,128,128]{2,1,0:T(8,128)S(1)} %get-tuple-element.9), channel_id=1, source_target_pairs={{1,0},{2,1},{3,2},{4,3},{5,4},{6,5},{7,6},{8,7},{9,8},{10,9},{11,1... | collective-permute-start | bytes 1179656 | tf_op jit(solution)/shard_map/ppermute | solution.py:285
  113.3 36.0 %collective-permute-start.2 = (f32[6,128,128]{2,1,0:T(8,128)S(1)}, f32[6,128,128]{2,1,0:T(8,128)S(1)}, u32[]{:S(2)}, u32[]{:S(2)}) collective-permute-start(f32[6,128,128]{2,1,0:T(8,128)S(1)} %get-tuple-element.10), channel_id=1, source_target_pairs={{0,1},{1,2},{2,3},{3,4},{4,5},{5,6},{6,7},{7,8},{8,9},{9,10},{10,1... | collective-permute-start | bytes 1179656 | tf_op jit(solution)/shard_map/ppermute | solution.py:284
  149.3 1.9 %copy-start.6 = (f32[1,6,8,128,128]{4,3,2,1,0:T(8,128)S(1)}, f32[1,6,8,128,128]{4,3,2,1,0:T(8,128)}, u32[]{:S(2)}) copy-start(f32[1,6,8,128,128]{4,3,2,1,0:T(8,128)} %param.10) | copy-start | bytes 9437188
  151.2 1.9 %copy-start.10 = (f32[6,1024,128]{2,1,0:T(8,128)S(1)}, f32[6,1024,128]{2,1,0:T(8,128)}, u32[]{:S(2)}) copy-start(f32[6,1024,128]{2,1,0:T(8,128)} %copy-done.9) | copy-start | bytes 9437188
  153.1 1.0 copy-start.13
  167.6 1.7 copy-start.7
  169.3 1.9 %copy-start.8 = (f32[6,8,128,128]{3,2,1,0:T(8,128)S(1)}, f32[6,8,128,128]{3,2,1,0:T(8,128)}, u32[]{:S(2)}) copy-start(f32[6,8,128,128]{3,2,1,0:T(8,128)} %copy-done.7) | copy-start | bytes 9437188

commit v2 on v0

v2 whole, which is shorter than its diff:
```python
import functools

import jax
import jax.numpy as jnp
from jax import lax
from jax.experimental import pallas as pl
from jax.experimental.pallas import tpu as pltpu
from jax.sharding import PartitionSpec as P

PENALTY = 4.0
TIME_STEP = 0.08
NVAR, CX, CY, CZ = 6, 8, 128, 128
ROWS = CX * CY
CAP = 8
SLOTS = 64
COMPS = 4
BLOCKS = 32
PEERS = COMPS * BLOCKS
OTHERS = COMPS - 1
PACK = NVAR * CAP
BAND = 32
F32 = jnp.float32
HBM = pl.BlockSpec(memory_space=pltpu.HBM)
SMEM = pl.BlockSpec(memory_space=pltpu.SMEM)
ANY = pl.BlockSpec(memory_space=pl.ANY)
DMA = pltpu.SemaphoreType.DMA


def shape(*dims):
    return jax.ShapeDtypeStruct(dims, F32)


def start_all(copies):
    for copy in copies:
        copy.start()


def wait_all(copies):
    for copy in copies:
        copy.wait()


def other(j):
    return lax.rem(lax.axis_index("comp") + j + 1, COMPS)


def block_of(ref, j):
    return ref.at[pl.ds(other(j) * BLOCKS, BLOCKS)]


def part_of(ref, j):
    return ref.at[pl.ds(j * BLOCKS, BLOCKS)]


def table_copies(tables, scratch, sems):
    return [pltpu.make_async_copy(a, b, sems.at[i]) for i, (a, b) in enumerate(zip(tables, scratch))]


def gather_rows(field, tables, buf, sent, sems):
    tile, count, weight = tables
    stores = []
    for j in range(OTHERS):
        first = other(j) * BLOCKS

        def peer_rows(b, carry):
            peer = first + b
            live = count[0, peer]
            for e in range(CAP):
                t = tile[e, peer]
                w = jnp.where(e < live, weight[e, peer], 0.0)
                for v in range(NVAR):
                    buf[j * BLOCKS + b, pl.ds(v * CAP + e, 1), :] = field[v, pl.ds(t, 1), :] * w
            return carry

        lax.fori_loop(0, BLOCKS, peer_rows, 0)
        stores.append(pltpu.make_async_copy(part_of(buf, j), block_of(sent, j), sems.at[j]))
        stores[-1].start()
    return stores


def reduce_rows(slots, loads, data, total):
    slot_ids = lax.broadcasted_iota(jnp.int32, (SLOTS, BLOCKS * CAP), 0)
    for j in range(OTHERS):
        onehot = (slots[pl.ds(other(j), 1), :] == slot_ids).astype(F32).astype(jnp.bfloat16)
        loads[j].wait()
        for v in range(NVAR):
            part = data[j * BLOCKS : (j + 1) * BLOCKS, v * CAP : (v + 1) * CAP, :].reshape(BLOCKS * CAP, CZ)
            high = part.astype(jnp.bfloat16)
            low = (part - high.astype(F32)).astype(jnp.bfloat16)
            both = jnp.dot(onehot, jnp.concatenate([high, low], axis=1), preferred_element_type=F32)
            both = both[:, :CZ] + both[:, CZ:]
            total[v] = both if j == 0 else total[v] + both


def add_halos(field, coupling, below, above, volume, scale):
    for side, halo, first in ((1, below, 0), (0, above, ROWS - CY)):

        def band(i, carry):
            y = pl.multiple_of(i * BAND, BAND)
            vol = volume[1 - side, pl.ds(y, BAND), :] * scale
            near = [halo[w, pl.ds(y, BAND), :] for w in range(NVAR)]
            for u in range(NVAR):
                flux = coupling[side, u] * near[0]
                for w in range(1, NVAR):
                    flux = flux + coupling[side, w * NVAR + u] * near[w]
                field[u, pl.ds(first + y, BAND), :] += vol * flux
            return carry

        lax.fori_loop(0, CY // BAND, band, 0)


def patch_rows(field, rows, total, scale):
    def patch(s, carry):
        t = rows[0, s]
        for v in range(NVAR):
            field[v, pl.ds(t, 1), :] += scale * total[v, pl.ds(s, 1), :]
        return carry

    lax.fori_loop(0, SLOTS, patch, 0)


def pack_kernel(tile, count, weight, field, sent, tile_s, count_s, weight_s, field_v, buf, sems, sent_sems):
    scratch = (tile_s, count_s, weight_s)
    copies = table_copies((tile, count, weight), scratch, sems)
    copies.append(pltpu.make_async_copy(field, field_v, sems.at[3]))
    start_all(copies)
    wait_all(copies)
    wait_all(gather_rows(field_v, scratch, buf, sent, sent_sems))


def arrive(slots, arrived, guess, below, above, volume, data, total, field, below_v, above_v, volume_v, sems):
    copies = [
        pltpu.make_async_copy(guess, field, sems.at[3]),
        pltpu.make_async_copy(below, below_v, sems.at[4]),
        pltpu.make_async_copy(above, above_v, sems.at[5]),
        pltpu.make_async_copy(volume.at[0], volume_v.at[0], sems.at[6]),
        pltpu.make_async_copy(volume.at[CX - 1], volume_v.at[1], sems.at[7]),
    ]
    loads = [pltpu.make_async_copy(block_of(arrived, j), part_of(data, j), sems.at[j]) for j in range(OTHERS)]
    start_all(loads + copies)
    reduce_rows(slots, loads, data, total)
    wait_all(copies)


def middle_kernel(
    coupling, rows, slots, tile, count, weight, arrived, guess, below, above, volume,
    sent, mid, low, high,
    tile_s, count_s, weight_s, data, total, field, below_v, above_v, volume_v, sems, table_sems, sent_sems,
):
    scratch = (tile_s, count_s, weight_s)
    tables = table_copies((tile, count, weight), scratch, table_sems)
    start_all(tables)
    arrive(slots, arrived, guess, below, above, volume, data, total, field, below_v, above_v, volume_v, sems)
    add_halos(field, coupling, below_v, above_v, volume_v, TIME_STEP)
    patch_rows(field, rows, total, TIME_STEP * PENALTY)
    stores = [
        pltpu.make_async_copy(field.at[:, pl.ds(0, CY), :], low, sems.at[0]),
        pltpu.make_async_copy(field.at[:, pl.ds(ROWS - CY, CY), :], high, sems.at[1]),
        pltpu.make_async_copy(field, mid, sems.at[2]),
    ]
    start_all(stores)
    wait_all(tables)
    wait_all(gather_rows(field, scratch, data, sent, sent_sems))
    wait_all(stores)


def finish_kernel(
    coupling, rows, slots, arrived, guess, below, above, volume,
    end,
    data, total, field, below_v, above_v, volume_v, sems,
):
    arrive(slots, arrived, guess, below, above, volume, data, total, field, below_v, above_v, volume_v, sems)
    add_halos(field, coupling, below_v, above_v, volume_v, 0.5 * TIME_STEP)
    patch_rows(field, rows, total, 0.5 * TIME_STEP * PENALTY)
    stores = [pltpu.make_async_copy(field.at[v], end.at[v], sems.at[v]) for v in range(NVAR)]
    start_all(stores)
    wait_all(stores)


def flux_kernel(second, coupling, rows, field, *refs):
    if second:
        base, source, volume, out, ext, sem = refs
    else:
        source, volume, out, ext, sem = refs
    x = pl.program_id(0)

    @pl.when(x == 0)
    def _():
        copy = pltpu.make_async_copy(field, ext.at[:, pl.ds(1, CX), pl.ds(8, CY), :], sem)
        copy.start()
        edge = jnp.zeros((NVAR, CX + 2, 8, CZ), F32)
        ext[:, :, 0:8, :] = edge
        ext[:, :, 8 + CY : 16 + CY, :] = edge
        plane = jnp.zeros((NVAR, CY, CZ), F32)
        ext[:, 0, 8 : 8 + CY, :] = plane
        ext[:, CX + 1, 8 : 8 + CY, :] = plane
        copy.wait()

    lane = lax.broadcasted_iota(jnp.int32, (BAND, CZ), 1)

    def band(i, carry):
        y = pl.multiple_of(i * BAND, BAND)
        flux = [jnp.zeros((BAND, CZ), F32) for _ in range(NVAR)]
        for w in range(NVAR):
            center = ext[w, x + 1, pl.ds(y + 8, BAND), :]
            for d in range(6):
                if d == 0:
                    near = ext[w, x + 2, pl.ds(y + 8, BAND), :]
                elif d == 1:
                    near = ext[w, x, pl.ds(y + 8, BAND), :]
                elif d == 2:
                    near = ext[w, x + 1, pl.ds(y + 9, BAND), :]
                elif d == 3:
                    near = ext[w, x + 1, pl.ds(y + 7, BAND), :]
                elif d == 4:
                    near = jnp.where(lane == CZ - 1, 0.0, pltpu.roll(center, CZ - 1, 1))
                else:
                    near = jnp.where(lane == 0, 0.0, pltpu.roll(center, 1, 1))
                diff = near - center
                for u in range(NVAR):
                    flux[u] = flux[u] + coupling[d, w * NVAR + u] * diff
        vol = volume[0, pl.ds(y, BAND), :]
        for u in range(NVAR):
            rate = vol * flux[u] + source[u, 0, pl.ds(y, BAND), :]
            center = ext[u, x + 1, pl.ds(y + 8, BAND), :]
            if second:
                value = 0.5 * (base[u, 0, pl.ds(y, BAND), :] + center) + (0.5 * TIME_STEP) * rate
            else:
                value = center + TIME_STEP * rate
            out[u, x, pl.ds(y, BAND), :] = value
        return carry

    lax.fori_loop(0, CY // BAND, band, 0)

    @pl.when(x == CX - 1)
    def _():
        scale = PENALTY * TIME_STEP * (0.5 if second else 1.0)

        def patch(s, carry):
            t = rows[0, s]
            a, b = t // CY, t % CY
            for v in range(NVAR):
                out[v, a, pl.ds(b, 1), :] -= scale * ext[v, a + 1, pl.ds(b + 8, 1), :]
            return carry

        lax.fori_loop(0, SLOTS, patch, 0)


TABLES = [
    pltpu.SMEM((CAP, PEERS), jnp.int32),
    pltpu.SMEM((1, PEERS), jnp.int32),
    pltpu.SMEM((CAP, PEERS), F32),
]
FIELD_V = pltpu.VMEM((NVAR, ROWS, CZ), F32)
DATA_V = pltpu.VMEM((OTHERS * BLOCKS, PACK, CZ), F32)
ARRIVE = [
    DATA_V,
    pltpu.VMEM((NVAR, SLOTS, CZ), F32),
    FIELD_V,
    pltpu.VMEM((NVAR, CY, CZ), F32),
    pltpu.VMEM((NVAR, CY, CZ), F32),
    pltpu.VMEM((2, CY, CZ), F32),
    DMA((8,)),
]
SLOT_ROWS = pl.BlockSpec((COMPS, BLOCKS * CAP), lambda: (0, 0))


def call(kernel, name, specs, inputs, out_shape, scratch, moved, flops):
    single = not isinstance(out_shape, list)
    return pl.pallas_call(
        kernel,
        in_specs=specs,
        out_specs=HBM if single else [HBM] * len(out_shape),
        out_shape=out_shape,
        scratch_shapes=scratch,
        compiler_params=pltpu.CompilerParams(vmem_limit_bytes=60 << 20),
        cost_estimate=pl.CostEstimate(flops=flops, bytes_accessed=moved, transcendentals=0),
        name=name,
    )(*inputs)


def pack(tables, field):
    return call(
        pack_kernel, "pack", [HBM] * 4, [*tables, field], shape(PEERS, PACK, CZ),
        [*TABLES, FIELD_V, DATA_V, DMA((4,)), DMA((OTHERS,))], 8 << 20, 10**6,
    )


def middle(matrices, rows, slots, tables, arrived, mid, below, above, volume):
    return call(
        middle_kernel, "middle", [SMEM, SMEM, SLOT_ROWS, HBM, HBM, HBM, ANY, HBM, ANY, ANY, HBM],
        [matrices, rows, slots, *tables, arrived, mid, below, above, volume],
        [shape(PEERS, PACK, CZ), shape(NVAR, ROWS, CZ), shape(NVAR, CY, CZ), shape(NVAR, CY, CZ)],
        [*TABLES, *ARRIVE, DMA((3,)), DMA((OTHERS,))], 16 << 20, 10**8,
    )


def finish(matrices, rows, slots, arrived, end, below, above, volume):
    return call(
        finish_kernel, "finish", [SMEM, SMEM, SLOT_ROWS, ANY, HBM, ANY, ANY, HBM],
        [matrices, rows, slots, arrived, end, below, above, volume],
        shape(NVAR, ROWS, CZ), ARRIVE, 10 << 20, 10**8,
    )


def advance(second, coupling, rows, field, streams, volume):
    return pl.pallas_call(
        functools.partial(flux_kernel, second),
        grid=(CX,),
        in_specs=[SMEM, SMEM, HBM]
        + [pl.BlockSpec((NVAR, 1, CY, CZ), lambda i: (0, i, 0, 0))] * len(streams)
        + [pl.BlockSpec((1, CY, CZ), lambda i: (i, 0, 0))],
        out_specs=pl.BlockSpec((NVAR, CX, CY, CZ), lambda i: (0, 0, 0, 0)),
        out_shape=shape(NVAR, CX, CY, CZ),
        scratch_shapes=[pltpu.VMEM((NVAR, CX + 2, CY + 16, CZ), F32), DMA(())],
        compiler_params=pltpu.CompilerParams(dimension_semantics=("arbitrary",), vmem_limit_bytes=60 << 20),
        cost_estimate=pl.CostEstimate(flops=60 * 10**6, bytes_accessed=40 << 20, transcendentals=0),
        name="advance_end" if second else "advance_mid",
    )(coupling, rows, field, *streams, volume)


def exchange(sent):
    return lax.all_to_all(sent, ("comp", "blk"), split_axis=0, concat_axis=0, tiled=True)


def halos(low, high):
    count = lax.axis_size("blk")
    below = lax.ppermute(high, "blk", [(i, i + 1) for i in range(count - 1)])
    above = lax.ppermute(low, "blk", [(i + 1, i) for i in range(count - 1)])
    return below, above


def shards(psi_start, adj_source, vol_inverse, coupling, send_tile, send_count, send_weight, recv_slot, fringe_row):
    start = psi_start[0]
    source = adj_source[0]
    volume = vol_inverse[0]
    matrices = coupling[0].reshape(6, NVAR * NVAR)
    tables = [send_tile[0].T, send_count, send_weight[0].T]
    slots = recv_slot[0].reshape(COMPS, BLOCKS * CAP)

    arrived = exchange(pack(tables, start.reshape(NVAR, ROWS, CZ)))
    below, above = halos(start[:, 0], start[:, -1])
    mid = advance(False, matrices, fringe_row, start, [source], volume).reshape(NVAR, ROWS, CZ)
    sent, mid, low, high = middle(matrices, fringe_row, slots, tables, arrived, mid, below, above, volume)
    arrived = exchange(sent)
    below, above = halos(low, high)
    end = advance(True, matrices, fringe_row, mid.reshape(NVAR, CX, CY, CZ), [start, source], volume)
    end = finish(matrices, fringe_row, slots, arrived, end.reshape(NVAR, ROWS, CZ), below, above, volume)
    return end.reshape(1, NVAR, CX, CY, CZ)


def solution(mesh):
    in_specs = (
        P("comp", None, "blk", None, None),
        P("comp", None, "blk", None, None),
        P("comp", "blk", None, None),
        P("comp", None, None, None),
        P(("comp", "blk"), None, None),
        P(("comp", "blk"), None),
        P(("comp", "blk"), None, None),
        P(("comp", "blk"), None, None),
        P(("comp", "blk"), None),
    )
    out_specs = P("comp", None, "blk", None, None)
    return jax.shard_map(shards, mesh=mesh, in_specs=in_specs, out_specs=out_specs, check_vma=False)
```

time: 284 us -> 129 us (0.45); the launches traced: 279 us -> 128 us
  matrix products: 110 us -> 0 us
  Pallas kernels: 0 us -> 54.4 us
  other arithmetic: 46.2 us -> 1.39 us
  local copies, waits for them, and re-layouts: 47.3 us -> 9.02 us
  waiting for transfers between devices: 38.6 us -> 31.9 us
  starting transfers between devices: 37.3 us -> 30.7 us
    dot_general x16 -> x0, matrix products: 110 us -> none  [the longest x14 103 us: apply_block(): jnp.einsum('vu,vxyz->uxyz', matrix, values, precision=lax.Precision.HIGHEST)]
    pallas_call x0 -> x5, Pallas kernels: none -> 54.4 us  [the longest x2 33.5 us: advance(): pl.pallas_call(functools.partial(flux_kernel, second), grid=(CX,), in_spe...]
    all_to_all x2, waiting for transfers between devices: 38.6 us -> 2.88 us  [exchange(): lax.all_to_all(sent, ('comp', 'blk'), split_axis=0, concat_axis=0, tiled=...]
    ppermute x4, waiting for transfers between devices: 0.01 us -> 29 us  [the longest x2 15.6 us: halos(): below = lax.ppermute(high, 'blk', [(i, i + 1) for i in range(count - 1)])]
    gather x4 -> x0, local copies, waits for them, and re-layouts: 26.3 us -> none  [the longest x2 20.8 us: fringe_values(): picked = jnp.take(flat, send_tile.reshape(-1), axis=1)]
    mul x4 -> x0, other arithmetic: 20 us -> none  [the longest x2 14.6 us: fringe_values(): picked * scale[None, :, None]]
    scatter-add x2 -> x0, other arithmetic: 13.6 us -> none  [residual_of(): rate_flat.at[:, rows, :].add(PENALTY * (interp - field_flat[:, rows, :]))]
    add x3 -> x0, other arithmetic: 12.5 us -> none  [the longest x2 10 us: shards(): middle = start + TIME_STEP * first]
  transfers between devices with their start and end apart: 6 -> 6, of which waited for: 1 -> 5; matrix products, arithmetic and copies ran while one was open for 38% -> 6% of each run, Pallas kernels for 0% -> 26%
where the time goes in v2:
time: 129 us; the launch traced here: 128 us
  Pallas kernels  54.4 us (42%)
  waiting for transfers between devices  31.9 us (25%)
  starting transfers between devices  30.7 us (24%)
  local copies, waits for them, and re-layouts  9.02 us (7%)
  other arithmetic  1.39 us (1%)
    pallas_call x2, Pallas kernels, advance(): pl.pallas_call(functools.partial(flux_kernel, second), grid=(CX,), in_spe...  33.5 us
    pallas_call x3, Pallas kernels, call(): pl.pallas_call(kernel, in_specs=specs, out_specs=HBM if single else [HBM]...  20.9 us
    all_to_all x2, starting transfers between devices, exchange(): lax.all_to_all(sent, ('comp', 'blk'), split_axis=0, concat_axis=0, tiled=...  19.6 us
    ppermute x2, waiting for transfers between devices, halos(): below = lax.ppermute(high, 'blk', [(i, i + 1) for i in range(count - 1)])  15.6 us
    ppermute x2, waiting for transfers between devices, halos(): above = lax.ppermute(low, 'blk', [(i + 1, i) for i in range(count - 1)])  13.5 us
    ppermute x2, starting transfers between devices, halos(): below = lax.ppermute(high, 'blk', [(i, i + 1) for i in range(count - 1)])  6.27 us
    ppermute x2, starting transfers between devices, halos(): above = lax.ppermute(low, 'blk', [(i + 1, i) for i in range(count - 1)])  4.88 us
    unnamed x11, local copies, waits for them, and re-layouts  4.03 us
  transfers between devices with their start and end apart: 6, of which 5 were waited for; matrix products, arithmetic and copies ran while one was open for 6% of the time, Pallas kernels for 26%

profile of v2, /device:TPU:1, one launch (start us, length us, event | category | flops | bytes accessed | tf_op | source)
XLA Modules:
  0.0 127.6 jit_solution(7731716353679123202)
XLA Ops:
  0.0 6.0 %pack.1 = f32[128,48,128]{2,1,0:T(8,128)} custom-call(s32[8,128]{1,0:T(8,128)} %bitcast.31, s32[1,128]{1,0:T(1,128)} %count.3, f32[8,128]{1,0:T(8,128)} %bitcast.33, f32[6,1024,128]{2,1,0:T(8,128)} %bitcast.18), custom_call_target="tpu_custom_call" | custom-call | flops 1000000 | bytes 8388608 | tf_op jit(solution)/shard_map/pack/pallas_call | solution.py:270
  6.0 0.0 copy-start.4
  6.0 11.5 %all-to-all-start = ((f32[128,48,128]{2,1,0:T(8,128)}), f32[128,48,128]{2,1,0:T(8,128)S(1)}, u32[]{:S(2)}, u32[]{:S(2)}) async-start(f32[128,48,128]{2,1,0:T(8,128)} %pack.1), calls=%async_computation | async-start | bytes 6291456 | tf_op jit(solution)/shard_map/all_to_all | solution.py:323
  17.5 2.1 %slice_bitcast_fusion = (f32[6,128,128]{2,1,0:T(8,128)}, f32[6,128,128]{2,1,0:T(8,128)}) fusion(f32[6,8,128,128]{3,2,1,0:T(8,128)} %bitcast.19), kind=kLoop, calls=%fused_computation | loop fusion | bytes 1572864 | tf_op jit(solution)/shard_map/squeeze | solution.py:342
  19.6 3.0 %collective-permute-start.1 = (f32[6,128,128]{2,1,0:T(8,128)}, f32[6,128,128]{2,1,0:T(8,128)S(1)}, u32[]{:S(2)}, u32[]{:S(2)}) collective-permute-start(f32[6,128,128]{2,1,0:T(8,128)} %get-tuple-element.13), channel_id=1, source_target_pairs={{1,0},{2,1},{3,2},{4,3},{5,4},{6,5},{7,6},{8,7},{9,8},{10,9},{11,1... | collective-permute-start | bytes 1179656 | tf_op jit(solution)/shard_map/ppermute | solution.py:329
  22.5 2.6 %collective-permute-start = (f32[6,128,128]{2,1,0:T(8,128)}, f32[6,128,128]{2,1,0:T(8,128)}, u32[]{:S(2)}, u32[]{:S(2)}) collective-permute-start(f32[6,128,128]{2,1,0:T(8,128)} %get-tuple-element.14), channel_id=1, source_target_pairs={{0,1},{1,2},{2,3},{3,4},{4,5},{5,6},{6,7},{7,8},{8,9},{9,10},{10,1... | collective-permute-start | bytes 1179656 | tf_op jit(solution)/shard_map/ppermute | solution.py:328
  25.1 1.4 %reduce = f32[6,6,6]{2,1,0:T(8,128)} reduce(f32[1,6,6,6]{3,0,2,1:T(1,128)} %param.12, f32[]{:T(128)} %constant.9), dimensions={0}, to_apply=%param.12.reduce_sub_computation | reduce | bytes 1732 | tf_op args[3]
  26.5 1.4 %reshape_squeeze.9.coupling = f32[6,36]{1,0:T(8,128)} reshape(f32[6,6,6]{2,1,0:T(8,128)} %reduce) | data formatting | bytes 1728 | tf_op jit(solution)/shard_map/reshape;squeeze | solution.py:337
  27.9 0.0 copy-done.4
  27.9 0.7 copy.11
  28.7 1.5 %reshape_squeeze.10.slots = s32[4,256]{1,0:T(4,128)} reshape(s32[1,128,8]{2,1,0:T(8,128)} %copy.11) | data formatting | bytes 8192 | tf_op jit(solution)/shard_map/reshape;squeeze | solution.py:339
  30.2 16.5 %advance_mid.1 = f32[6,8,128,128]{3,2,1,0:T(8,128)} custom-call(f32[6,36]{1,0:T(8,128)} %reshape_squeeze.9.coupling, s32[1,64]{1,0:T(1,128)} %rows.7, f32[6,8,128,128]{3,2,1,0:T(8,128)} %bitcast.20, f32[6,8,128,128]{3,2,1,0:T(8,128)} %bitcast.22, f32[8,128,128]{2,1,0:T(8,128)} %bitcast.26), custom_call_target="tpu_custom_call" | custom-call | flops 60000000 | bytes 41943040 | tf_op jit(solution)/shard_map/advance_mid/pallas_call | solution.py:307
  46.7 11.2 %collective-permute-done.1.above = f32[6,128,128]{2,1,0:T(8,128)S(1)} collective-permute-done((f32[6,128,128]{2,1,0:T(8,128)}, f32[6,128,128]{2,1,0:T(8,128)S(1)}, u32[]{:S(2)}, u32[]{:S(2)}) %collective-permute-start.1) | collective-permute-done | bytes 393248 | tf_op jit(solution)/shard_map/ppermute | solution.py:329
  57.9 0.0 copy-start.2
  57.9 0.0 collective-permute-done.below
  57.9 1.4 %all-to-all-done.arrived = f32[128,48,128]{2,1,0:T(8,128)S(1)} async-done(((f32[128,48,128]{2,1,0:T(8,128)}), f32[128,48,128]{2,1,0:T(8,128)S(1)}, u32[]{:S(2)}, u32[]{:S(2)}) %all-to-all-start) | async-done | bytes 3145760 | tf_op jit(solution)/shard_map/all_to_all | solution.py:323
  59.3 0.0 copy-start
  59.3 0.0 copy-done.2
  59.3 1.7 %copy-done = f32[128,48,128]{2,1,0:T(8,128)} copy-done((f32[128,48,128]{2,1,0:T(8,128)}, f32[128,48,128]{2,1,0:T(8,128)S(1)}, u32[]{:S(2)}) %copy-start) | copy-done | bytes 3145752
  61.0 8.8 %middle.1 = (f32[128,48,128]{2,1,0:T(8,128)}, f32[6,1024,128]{2,1,0:T(8,128)}, f32[6,128,128]{2,1,0:T(8,128)}, f32[6,128,128]{2,1,0:T(8,128)}) custom-call(f32[6,36]{1,0:T(8,128)} %reshape_squeeze.9.coupling, s32[1,64]{1,0:T(1,128)} %rows.7, s32[4,256]{1,0:T(4,128)} %reshape_squeeze.10.slots, s32[8,128]{1,0:T(8,128)} %bitcast.32, s32[1,128]{1,0:T(1,128)} %count.3, ...), custom_call_target="tpu_custom_call" | custom-call | flops 100000000 | bytes 16777216 | tf_op jit(solution)/shard_map/middle/pallas_call | solution.py:270
  69.8 8.1 %all-to-all-start.1 = ((f32[128,48,128]{2,1,0:T(8,128)}), f32[128,48,128]{2,1,0:T(8,128)S(1)}, u32[]{:S(2)}, u32[]{:S(2)}) async-start(f32[128,48,128]{2,1,0:T(8,128)} %get-tuple-element.9), calls=%async_computation.1 | async-start | bytes 6291456 | tf_op jit(solution)/shard_map/all_to_all | solution.py:323
  77.9 3.7 %collective-permute-start.2 = (f32[6,128,128]{2,1,0:T(8,128)}, f32[6,128,128]{2,1,0:T(8,128)S(1)}, u32[]{:S(2)}, u32[]{:S(2)}) collective-permute-start(f32[6,128,128]{2,1,0:T(8,128)} %get-tuple-element.11), channel_id=1, source_target_pairs={{0,1},{1,2},{2,3},{3,4},{4,5},{5,6},{6,7},{7,8},{8,9},{9,10},{10,1... | collective-permute-start | bytes 1179656 | tf_op jit(solution)/shard_map/ppermute | solution.py:328
  81.5 1.9 %collective-permute-start.3 = (f32[6,128,128]{2,1,0:T(8,128)}, f32[6,128,128]{2,1,0:T(8,128)}, u32[]{:S(2)}, u32[]{:S(2)}) collective-permute-start(f32[6,128,128]{2,1,0:T(8,128)} %get-tuple-element.12), channel_id=1, source_target_pairs={{1,0},{2,1},{3,2},{4,3},{5,4},{6,5},{7,6},{8,7},{9,8},{10,9},{11,1... | collective-permute-start | bytes 1179656 | tf_op jit(solution)/shard_map/ppermute | solution.py:329
  83.5 16.9 %advance_end.1 = f32[6,8,128,128]{3,2,1,0:T(8,128)} custom-call(f32[6,36]{1,0:T(8,128)} %reshape_squeeze.9.coupling, s32[1,64]{1,0:T(1,128)} %rows.7, f32[6,8,128,128]{3,2,1,0:T(8,128)} %bitcast.30, f32[6,8,128,128]{3,2,1,0:T(8,128)} %bitcast.21, f32[6,8,128,128]{3,2,1,0:T(8,128)} %bitcast.23, f32[8,128,128]{2,1,0:T(8,128)} %bitcast.28), custom_call_target="tpu_custom_call" | custom-call | flops 60000000 | bytes 41943040 | tf_op jit(solution)/shard_map/advance_end/pallas_call | solution.py:307
  100.4 15.6 %collective-permute-done.2.below = f32[6,128,128]{2,1,0:T(8,128)S(1)} collective-permute-done((f32[6,128,128]{2,1,0:T(8,128)}, f32[6,128,128]{2,1,0:T(8,128)S(1)}, u32[]{:S(2)}, u32[]{:S(2)}) %collective-permute-start.2) | collective-permute-done | bytes 393248 | tf_op jit(solution)/shard_map/ppermute | solution.py:328
  116.0 0.0 copy-start.3
  116.0 2.3 %collective-permute-done.3.above = f32[6,128,128]{2,1,0:T(8,128)} collective-permute-done((f32[6,128,128]{2,1,0:T(8,128)}, f32[6,128,128]{2,1,0:T(8,128)}, u32[]{:S(2)}, u32[]{:S(2)}) %collective-permute-start.3) | collective-permute-done | bytes 393248 | tf_op jit(solution)/shard_map/ppermute | solution.py:329
  118.3 1.4 %all-to-all-done.1.arrived = f32[128,48,128]{2,1,0:T(8,128)S(1)} async-done(((f32[128,48,128]{2,1,0:T(8,128)}), f32[128,48,128]{2,1,0:T(8,128)S(1)}, u32[]{:S(2)}, u32[]{:S(2)}) %all-to-all-start.1) | async-done | bytes 3145760 | tf_op jit(solution)/shard_map/all_to_all | solution.py:323
  119.7 0.0 copy-start.1
  119.7 0.0 copy-done.3
  119.7 1.6 %copy-done.1 = f32[128,48,128]{2,1,0:T(8,128)} copy-done((f32[128,48,128]{2,1,0:T(8,128)}, f32[128,48,128]{2,1,0:T(8,128)S(1)}, u32[]{:S(2)}) %copy-start.1) | copy-done | bytes 3145752
  121.3 6.2 %finish.1 = f32[6,1024,128]{2,1,0:T(8,128)} custom-call(f32[6,36]{1,0:T(8,128)} %reshape_squeeze.9.coupling, s32[1,64]{1,0:T(1,128)} %rows.7, s32[4,256]{1,0:T(4,128)} %reshape_squeeze.10.slots, f32[128,48,128]{2,1,0:T(8,128)} %copy-done.1, f32[6,1024,128]{2,1,0:T(8,128)} %bitcast.25, f32[6,128,128]{2,1,0:T(8,128)} %copy-done.3, ...), custom_call_target="tpu_custom_call" | custom-call | flops 100000000 | bytes 10485760 | tf_op jit(solution)/shard_map/finish/pallas_call | solution.py:270
Async XLA Ops:
  6.0 22.0 %copy-start.4 = (s32[1,128,8]{1,2,0:T(8,128)S(1)}, s32[1,128,8]{1,2,0:T(8,128)}, u32[]{:S(2)}) copy-start(s32[1,128,8]{1,2,0:T(8,128)} %param.16) | copy-start | bytes 12292
  6.0 53.4 %all-to-all-start = ((f32[128,48,128]{2,1,0:T(8,128)}), f32[128,48,128]{2,1,0:T(8,128)S(1)}, u32[]{:S(2)}, u32[]{:S(2)}) async-start(f32[128,48,128]{2,1,0:T(8,128)} %pack.1), calls=%async_computation | async-start | bytes 6291456 | tf_op jit(solution)/shard_map/all_to_all | solution.py:323
  19.6 38.3 %collective-permute-start.1 = (f32[6,128,128]{2,1,0:T(8,128)}, f32[6,128,128]{2,1,0:T(8,128)S(1)}, u32[]{:S(2)}, u32[]{:S(2)}) collective-permute-start(f32[6,128,128]{2,1,0:T(8,128)} %get-tuple-element.13), channel_id=1, source_target_pairs={{1,0},{2,1},{3,2},{4,3},{5,4},{6,5},{7,6},{8,7},{9,8},{10,9},{11,1... | collective-permute-start | bytes 1179656 | tf_op jit(solution)/shard_map/ppermute | solution.py:329
  22.5 35.4 %collective-permute-start = (f32[6,128,128]{2,1,0:T(8,128)}, f32[6,128,128]{2,1,0:T(8,128)}, u32[]{:S(2)}, u32[]{:S(2)}) collective-permute-start(f32[6,128,128]{2,1,0:T(8,128)} %get-tuple-element.14), channel_id=1, source_target_pairs={{0,1},{1,2},{2,3},{3,4},{4,5},{5,6},{6,7},{7,8},{8,9},{9,10},{10,1... | collective-permute-start | bytes 1179656 | tf_op jit(solution)/shard_map/ppermute | solution.py:328
  57.9 1.4 %copy-start.2 = (f32[6,128,128]{2,1,0:T(8,128)}, f32[6,128,128]{2,1,0:T(8,128)S(1)}, u32[]{:S(2)}) copy-start(f32[6,128,128]{2,1,0:T(8,128)S(1)} %collective-permute-done.1.above) | copy-start | bytes 1179652
  59.3 1.7 %copy-start = (f32[128,48,128]{2,1,0:T(8,128)}, f32[128,48,128]{2,1,0:T(8,128)S(1)}, u32[]{:S(2)}) copy-start(f32[128,48,128]{2,1,0:T(8,128)S(1)} %all-to-all-done.arrived) | copy-start | bytes 9437188
  69.8 49.9 %all-to-all-start.1 = ((f32[128,48,128]{2,1,0:T(8,128)}), f32[128,48,128]{2,1,0:T(8,128)S(1)}, u32[]{:S(2)}, u32[]{:S(2)}) async-start(f32[128,48,128]{2,1,0:T(8,128)} %get-tuple-element.9), calls=%async_computation.1 | async-start | bytes 6291456 | tf_op jit(solution)/shard_map/all_to_all | solution.py:323
  77.9 38.1 %collective-permute-start.2 = (f32[6,128,128]{2,1,0:T(8,128)}, f32[6,128,128]{2,1,0:T(8,128)S(1)}, u32[]{:S(2)}, u32[]{:S(2)}) collective-permute-start(f32[6,128,128]{2,1,0:T(8,128)} %get-tuple-element.11), channel_id=1, source_target_pairs={{0,1},{1,2},{2,3},{3,4},{4,5},{5,6},{6,7},{7,8},{8,9},{9,10},{10,1... | collective-permute-start | bytes 1179656 | tf_op jit(solution)/shard_map/ppermute | solution.py:328
  81.5 36.7 %collective-permute-start.3 = (f32[6,128,128]{2,1,0:T(8,128)}, f32[6,128,128]{2,1,0:T(8,128)}, u32[]{:S(2)}, u32[]{:S(2)}) collective-permute-start(f32[6,128,128]{2,1,0:T(8,128)} %get-tuple-element.12), channel_id=1, source_target_pairs={{1,0},{2,1},{3,2},{4,3},{5,4},{6,5},{7,6},{8,7},{9,8},{10,9},{11,1... | collective-permute-start | bytes 1179656 | tf_op jit(solution)/shard_map/ppermute | solution.py:329
  116.0 3.7 %copy-start.3 = (f32[6,128,128]{2,1,0:T(8,128)}, f32[6,128,128]{2,1,0:T(8,128)S(1)}, u32[]{:S(2)}) copy-start(f32[6,128,128]{2,1,0:T(8,128)S(1)} %collective-permute-done.2.below) | copy-start | bytes 1179652
  119.7 1.6 %copy-start.1 = (f32[128,48,128]{2,1,0:T(8,128)}, f32[128,48,128]{2,1,0:T(8,128)S(1)}, u32[]{:S(2)}) copy-start(f32[128,48,128]{2,1,0:T(8,128)S(1)} %all-to-all-done.1.arrived) | copy-start | bytes 9437188

commit v3 on v2

--- a/solution.py
+++ b/solution.py
@@ -19,10 +19,11 @@
 OTHERS = COMPS - 1
 PACK = NVAR * CAP
 BAND = 32
+EDGE = 8
+VMEM_LIMIT = 67_000_000
 F32 = jnp.float32
 HBM = pl.BlockSpec(memory_space=pltpu.HBM)
 SMEM = pl.BlockSpec(memory_space=pltpu.SMEM)
-ANY = pl.BlockSpec(memory_space=pl.ANY)
 DMA = pltpu.SemaphoreType.DMA
 
 
@@ -52,12 +53,9 @@
     return ref.at[pl.ds(j * BLOCKS, BLOCKS)]
 
 
-def table_copies(tables, scratch, sems):
-    return [pltpu.make_async_copy(a, b, sems.at[i]) for i, (a, b) in enumerate(zip(tables, scratch))]
-
-
 def gather_rows(field, tables, buf, sent, sems):
     tile, count, weight = tables
+    row_ids = lax.broadcasted_iota(jnp.int32, (CAP, CZ), 0)
     stores = []
     for j in range(OTHERS):
         first = other(j) * BLOCKS
@@ -65,11 +63,16 @@
         def peer_rows(b, carry):
             peer = first + b
             live = count[0, peer]
-            for e in range(CAP):
-                t = tile[e, peer]
-                w = jnp.where(e < live, weight[e, peer], 0.0)
-                for v in range(NVAR):
-                    buf[j * BLOCKS + b, pl.ds(v * CAP + e, 1), :] = field[v, pl.ds(t, 1), :] * w
+            spots = [tile[e, peer] + (EDGE - e) for e in range(CAP)]
+            scale = jnp.full((CAP, CZ), weight[0, peer])
+            for e in range(1, CAP):
+                scale = jnp.where(row_ids == e, weight[e, peer], scale)
+            scale = jnp.where(row_ids < live, scale, 0.0)
+            for v in range(NVAR):
+                rows = field[v, pl.ds(spots[0], CAP), :]
+                for e in range(1, CAP):
+                    rows = jnp.where(row_ids == e, field[v, pl.ds(spots[e], CAP), :], rows)
+                buf[j * BLOCKS + b, v * CAP : (v + 1) * CAP, :] = rows * scale
             return carry
 
         lax.fori_loop(0, BLOCKS, peer_rows, 0)
@@ -93,7 +96,7 @@
 
 
 def add_halos(field, coupling, below, above, volume, scale):
-    for side, halo, first in ((1, below, 0), (0, above, ROWS - CY)):
+    for side, halo, first in ((1, below, EDGE), (0, above, EDGE + ROWS - CY)):
 
         def band(i, carry):
             y = pl.multiple_of(i * BAND, BAND)
@@ -111,7 +114,7 @@
 
 def patch_rows(field, rows, total, scale):
     def patch(s, carry):
-        t = rows[0, s]
+        t = rows[0, s] + EDGE
         for v in range(NVAR):
             field[v, pl.ds(t, 1), :] += scale * total[v, pl.ds(s, 1), :]
         return carry
@@ -119,60 +122,61 @@
     lax.fori_loop(0, SLOTS, patch, 0)
 
 
+def inner(field, first=0, size=ROWS):
+    return field.at[:, pl.ds(EDGE + first, size), :]
+
+
+def copies_of(pairs, sems, first=0):
+    return [pltpu.make_async_copy(a, b, sems.at[first + i]) for i, (a, b) in enumerate(pairs)]
+
+
 def pack_kernel(tile, count, weight, field, sent, tile_s, count_s, weight_s, field_v, buf, sems, sent_sems):
     scratch = (tile_s, count_s, weight_s)
-    copies = table_copies((tile, count, weight), scratch, sems)
-    copies.append(pltpu.make_async_copy(field, field_v, sems.at[3]))
+    pairs = list(zip((tile, count, weight), scratch)) + [(field, inner(field_v))]
+    copies = copies_of(pairs, sems)
     start_all(copies)
     wait_all(copies)
     wait_all(gather_rows(field_v, scratch, buf, sent, sent_sems))
 
 
-def arrive(slots, arrived, guess, below, above, volume, data, total, field, below_v, above_v, volume_v, sems):
-    copies = [
-        pltpu.make_async_copy(guess, field, sems.at[3]),
-        pltpu.make_async_copy(below, below_v, sems.at[4]),
-        pltpu.make_async_copy(above, above_v, sems.at[5]),
-        pltpu.make_async_copy(volume.at[0], volume_v.at[0], sems.at[6]),
-        pltpu.make_async_copy(volume.at[CX - 1], volume_v.at[1], sems.at[7]),
-    ]
-    loads = [pltpu.make_async_copy(block_of(arrived, j), part_of(data, j), sems.at[j]) for j in range(OTHERS)]
-    start_all(loads + copies)
-    reduce_rows(slots, loads, data, total)
-    wait_all(copies)
-
-
-def middle_kernel(
-    coupling, rows, slots, tile, count, weight, arrived, guess, below, above, volume,
-    sent, mid, low, high,
-    tile_s, count_s, weight_s, data, total, field, below_v, above_v, volume_v, sems, table_sems, sent_sems,
-):
-    scratch = (tile_s, count_s, weight_s)
-    tables = table_copies((tile, count, weight), scratch, table_sems)
-    start_all(tables)
-    arrive(slots, arrived, guess, below, above, volume, data, total, field, below_v, above_v, volume_v, sems)
-    add_halos(field, coupling, below_v, above_v, volume_v, TIME_STEP)
+def arrive(inputs, scratch, sems):
+    coupling, rows, slots, arrived, guess, below, above, volume = inputs
+    coupling_s, rows_s, slots_v, data, total, field, below_v, above_v, volume_v = scratch
+    loads = [(slots, slots_v)] + [(block_of(arrived, j), part_of(data, j)) for j in range(OTHERS)]
+    others = [(guess, inner(field)), (coupling, coupling_s), (rows, rows_s), (below, below_v), (above, above_v)]
+    others += [(volume.at[0], volume_v.at[0]), (volume.at[CX - 1], volume_v.at[1])]
+    loads = copies_of(loads, sems)
+    others = copies_of(others, sems, len(loads))
+    start_all(loads + others)
+    loads[0].wait()
+    reduce_rows(slots_v, loads[1:], data, total)
+    wait_all(others)
+
+
+def middle_kernel(*refs):
+    tables, inputs, refs = refs[:3], refs[3:11], refs[11:]
+    sent, mid, low, high, refs = *refs[:4], refs[4:]
+    table_scratch, scratch, (sems, table_sems, sent_sems) = refs[:3], refs[3:12], refs[12:]
+    coupling, rows, _, data, total, field, below, above, volume = scratch
+    table_copies = copies_of(list(zip(tables, table_scratch)), table_sems)
+    start_all(table_copies)
+    arrive(inputs, scratch, sems)
+    add_halos(field, coupling, below, above, volume, TIME_STEP)
     patch_rows(field, rows, total, TIME_STEP * PENALTY)
-    stores = [
-        pltpu.make_async_copy(field.at[:, pl.ds(0, CY), :], low, sems.at[0]),
-        pltpu.make_async_copy(field.at[:, pl.ds(ROWS - CY, CY), :], high, sems.at[1]),
-        pltpu.make_async_copy(field, mid, sems.at[2]),
-    ]
+    stores = copies_of([(inner(field), mid), (inner(field, 0, CY), low), (inner(field, ROWS - CY, CY), high)], sems)
     start_all(stores)
-    wait_all(tables)
-    wait_all(gather_rows(field, scratch, data, sent, sent_sems))
+    wait_all(table_copies)
+    wait_all(gather_rows(field, table_scratch, data, sent, sent_sems))
     wait_all(stores)
 
 
-def finish_kernel(
-    coupling, rows, slots, arrived, guess, below, above, volume,
-    end,
-    data, total, field, below_v, above_v, volume_v, sems,
-):
-    arrive(slots, arrived, guess, below, above, volume, data, total, field, below_v, above_v, volume_v, sems)
-    add_halos(field, coupling, below_v, above_v, volume_v, 0.5 * TIME_STEP)
+def finish_kernel(*refs):
+    inputs, end, scratch, sems = refs[:8], refs[8], refs[9:18], refs[18]
+    coupling, rows, _, _, total, field, below, above, volume = scratch
+    arrive(inputs, scratch, sems)
+    add_halos(field, coupling, below, above, volume, 0.5 * TIME_STEP)
     patch_rows(field, rows, total, 0.5 * TIME_STEP * PENALTY)
-    stores = [pltpu.make_async_copy(field.at[v], end.at[v], sems.at[v]) for v in range(NVAR)]
+    stores = copies_of([(inner(field), end)], sems)
     start_all(stores)
     wait_all(stores)
 
@@ -251,29 +255,31 @@
     pltpu.SMEM((1, PEERS), jnp.int32),
     pltpu.SMEM((CAP, PEERS), F32),
 ]
-FIELD_V = pltpu.VMEM((NVAR, ROWS, CZ), F32)
+FIELD_V = pltpu.VMEM((NVAR, ROWS + 2 * EDGE, CZ), F32)
 DATA_V = pltpu.VMEM((OTHERS * BLOCKS, PACK, CZ), F32)
 ARRIVE = [
+    pltpu.SMEM((6, NVAR * NVAR), F32),
+    pltpu.SMEM((1, SLOTS), jnp.int32),
+    pltpu.VMEM((COMPS, BLOCKS * CAP), jnp.int32),
     DATA_V,
     pltpu.VMEM((NVAR, SLOTS, CZ), F32),
     FIELD_V,
     pltpu.VMEM((NVAR, CY, CZ), F32),
     pltpu.VMEM((NVAR, CY, CZ), F32),
     pltpu.VMEM((2, CY, CZ), F32),
-    DMA((8,)),
+    DMA((12,)),
 ]
-SLOT_ROWS = pl.BlockSpec((COMPS, BLOCKS * CAP), lambda: (0, 0))
-
-
-def call(kernel, name, specs, inputs, out_shape, scratch, moved, flops):
+
+
+def call(kernel, name, inputs, out_shape, scratch, moved, flops):
     single = not isinstance(out_shape, list)
     return pl.pallas_call(
         kernel,
-        in_specs=specs,
+        in_specs=[HBM] * len(inputs),
         out_specs=HBM if single else [HBM] * len(out_shape),
         out_shape=out_shape,
         scratch_shapes=scratch,
-        compiler_params=pltpu.CompilerParams(vmem_limit_bytes=60 << 20),
+        compiler_params=pltpu.CompilerParams(vmem_limit_bytes=VMEM_LIMIT),
         cost_estimate=pl.CostEstimate(flops=flops, bytes_accessed=moved, transcendentals=0),
         name=name,
     )(*inputs)
@@ -281,26 +287,22 @@
 
 def pack(tables, field):
     return call(
-        pack_kernel, "pack", [HBM] * 4, [*tables, field], shape(PEERS, PACK, CZ),
+        pack_kernel, "pack", [*tables, field], shape(PEERS, PACK, CZ),
         [*TABLES, FIELD_V, DATA_V, DMA((4,)), DMA((OTHERS,))], 8 << 20, 10**6,
     )
 
 
-def middle(matrices, rows, slots, tables, arrived, mid, below, above, volume):
+def middle(tables, inputs):
+    plane = shape(NVAR, CY, CZ)
     return call(
-        middle_kernel, "middle", [SMEM, SMEM, SLOT_ROWS, HBM, HBM, HBM, ANY, HBM, ANY, ANY, HBM],
-        [matrices, rows, slots, *tables, arrived, mid, below, above, volume],
-        [shape(PEERS, PACK, CZ), shape(NVAR, ROWS, CZ), shape(NVAR, CY, CZ), shape(NVAR, CY, CZ)],
+        middle_kernel, "middle", [*tables, *inputs],
+        [shape(PEERS, PACK, CZ), shape(NVAR, ROWS, CZ), plane, plane],
         [*TABLES, *ARRIVE, DMA((3,)), DMA((OTHERS,))], 16 << 20, 10**8,
     )
 
 
-def finish(matrices, rows, slots, arrived, end, below, above, volume):
-    return call(
-        finish_kernel, "finish", [SMEM, SMEM, SLOT_ROWS, ANY, HBM, ANY, ANY, HBM],
-        [matrices, rows, slots, arrived, end, below, above, volume],
-        shape(NVAR, ROWS, CZ), ARRIVE, 10 << 20, 10**8,
-    )
+def finish(inputs):
+    return call(finish_kernel, "finish", inputs, shape(NVAR, ROWS, CZ), ARRIVE, 10 << 20, 10**8)
 
 
 def advance(second, coupling, rows, field, streams, volume):
@@ -313,7 +315,7 @@
         out_specs=pl.BlockSpec((NVAR, CX, CY, CZ), lambda i: (0, 0, 0, 0)),
         out_shape=shape(NVAR, CX, CY, CZ),
         scratch_shapes=[pltpu.VMEM((NVAR, CX + 2, CY + 16, CZ), F32), DMA(())],
-        compiler_params=pltpu.CompilerParams(dimension_semantics=("arbitrary",), vmem_limit_bytes=60 << 20),
+        compiler_params=pltpu.CompilerParams(dimension_semantics=("arbitrary",), vmem_limit_bytes=VMEM_LIMIT),
         cost_estimate=pl.CostEstimate(flops=60 * 10**6, bytes_accessed=40 << 20, transcendentals=0),
         name="advance_end" if second else "advance_mid",
     )(coupling, rows, field, *streams, volume)
@@ -338,14 +340,16 @@
     tables = [send_tile[0].T, send_count, send_weight[0].T]
     slots = recv_slot[0].reshape(COMPS, BLOCKS * CAP)
 
-    arrived = exchange(pack(tables, start.reshape(NVAR, ROWS, CZ)))
+    tiled = (NVAR, ROWS, CZ)
+
+    arrived = exchange(pack(tables, start.reshape(tiled)))
     below, above = halos(start[:, 0], start[:, -1])
-    mid = advance(False, matrices, fringe_row, start, [source], volume).reshape(NVAR, ROWS, CZ)
-    sent, mid, low, high = middle(matrices, fringe_row, slots, tables, arrived, mid, below, above, volume)
+    mid = advance(False, matrices, fringe_row, start, [source], volume).reshape(tiled)
+    sent, mid, low, high = middle(tables, [matrices, fringe_row, slots, arrived, mid, below, above, volume])
     arrived = exchange(sent)
     below, above = halos(low, high)
     end = advance(True, matrices, fringe_row, mid.reshape(NVAR, CX, CY, CZ), [start, source], volume)
-    end = finish(matrices, fringe_row, slots, arrived, end.reshape(NVAR, ROWS, CZ), below, above, volume)
+    end = finish([matrices, fringe_row, slots, arrived, end.reshape(tiled), below, above, volume])
     return end.reshape(1, NVAR, CX, CY, CZ)
 
 

time: 129 us -> 122 us (0.946)
  local copies, waits for them, and re-layouts: 9.02 us -> 3.53 us
  Pallas kernels: 54.4 us -> 51.2 us
  waiting for transfers between devices: 31.9 us -> 34.8 us
  other arithmetic: 1.39 us -> 0.05 us
    unnamed x11 -> x5, local copies, waits for them, and re-layouts: 4.03 us -> 0.11 us
    pallas_call x3, Pallas kernels: 20.9 us -> 17.7 us  [call(): pl.pallas_call(kernel, in_specs=[HBM] * len(inputs), out_specs=HBM if sin...]
    ppermute x2, waiting for transfers between devices: 13.5 us -> 16.2 us  [halos(): above = lax.ppermute(low, 'blk', [(i + 1, i) for i in range(count - 1)])]
    unnamed x1, other arithmetic: 1.39 us -> 0.05 us
  transfers between devices with their start and end apart: 6 -> 6, of which waited for: 5 -> 5; matrix products, arithmetic and copies ran while one was open for 6% -> 3% of each run, Pallas kernels for 26% -> 28%
where the time goes in v3:
time: 122 us; the launch traced here: 121 us
  Pallas kernels  51.2 us (42%)
  waiting for transfers between devices  34.8 us (29%)
  starting transfers between devices  31.4 us (26%)
  local copies, waits for them, and re-layouts  3.53 us (3%)
    pallas_call x2, Pallas kernels, advance(): pl.pallas_call(functools.partial(flux_kernel, second), grid=(CX,), in_spe...  33.5 us
    all_to_all x2, starting transfers between devices, exchange(): lax.all_to_all(sent, ('comp', 'blk'), split_axis=0, concat_axis=0, tiled=...  20.2 us
    pallas_call x3, Pallas kernels, call(): pl.pallas_call(kernel, in_specs=[HBM] * len(inputs), out_specs=HBM if sin...  17.7 us
    ppermute x2, waiting for transfers between devices, halos(): above = lax.ppermute(low, 'blk', [(i + 1, i) for i in range(count - 1)])  16.2 us
    ppermute x2, waiting for transfers between devices, halos(): below = lax.ppermute(high, 'blk', [(i, i + 1) for i in range(count - 1)])  16 us
    ppermute x2, starting transfers between devices, halos(): below = lax.ppermute(high, 'blk', [(i, i + 1) for i in range(count - 1)])  6.2 us
    ppermute x2, starting transfers between devices, halos(): above = lax.ppermute(low, 'blk', [(i + 1, i) for i in range(count - 1)])  4.95 us
    all_to_all x2, waiting for transfers between devices, exchange(): lax.all_to_all(sent, ('comp', 'blk'), split_axis=0, concat_axis=0, tiled=...  2.57 us
  transfers between devices with their start and end apart: 6, of which 5 were waited for; matrix products, arithmetic and copies ran while one was open for 3% of the time, Pallas kernels for 28%

profile of v3, /device:TPU:1, one launch (start us, length us, event | category | flops | bytes accessed | tf_op | source)
XLA Modules:
  0.0 121.1 jit_solution(11591964060330393856)
XLA Ops:
  0.0 5.1 %pack.1 = f32[128,48,128]{2,1,0:T(8,128)} custom-call(s32[8,128]{1,0:T(8,128)} %bitcast.31, s32[1,128]{1,0:T(1,128)} %refs_1_.2, f32[8,128]{1,0:T(8,128)} %bitcast.33, f32[6,1024,128]{2,1,0:T(8,128)} %bitcast.18), custom_call_target="tpu_custom_call" | custom-call | flops 1000000 | bytes 8388608 | tf_op jit(solution)/shard_map/pack/pallas_call | solution.py:276
  5.1 0.0 copy-start
  5.1 0.0 copy-start.1
  5.1 11.9 %all-to-all-start = ((f32[128,48,128]{2,1,0:T(8,128)}), f32[128,48,128]{2,1,0:T(8,128)}, u32[]{:S(2)}, u32[]{:S(2)}) async-start(f32[128,48,128]{2,1,0:T(8,128)} %pack.1), calls=%async_computation | async-start | bytes 6291456 | tf_op jit(solution)/shard_map/all_to_all | solution.py:325
  17.1 2.1 %slice_bitcast_fusion = (f32[6,128,128]{2,1,0:T(8,128)}, f32[6,128,128]{2,1,0:T(8,128)}) fusion(f32[6,8,128,128]{3,2,1,0:T(8,128)} %bitcast.19), kind=kLoop, calls=%fused_computation | loop fusion | bytes 1572864 | tf_op jit(solution)/shard_map/squeeze | solution.py:346
  19.1 3.0 %collective-permute-start.1 = (f32[6,128,128]{2,1,0:T(8,128)}, f32[6,128,128]{2,1,0:T(8,128)}, u32[]{:S(2)}, u32[]{:S(2)}) collective-permute-start(f32[6,128,128]{2,1,0:T(8,128)} %get-tuple-element.13), channel_id=1, source_target_pairs={{1,0},{2,1},{3,2},{4,3},{5,4},{6,5},{7,6},{8,7},{9,8},{10,9},{11,1... | collective-permute-start | bytes 1179656 | tf_op jit(solution)/shard_map/ppermute | solution.py:331
  22.2 2.5 %collective-permute-start = (f32[6,128,128]{2,1,0:T(8,128)}, f32[6,128,128]{2,1,0:T(8,128)}, u32[]{:S(2)}, u32[]{:S(2)}) collective-permute-start(f32[6,128,128]{2,1,0:T(8,128)} %get-tuple-element.14), channel_id=1, source_target_pairs={{0,1},{1,2},{2,3},{3,4},{4,5},{5,6},{6,7},{7,8},{8,9},{9,10},{10,1... | collective-permute-start | bytes 1179656 | tf_op jit(solution)/shard_map/ppermute | solution.py:330
  24.7 0.0 copy-done
  24.7 0.1 reduce
  24.8 0.7 reshape_squeeze.9.coupling.refs_3_.refs_0_
  25.4 0.0 copy-done.1
  25.4 0.1 copy.11
  25.5 0.7 reshape_squeeze.10.refs_5_.refs_2_
  26.2 16.6 %advance_mid.1 = f32[6,8,128,128]{3,2,1,0:T(8,128)} custom-call(f32[6,36]{1,0:T(8,128)} %reshape_squeeze.9.coupling.refs_3_.refs_0_, s32[1,64]{1,0:T(1,128)} %refs_1_.3, f32[6,8,128,128]{3,2,1,0:T(8,128)} %bitcast.20, f32[6,8,128,128]{3,2,1,0:T(8,128)} %bitcast.22, f32[8,128,128]{2,1,0:T(8,128)} %bitcast.26), custom_call_target="tpu_custom_call" | custom-call | flops 60000000 | bytes 41943040 | tf_op jit(solution)/shard_map/advance_mid/pallas_call | solution.py:309
  42.8 14.5 %collective-permute-done.1.refs_9_ = f32[6,128,128]{2,1,0:T(8,128)} collective-permute-done((f32[6,128,128]{2,1,0:T(8,128)}, f32[6,128,128]{2,1,0:T(8,128)}, u32[]{:S(2)}, u32[]{:S(2)}) %collective-permute-start.1) | collective-permute-done | bytes 393248 | tf_op jit(solution)/shard_map/ppermute | solution.py:331
  57.3 0.0 collective-permute-done.refs_8_
  57.3 1.3 %all-to-all-done.refs_6_ = f32[128,48,128]{2,1,0:T(8,128)} async-done(((f32[128,48,128]{2,1,0:T(8,128)}), f32[128,48,128]{2,1,0:T(8,128)}, u32[]{:S(2)}, u32[]{:S(2)}) %all-to-all-start) | async-done | bytes 3145760 | tf_op jit(solution)/shard_map/all_to_all | solution.py:325
  58.6 7.2 %middle.1 = (f32[128,48,128]{2,1,0:T(8,128)}, f32[6,1024,128]{2,1,0:T(8,128)}, f32[6,128,128]{2,1,0:T(8,128)}, f32[6,128,128]{2,1,0:T(8,128)}) custom-call(s32[8,128]{1,0:T(8,128)} %bitcast.32, s32[1,128]{1,0:T(1,128)} %refs_1_.2, f32[8,128]{1,0:T(8,128)} %bitcast.34, f32[6,36]{1,0:T(8,128)} %reshape_squeeze.9.coupling.refs_3_.refs_0_, s32[1,64]{1,0:T(1,128)} %refs_1_.3, ...), custom_call_target="tpu_custom_call" | custom-call | flops 100000000 | bytes 16777216 | tf_op jit(solution)/shard_map/middle/pallas_call | solution.py:276
  65.8 8.3 %all-to-all-start.1 = ((f32[128,48,128]{2,1,0:T(8,128)}), f32[128,48,128]{2,1,0:T(8,128)}, u32[]{:S(2)}, u32[]{:S(2)}) async-start(f32[128,48,128]{2,1,0:T(8,128)} %get-tuple-element.9), calls=%async_computation.1 | async-start | bytes 6291456 | tf_op jit(solution)/shard_map/all_to_all | solution.py:325
  74.2 3.7 %collective-permute-start.2 = (f32[6,128,128]{2,1,0:T(8,128)}, f32[6,128,128]{2,1,0:T(8,128)}, u32[]{:S(2)}, u32[]{:S(2)}) collective-permute-start(f32[6,128,128]{2,1,0:T(8,128)} %get-tuple-element.11), channel_id=1, source_target_pairs={{0,1},{1,2},{2,3},{3,4},{4,5},{5,6},{6,7},{7,8},{8,9},{9,10},{10,1... | collective-permute-start | bytes 1179656 | tf_op jit(solution)/shard_map/ppermute | solution.py:330
  77.8 1.9 %collective-permute-start.3 = (f32[6,128,128]{2,1,0:T(8,128)}, f32[6,128,128]{2,1,0:T(8,128)}, u32[]{:S(2)}, u32[]{:S(2)}) collective-permute-start(f32[6,128,128]{2,1,0:T(8,128)} %get-tuple-element.12), channel_id=1, source_target_pairs={{1,0},{2,1},{3,2},{4,3},{5,4},{6,5},{7,6},{8,7},{9,8},{10,9},{11,1... | collective-permute-start | bytes 1179656 | tf_op jit(solution)/shard_map/ppermute | solution.py:331
  79.8 17.0 %advance_end.1 = f32[6,8,128,128]{3,2,1,0:T(8,128)} custom-call(f32[6,36]{1,0:T(8,128)} %reshape_squeeze.9.coupling.refs_3_.refs_0_, s32[1,64]{1,0:T(1,128)} %refs_1_.3, f32[6,8,128,128]{3,2,1,0:T(8,128)} %bitcast.30, f32[6,8,128,128]{3,2,1,0:T(8,128)} %bitcast.21, f32[6,8,128,128]{3,2,1,0:T(8,128)} %bitcast.23, f32[8,128,128]{2,1,0:T(8,128)} %bitcast.28), custom_call_target="tpu_custom_call" | custom-call | flops 60000000 | bytes 41943040 | tf_op jit(solution)/shard_map/advance_end/pallas_call | solution.py:309
  96.7 16.0 %collective-permute-done.2.refs_5_ = f32[6,128,128]{2,1,0:T(8,128)} collective-permute-done((f32[6,128,128]{2,1,0:T(8,128)}, f32[6,128,128]{2,1,0:T(8,128)}, u32[]{:S(2)}, u32[]{:S(2)}) %collective-permute-start.2) | collective-permute-done | bytes 393248 | tf_op jit(solution)/shard_map/ppermute | solution.py:330
  112.7 1.7 %collective-permute-done.3.refs_6_ = f32[6,128,128]{2,1,0:T(8,128)} collective-permute-done((f32[6,128,128]{2,1,0:T(8,128)}, f32[6,128,128]{2,1,0:T(8,128)}, u32[]{:S(2)}, u32[]{:S(2)}) %collective-permute-start.3) | collective-permute-done | bytes 393248 | tf_op jit(solution)/shard_map/ppermute | solution.py:331
  114.4 1.3 %all-to-all-done.1.refs_3_ = f32[128,48,128]{2,1,0:T(8,128)} async-done(((f32[128,48,128]{2,1,0:T(8,128)}), f32[128,48,128]{2,1,0:T(8,128)}, u32[]{:S(2)}, u32[]{:S(2)}) %all-to-all-start.1) | async-done | bytes 3145760 | tf_op jit(solution)/shard_map/all_to_all | solution.py:325
  115.7 5.4 %finish.1 = f32[6,1024,128]{2,1,0:T(8,128)} custom-call(f32[6,36]{1,0:T(8,128)} %reshape_squeeze.9.coupling.refs_3_.refs_0_, s32[1,64]{1,0:T(1,128)} %refs_1_.3, s32[4,256]{1,0:T(4,128)} %reshape_squeeze.10.refs_5_.refs_2_, f32[128,48,128]{2,1,0:T(8,128)} %all-to-all-done.1.refs_3_, f32[6,1024,128]{2,1,0:T(8,128)} %bitcast.25, ...), custom_call_target="tpu_custom_call" | custom-call | flops 100000000 | bytes 10485760 | tf_op jit(solution)/shard_map/finish/pallas_call | solution.py:276
Async XLA Ops:
  5.1 19.6 %copy-start = (f32[1,6,6,6]{3,0,2,1:T(1,128)S(1)}, f32[1,6,6,6]{3,0,2,1:T(1,128)}, u32[]{:S(2)}) copy-start(f32[1,6,6,6]{3,0,2,1:T(1,128)} %param.12) | copy-start | bytes 2596
  5.1 20.3 %copy-start.1 = (s32[1,128,8]{1,2,0:T(8,128)S(1)}, s32[1,128,8]{1,2,0:T(8,128)}, u32[]{:S(2)}) copy-start(s32[1,128,8]{1,2,0:T(8,128)} %param.16) | copy-start | bytes 12292
  5.1 53.5 %all-to-all-start = ((f32[128,48,128]{2,1,0:T(8,128)}), f32[128,48,128]{2,1,0:T(8,128)}, u32[]{:S(2)}, u32[]{:S(2)}) async-start(f32[128,48,128]{2,1,0:T(8,128)} %pack.1), calls=%async_computation | async-start | bytes 6291456 | tf_op jit(solution)/shard_map/all_to_all | solution.py:325
  19.1 38.2 %collective-permute-start.1 = (f32[6,128,128]{2,1,0:T(8,128)}, f32[6,128,128]{2,1,0:T(8,128)}, u32[]{:S(2)}, u32[]{:S(2)}) collective-permute-start(f32[6,128,128]{2,1,0:T(8,128)} %get-tuple-element.13), channel_id=1, source_target_pairs={{1,0},{2,1},{3,2},{4,3},{5,4},{6,5},{7,6},{8,7},{9,8},{10,9},{11,1... | collective-permute-start | bytes 1179656 | tf_op jit(solution)/shard_map/ppermute | solution.py:331
  22.2 35.2 %collective-permute-start = (f32[6,128,128]{2,1,0:T(8,128)}, f32[6,128,128]{2,1,0:T(8,128)}, u32[]{:S(2)}, u32[]{:S(2)}) collective-permute-start(f32[6,128,128]{2,1,0:T(8,128)} %get-tuple-element.14), channel_id=1, source_target_pairs={{0,1},{1,2},{2,3},{3,4},{4,5},{5,6},{6,7},{7,8},{8,9},{9,10},{10,1... | collective-permute-start | bytes 1179656 | tf_op jit(solution)/shard_map/ppermute | solution.py:330
  65.8 49.9 %all-to-all-start.1 = ((f32[128,48,128]{2,1,0:T(8,128)}), f32[128,48,128]{2,1,0:T(8,128)}, u32[]{:S(2)}, u32[]{:S(2)}) async-start(f32[128,48,128]{2,1,0:T(8,128)} %get-tuple-element.9), calls=%async_computation.1 | async-start | bytes 6291456 | tf_op jit(solution)/shard_map/all_to_all | solution.py:325
  74.2 38.5 %collective-permute-start.2 = (f32[6,128,128]{2,1,0:T(8,128)}, f32[6,128,128]{2,1,0:T(8,128)}, u32[]{:S(2)}, u32[]{:S(2)}) collective-permute-start(f32[6,128,128]{2,1,0:T(8,128)} %get-tuple-element.11), channel_id=1, source_target_pairs={{0,1},{1,2},{2,3},{3,4},{4,5},{5,6},{6,7},{7,8},{8,9},{9,10},{10,1... | collective-permute-start | bytes 1179656 | tf_op jit(solution)/shard_map/ppermute | solution.py:330
  77.8 36.6 %collective-permute-start.3 = (f32[6,128,128]{2,1,0:T(8,128)}, f32[6,128,128]{2,1,0:T(8,128)}, u32[]{:S(2)}, u32[]{:S(2)}) collective-permute-start(f32[6,128,128]{2,1,0:T(8,128)} %get-tuple-element.12), channel_id=1, source_target_pairs={{1,0},{2,1},{3,2},{4,3},{5,4},{6,5},{7,6},{8,7},{9,8},{10,9},{11,1... | collective-permute-start | bytes 1179656 | tf_op jit(solution)/shard_map/ppermute | solution.py:331

commit v4 on v3

--- a/solution.py
+++ b/solution.py
@@ -18,12 +18,17 @@
 PEERS = COMPS * BLOCKS
 OTHERS = COMPS - 1
 PACK = NVAR * CAP
+SPLIT = 2
+PIECES = OTHERS * SPLIT
 BAND = 32
 EDGE = 8
-VMEM_LIMIT = 67_000_000
+BATCH = 4
+WHOLE_VMEM = 67_000_000
+VMEM_LIMIT = 63_500_000
 F32 = jnp.float32
 HBM = pl.BlockSpec(memory_space=pltpu.HBM)
 SMEM = pl.BlockSpec(memory_space=pltpu.SMEM)
+VMEM = pl.BlockSpec(memory_space=pltpu.VMEM)
 DMA = pltpu.SemaphoreType.DMA
 
 
@@ -56,9 +61,10 @@
 def gather_rows(field, tables, buf, sent, sems):
     tile, count, weight = tables
     row_ids = lax.broadcasted_iota(jnp.int32, (CAP, CZ), 0)
+    size = BLOCKS // SPLIT
     stores = []
-    for j in range(OTHERS):
-        first = other(j) * BLOCKS
+    for piece in range(PIECES):
+        first = other(piece // SPLIT) * BLOCKS + (piece % SPLIT) * size
 
         def peer_rows(b, carry):
             peer = first + b
@@ -72,11 +78,12 @@
                 rows = field[v, pl.ds(spots[0], CAP), :]
                 for e in range(1, CAP):
                     rows = jnp.where(row_ids == e, field[v, pl.ds(spots[e], CAP), :], rows)
-                buf[j * BLOCKS + b, v * CAP : (v + 1) * CAP, :] = rows * scale
+                buf[piece * size + b, v * CAP : (v + 1) * CAP, :] = rows * scale
             return carry
 
-        lax.fori_loop(0, BLOCKS, peer_rows, 0)
-        stores.append(pltpu.make_async_copy(part_of(buf, j), block_of(sent, j), sems.at[j]))
+        lax.fori_loop(0, size, peer_rows, 0, unroll=4)
+        ready = buf.at[pl.ds(piece * size, size)]
+        stores.append(pltpu.make_async_copy(ready, sent.at[pl.ds(first, size)], sems.at[piece]))
         stores[-1].start()
     return stores
 
@@ -95,7 +102,7 @@
             total[v] = both if j == 0 else total[v] + both
 
 
-def add_halos(field, coupling, below, above, volume, scale):
+def settle(field, coupling, rows, total, below, above, volume, scale):
     for side, halo, first in ((1, below, EDGE), (0, above, EDGE + ROWS - CY)):
 
         def band(i, carry):
@@ -111,15 +118,19 @@
 
         lax.fori_loop(0, CY // BAND, band, 0)
 
-
-def patch_rows(field, rows, total, scale):
-    def patch(s, carry):
-        t = rows[0, s] + EDGE
-        for v in range(NVAR):
-            field[v, pl.ds(t, 1), :] += scale * total[v, pl.ds(s, 1), :]
+    def patch(i, carry):
+        slots = [i * BATCH + k for k in range(BATCH)]
+        spots = [rows[0, s] + EDGE for s in slots]
+        sums = []
+        for s, t in zip(slots, spots):
+            for v in range(NVAR):
+                sums.append(field[v, pl.ds(t, 1), :] + (PENALTY * scale) * total[v, pl.ds(s, 1), :])
+        for k, t in enumerate(spots):
+            for v in range(NVAR):
+                field[v, pl.ds(t, 1), :] = sums[k * NVAR + v]
         return carry
 
-    lax.fori_loop(0, SLOTS, patch, 0)
+    lax.fori_loop(0, SLOTS // BATCH, patch, 0)
 
 
 def inner(field, first=0, size=ROWS):
@@ -132,18 +143,17 @@
 
 def pack_kernel(tile, count, weight, field, sent, tile_s, count_s, weight_s, field_v, buf, sems, sent_sems):
     scratch = (tile_s, count_s, weight_s)
-    pairs = list(zip((tile, count, weight), scratch)) + [(field, inner(field_v))]
-    copies = copies_of(pairs, sems)
+    copies = copies_of(list(zip((tile, count, weight), scratch)) + [(field, inner(field_v))], sems)
     start_all(copies)
     wait_all(copies)
     wait_all(gather_rows(field_v, scratch, buf, sent, sent_sems))
 
 
-def arrive(inputs, scratch, sems):
-    coupling, rows, slots, arrived, guess, below, above, volume = inputs
-    coupling_s, rows_s, slots_v, data, total, field, below_v, above_v, volume_v = scratch
+def arrive(inputs, scratch, sems, field, scale):
+    coupling, rows, slots, arrived, below, above, volume = inputs
+    coupling_s, rows_s, slots_v, data, total, below_v, above_v, volume_v = scratch
     loads = [(slots, slots_v)] + [(block_of(arrived, j), part_of(data, j)) for j in range(OTHERS)]
-    others = [(guess, inner(field)), (coupling, coupling_s), (rows, rows_s), (below, below_v), (above, above_v)]
+    others = [(coupling, coupling_s), (rows, rows_s), (below, below_v), (above, above_v)]
     others += [(volume.at[0], volume_v.at[0]), (volume.at[CX - 1], volume_v.at[1])]
     loads = copies_of(loads, sems)
     others = copies_of(others, sems, len(loads))
@@ -151,34 +161,29 @@
     loads[0].wait()
     reduce_rows(slots_v, loads[1:], data, total)
     wait_all(others)
+    settle(field, coupling_s, rows_s, total, below_v, above_v, volume_v, scale)
 
 
 def middle_kernel(*refs):
-    tables, inputs, refs = refs[:3], refs[3:11], refs[11:]
-    sent, mid, low, high, refs = *refs[:4], refs[4:]
-    table_scratch, scratch, (sems, table_sems, sent_sems) = refs[:3], refs[3:12], refs[12:]
-    coupling, rows, _, data, total, field, below, above, volume = scratch
+    tables, inputs, refs = refs[:3], refs[4:11], refs[11:]
+    field, sent, mid, low, high, refs = *refs[:5], refs[5:]
+    table_scratch, scratch, (sems, table_sems, sent_sems) = refs[:3], refs[3:11], refs[11:]
     table_copies = copies_of(list(zip(tables, table_scratch)), table_sems)
     start_all(table_copies)
-    arrive(inputs, scratch, sems)
-    add_halos(field, coupling, below, above, volume, TIME_STEP)
-    patch_rows(field, rows, total, TIME_STEP * PENALTY)
+    arrive(inputs, scratch, sems, field, TIME_STEP)
     stores = copies_of([(inner(field), mid), (inner(field, 0, CY), low), (inner(field, ROWS - CY, CY), high)], sems)
     start_all(stores)
     wait_all(table_copies)
-    wait_all(gather_rows(field, table_scratch, data, sent, sent_sems))
+    wait_all(gather_rows(field, table_scratch, scratch[3], sent, sent_sems))
     wait_all(stores)
 
 
 def finish_kernel(*refs):
-    inputs, end, scratch, sems = refs[:8], refs[8], refs[9:18], refs[18]
-    coupling, rows, _, _, total, field, below, above, volume = scratch
-    arrive(inputs, scratch, sems)
-    add_halos(field, coupling, below, above, volume, 0.5 * TIME_STEP)
-    patch_rows(field, rows, total, 0.5 * TIME_STEP * PENALTY)
-    stores = copies_of([(inner(field), end)], sems)
-    start_all(stores)
-    wait_all(stores)
+    inputs, (field, end), scratch, sems = refs[1:8], refs[8:10], refs[10:18], refs[18]
+    arrive(inputs, scratch, sems, field, 0.5 * TIME_STEP)
+    store = pltpu.make_async_copy(inner(field), end, sems.at[0])
+    store.start()
+    store.wait()
 
 
 def flux_kernel(second, coupling, rows, field, *refs):
@@ -231,7 +236,7 @@
                 value = 0.5 * (base[u, 0, pl.ds(y, BAND), :] + center) + (0.5 * TIME_STEP) * rate
             else:
                 value = center + TIME_STEP * rate
-            out[u, x, pl.ds(y, BAND), :] = value
+            out[u, pl.ds(EDGE + x * CY + y, BAND), :] = value
         return carry
 
     lax.fori_loop(0, CY // BAND, band, 0)
@@ -244,7 +249,7 @@
             t = rows[0, s]
             a, b = t // CY, t % CY
             for v in range(NVAR):
-                out[v, a, pl.ds(b, 1), :] -= scale * ext[v, a + 1, pl.ds(b + 8, 1), :]
+                out[v, pl.ds(t + EDGE, 1), :] -= scale * ext[v, a + 1, pl.ds(b + 8, 1), :]
             return carry
 
         lax.fori_loop(0, SLOTS, patch, 0)
@@ -263,46 +268,52 @@
     pltpu.VMEM((COMPS, BLOCKS * CAP), jnp.int32),
     DATA_V,
     pltpu.VMEM((NVAR, SLOTS, CZ), F32),
-    FIELD_V,
     pltpu.VMEM((NVAR, CY, CZ), F32),
     pltpu.VMEM((NVAR, CY, CZ), F32),
     pltpu.VMEM((2, CY, CZ), F32),
-    DMA((12,)),
+    DMA((10,)),
 ]
 
 
-def call(kernel, name, inputs, out_shape, scratch, moved, flops):
-    single = not isinstance(out_shape, list)
+def call(kernel, name, inputs, out_shape, scratch, moved, flops, limit, held=None):
+    specs = [HBM] * len(inputs)
+    out_specs = [HBM] * len(out_shape)
+    aliases = {}
+    if held is not None:
+        specs[held] = out_specs[0] = VMEM
+        aliases = {held: 0}
     return pl.pallas_call(
         kernel,
-        in_specs=[HBM] * len(inputs),
-        out_specs=HBM if single else [HBM] * len(out_shape),
+        in_specs=specs,
+        out_specs=out_specs,
         out_shape=out_shape,
         scratch_shapes=scratch,
-        compiler_params=pltpu.CompilerParams(vmem_limit_bytes=VMEM_LIMIT),
+        input_output_aliases=aliases,
+        compiler_params=pltpu.CompilerParams(vmem_limit_bytes=limit),
         cost_estimate=pl.CostEstimate(flops=flops, bytes_accessed=moved, transcendentals=0),
         name=name,
     )(*inputs)
 
 
 def pack(tables, field):
+    (sent,) = call(
+        pack_kernel, "pack", [*tables, field], [shape(PEERS, PACK, CZ)],
+        [*TABLES, FIELD_V, DATA_V, DMA((4,)), DMA((PIECES,))], 8 << 20, 10**6, WHOLE_VMEM,
+    )
+    return sent
+
+
+def middle(tables, field, inputs):
     return call(
-        pack_kernel, "pack", [*tables, field], shape(PEERS, PACK, CZ),
-        [*TABLES, FIELD_V, DATA_V, DMA((4,)), DMA((OTHERS,))], 8 << 20, 10**6,
-    )
-
-
-def middle(tables, inputs):
-    plane = shape(NVAR, CY, CZ)
-    return call(
-        middle_kernel, "middle", [*tables, *inputs],
-        [shape(PEERS, PACK, CZ), shape(NVAR, ROWS, CZ), plane, plane],
-        [*TABLES, *ARRIVE, DMA((3,)), DMA((OTHERS,))], 16 << 20, 10**8,
-    )
-
-
-def finish(inputs):
-    return call(finish_kernel, "finish", inputs, shape(NVAR, ROWS, CZ), ARRIVE, 10 << 20, 10**8)
+        middle_kernel, "middle", [*tables, field, *inputs],
+        [FIELD_V, shape(PEERS, PACK, CZ), shape(NVAR, ROWS, CZ), shape(NVAR, CY, CZ), shape(NVAR, CY, CZ)],
+        [*TABLES, *ARRIVE, DMA((3,)), DMA((PIECES,))], 16 << 20, 10**8, VMEM_LIMIT, 3,
+    )[1:]
+
+
+def finish(field, inputs):
+    out_shape = [FIELD_V, shape(NVAR, ROWS, CZ)]
+    return call(finish_kernel, "finish", [field, *inputs], out_shape, ARRIVE, 10 << 20, 10**8, VMEM_LIMIT, 0)[1]
 
 
 def advance(second, coupling, rows, field, streams, volume):
@@ -312,8 +323,8 @@
         in_specs=[SMEM, SMEM, HBM]
         + [pl.BlockSpec((NVAR, 1, CY, CZ), lambda i: (0, i, 0, 0))] * len(streams)
         + [pl.BlockSpec((1, CY, CZ), lambda i: (i, 0, 0))],
-        out_specs=pl.BlockSpec((NVAR, CX, CY, CZ), lambda i: (0, 0, 0, 0)),
-        out_shape=shape(NVAR, CX, CY, CZ),
+        out_specs=VMEM,
+        out_shape=FIELD_V,
         scratch_shapes=[pltpu.VMEM((NVAR, CX + 2, CY + 16, CZ), F32), DMA(())],
         compiler_params=pltpu.CompilerParams(dimension_semantics=("arbitrary",), vmem_limit_bytes=VMEM_LIMIT),
         cost_estimate=pl.CostEstimate(flops=60 * 10**6, bytes_accessed=40 << 20, transcendentals=0),
@@ -344,12 +355,12 @@
 
     arrived = exchange(pack(tables, start.reshape(tiled)))
     below, above = halos(start[:, 0], start[:, -1])
-    mid = advance(False, matrices, fringe_row, start, [source], volume).reshape(tiled)
-    sent, mid, low, high = middle(tables, [matrices, fringe_row, slots, arrived, mid, below, above, volume])
+    field = advance(False, matrices, fringe_row, start, [source], volume)
+    sent, mid, low, high = middle(tables, field, [matrices, fringe_row, slots, arrived, below, above, volume])
     arrived = exchange(sent)
     below, above = halos(low, high)
-    end = advance(True, matrices, fringe_row, mid.reshape(NVAR, CX, CY, CZ), [start, source], volume)
-    end = finish([matrices, fringe_row, slots, arrived, end.reshape(tiled), below, above, volume])
+    field = advance(True, matrices, fringe_row, mid.reshape(NVAR, CX, CY, CZ), [start, source], volume)
+    end = finish(field, [matrices, fringe_row, slots, arrived, below, above, volume])
     return end.reshape(1, NVAR, CX, CY, CZ)
 
 

time: 122 us -> 118 us (0.967)
  Pallas kernels: 51.2 us -> 44.5 us
  waiting for transfers between devices: 34.8 us -> 38.2 us
    pallas_call x2, Pallas kernels: 33.5 us -> 30.1 us  [advance(): pl.pallas_call(functools.partial(flux_kernel, second), grid=(CX,), in_spe...]
    pallas_call x3, Pallas kernels: 17.7 us -> 14.4 us  [call(): pl.pallas_call(kernel, in_specs=specs, out_specs=out_specs, out_shape=out...]
    ppermute x2, waiting for transfers between devices: 16.2 us -> 18 us  [halos(): above = lax.ppermute(low, 'blk', [(i + 1, i) for i in range(count - 1)])]
    ppermute x2, waiting for transfers between devices: 16 us -> 17.7 us  [halos(): below = lax.ppermute(high, 'blk', [(i, i + 1) for i in range(count - 1)])]
  transfers between devices with their start and end apart: 6 -> 6, of which waited for: 5 -> 5; matrix products, arithmetic and copies ran while one was open for 3% -> 3% of each run, Pallas kernels for 28% -> 26%
where the time goes in v4:
time: 118 us
  Pallas kernels  44.5 us (38%)
  waiting for transfers between devices  38.2 us (32%)
  starting transfers between devices  31.4 us (27%)
  local copies, waits for them, and re-layouts  3.53 us (3%)
    pallas_call x2, Pallas kernels, advance(): pl.pallas_call(functools.partial(flux_kernel, second), grid=(CX,), in_spe...  30.1 us
    all_to_all x2, starting transfers between devices, exchange(): lax.all_to_all(sent, ('comp', 'blk'), split_axis=0, concat_axis=0, tiled=...  20.2 us
    ppermute x2, waiting for transfers between devices, halos(): above = lax.ppermute(low, 'blk', [(i + 1, i) for i in range(count - 1)])  18 us
    ppermute x2, waiting for transfers between devices, halos(): below = lax.ppermute(high, 'blk', [(i, i + 1) for i in range(count - 1)])  17.7 us
    pallas_call x3, Pallas kernels, call(): pl.pallas_call(kernel, in_specs=specs, out_specs=out_specs, out_shape=out...  14.4 us
    ppermute x2, starting transfers between devices, halos(): below = lax.ppermute(high, 'blk', [(i, i + 1) for i in range(count - 1)])  6.2 us
    ppermute x2, starting transfers between devices, halos(): above = lax.ppermute(low, 'blk', [(i + 1, i) for i in range(count - 1)])  4.95 us
    all_to_all x2, waiting for transfers between devices, exchange(): lax.all_to_all(sent, ('comp', 'blk'), split_axis=0, concat_axis=0, tiled=...  2.57 us
  transfers between devices with their start and end apart: 6, of which 5 were waited for; matrix products, arithmetic and copies ran while one was open for 3% of the time, Pallas kernels for 26%

profile of v4, /device:TPU:1, one launch (start us, length us, event | category | flops | bytes accessed | tf_op | source)
XLA Modules:
  0.0 117.8 jit_solution(16416123096679097082)
XLA Ops:
  0.0 4.3 %pack.1 = f32[128,48,128]{2,1,0:T(8,128)} custom-call(s32[8,128]{1,0:T(8,128)} %bitcast.27, s32[1,128]{1,0:T(1,128)} %refs_1_.1, f32[8,128]{1,0:T(8,128)} %bitcast.29, f32[6,1024,128]{2,1,0:T(8,128)} %bitcast.16), custom_call_target="tpu_custom_call" | custom-call | flops 1000000 | bytes 8388608 | tf_op jit(solution)/shard_map/pack/pallas_call | solution.py:285
  4.3 0.0 copy-start
  4.3 0.0 copy-start.1
  4.3 11.9 %all-to-all-start = ((f32[128,48,128]{2,1,0:T(8,128)}), f32[128,48,128]{2,1,0:T(8,128)}, u32[]{:S(2)}, u32[]{:S(2)}) async-start(f32[128,48,128]{2,1,0:T(8,128)} %pack.1), calls=%async_computation | async-start | bytes 6291456 | tf_op jit(solution)/shard_map/all_to_all | solution.py:336
  16.2 2.1 %slice_bitcast_fusion = (f32[6,128,128]{2,1,0:T(8,128)}, f32[6,128,128]{2,1,0:T(8,128)}) fusion(f32[6,8,128,128]{3,2,1,0:T(8,128)} %bitcast.17), kind=kLoop, calls=%fused_computation | loop fusion | bytes 1572864 | tf_op jit(solution)/shard_map/squeeze | solution.py:357
  18.3 3.0 %collective-permute-start.1 = (f32[6,128,128]{2,1,0:T(8,128)}, f32[6,128,128]{2,1,0:T(8,128)}, u32[]{:S(2)}, u32[]{:S(2)}) collective-permute-start(f32[6,128,128]{2,1,0:T(8,128)} %get-tuple-element.15), channel_id=1, source_target_pairs={{1,0},{2,1},{3,2},{4,3},{5,4},{6,5},{7,6},{8,7},{9,8},{10,9},{11,1... | collective-permute-start | bytes 1179656 | tf_op jit(solution)/shard_map/ppermute | solution.py:342
  21.3 2.5 %collective-permute-start = (f32[6,128,128]{2,1,0:T(8,128)}, f32[6,128,128]{2,1,0:T(8,128)}, u32[]{:S(2)}, u32[]{:S(2)}) collective-permute-start(f32[6,128,128]{2,1,0:T(8,128)} %get-tuple-element.16), channel_id=1, source_target_pairs={{0,1},{1,2},{2,3},{3,4},{4,5},{5,6},{6,7},{7,8},{8,9},{9,10},{10,1... | collective-permute-start | bytes 1179656 | tf_op jit(solution)/shard_map/ppermute | solution.py:341
  23.8 0.0 copy-done
  23.9 0.1 reduce
  23.9 0.7 reshape_squeeze.9.coupling.refs_4_.refs_1_
  24.6 0.0 copy-done.1
  24.6 0.1 copy.13
  24.7 0.7 reshape_squeeze.10.refs_6_.refs_3_
  25.4 14.8 %advance_mid.1.refs_3_ = f32[6,1040,128]{2,1,0:T(8,128)S(1)} custom-call(f32[6,36]{1,0:T(8,128)} %reshape_squeeze.9.coupling.refs_4_.refs_1_, s32[1,64]{1,0:T(1,128)} %refs_2_.1, f32[6,8,128,128]{3,2,1,0:T(8,128)} %bitcast.18, f32[6,8,128,128]{3,2,1,0:T(8,128)} %bitcast.20, f32[8,128,128]{2,1,0:T(8,128)} %bitcast.22), custom_call_target="tpu_custom_call" | custom-call | flops 60000000 | bytes 41943040 | tf_op jit(solution)/shard_map/advance_mid/pallas_call | solution.py:320
  40.2 16.3 %collective-permute-done.1.refs_9_ = f32[6,128,128]{2,1,0:T(8,128)} collective-permute-done((f32[6,128,128]{2,1,0:T(8,128)}, f32[6,128,128]{2,1,0:T(8,128)}, u32[]{:S(2)}, u32[]{:S(2)}) %collective-permute-start.1) | collective-permute-done | bytes 393248 | tf_op jit(solution)/shard_map/ppermute | solution.py:342
  56.4 0.0 collective-permute-done.refs_8_
  56.4 1.3 %all-to-all-done.refs_7_ = f32[128,48,128]{2,1,0:T(8,128)} async-done(((f32[128,48,128]{2,1,0:T(8,128)}), f32[128,48,128]{2,1,0:T(8,128)}, u32[]{:S(2)}, u32[]{:S(2)}) %all-to-all-start) | async-done | bytes 3145760 | tf_op jit(solution)/shard_map/all_to_all | solution.py:336
  57.7 5.6 %middle.1 = (f32[6,1040,128]{2,1,0:T(8,128)S(1)}, f32[128,48,128]{2,1,0:T(8,128)}, f32[6,1024,128]{2,1,0:T(8,128)}, f32[6,128,128]{2,1,0:T(8,128)}, f32[6,128,128]{2,1,0:T(8,128)}) custom-call(s32[8,128]{1,0:T(8,128)} %bitcast.28, s32[1,128]{1,0:T(1,128)} %refs_1_.1, f32[8,128]{1,0:T(8,128)} %bitcast.30, ...), custom_call_target="tpu_custom_call", output_to_operand_aliasing={{0}: (3, {})} | custom-call | flops 100000000 | bytes 16777216 | tf_op jit(solution)/shard_map/middle/pallas_call | solution.py:285
  63.3 8.3 %all-to-all-start.1 = ((f32[128,48,128]{2,1,0:T(8,128)}), f32[128,48,128]{2,1,0:T(8,128)}, u32[]{:S(2)}, u32[]{:S(2)}) async-start(f32[128,48,128]{2,1,0:T(8,128)} %get-tuple-element.11), calls=%async_computation.1 | async-start | bytes 6291456 | tf_op jit(solution)/shard_map/all_to_all | solution.py:336
  71.7 3.7 %collective-permute-start.2 = (f32[6,128,128]{2,1,0:T(8,128)}, f32[6,128,128]{2,1,0:T(8,128)}, u32[]{:S(2)}, u32[]{:S(2)}) collective-permute-start(f32[6,128,128]{2,1,0:T(8,128)} %get-tuple-element.12), channel_id=1, source_target_pairs={{0,1},{1,2},{2,3},{3,4},{4,5},{5,6},{6,7},{7,8},{8,9},{9,10},{10,1... | collective-permute-start | bytes 1179656 | tf_op jit(solution)/shard_map/ppermute | solution.py:341
  75.4 1.9 %collective-permute-start.3 = (f32[6,128,128]{2,1,0:T(8,128)}, f32[6,128,128]{2,1,0:T(8,128)}, u32[]{:S(2)}, u32[]{:S(2)}) collective-permute-start(f32[6,128,128]{2,1,0:T(8,128)} %get-tuple-element.13), channel_id=1, source_target_pairs={{1,0},{2,1},{3,2},{4,3},{5,4},{6,5},{7,6},{8,7},{9,8},{10,9},{11,1... | collective-permute-start | bytes 1179656 | tf_op jit(solution)/shard_map/ppermute | solution.py:342
  77.3 15.3 %advance_end.1.refs_0_ = f32[6,1040,128]{2,1,0:T(8,128)S(1)} custom-call(f32[6,36]{1,0:T(8,128)} %reshape_squeeze.9.coupling.refs_4_.refs_1_, s32[1,64]{1,0:T(1,128)} %refs_2_.1, f32[6,8,128,128]{3,2,1,0:T(8,128)} %bitcast.26, f32[6,8,128,128]{3,2,1,0:T(8,128)} %bitcast.19, f32[6,8,128,128]{3,2,1,0:T(8,128)} %bitcast.21, f32[8,128,128]{2,1,0:T(8,128)} %bitcast.24), custom_call_target="tpu_custom_call" | custom-call | flops 60000000 | bytes 41943040 | tf_op jit(solution)/shard_map/advance_end/pallas_call | solution.py:320
  92.5 17.7 %collective-permute-done.2.refs_5_ = f32[6,128,128]{2,1,0:T(8,128)} collective-permute-done((f32[6,128,128]{2,1,0:T(8,128)}, f32[6,128,128]{2,1,0:T(8,128)}, u32[]{:S(2)}, u32[]{:S(2)}) %collective-permute-start.2) | collective-permute-done | bytes 393248 | tf_op jit(solution)/shard_map/ppermute | solution.py:341
  110.2 1.7 %collective-permute-done.3.refs_6_ = f32[6,128,128]{2,1,0:T(8,128)} collective-permute-done((f32[6,128,128]{2,1,0:T(8,128)}, f32[6,128,128]{2,1,0:T(8,128)}, u32[]{:S(2)}, u32[]{:S(2)}) %collective-permute-start.3) | collective-permute-done | bytes 393248 | tf_op jit(solution)/shard_map/ppermute | solution.py:342
  111.9 1.3 %all-to-all-done.1.refs_4_ = f32[128,48,128]{2,1,0:T(8,128)} async-done(((f32[128,48,128]{2,1,0:T(8,128)}), f32[128,48,128]{2,1,0:T(8,128)}, u32[]{:S(2)}, u32[]{:S(2)}) %all-to-all-start.1) | async-done | bytes 3145760 | tf_op jit(solution)/shard_map/all_to_all | solution.py:336
  113.2 4.5 %finish.1 = (f32[6,1040,128]{2,1,0:T(8,128)S(1)}, f32[6,1024,128]{2,1,0:T(8,128)}) custom-call(f32[6,1040,128]{2,1,0:T(8,128)S(1)} %advance_end.1.refs_0_, f32[6,36]{1,0:T(8,128)} %reshape_squeeze.9.coupling.refs_4_.refs_1_, s32[1,64]{1,0:T(1,128)} %refs_2_.1, s32[4,256]{1,0:T(4,128)} %reshape_squeeze.10.refs_6_.refs_3_, ...), custom_call_target="tpu_custom_call", output_to_operand_aliasing={{0}: (0, {})} | custom-call | flops 100000000 | bytes 10485760 | tf_op jit(solution)/shard_map/finish/pallas_call | solution.py:285
Async XLA Ops:
  4.3 19.6 %copy-start = (f32[1,6,6,6]{3,0,2,1:T(1,128)S(1)}, f32[1,6,6,6]{3,0,2,1:T(1,128)}, u32[]{:S(2)}) copy-start(f32[1,6,6,6]{3,0,2,1:T(1,128)} %param.12) | copy-start | bytes 2596
  4.3 20.3 %copy-start.1 = (s32[1,128,8]{1,2,0:T(8,128)S(1)}, s32[1,128,8]{1,2,0:T(8,128)}, u32[]{:S(2)}) copy-start(s32[1,128,8]{1,2,0:T(8,128)} %param.16) | copy-start | bytes 12292
  4.3 53.4 %all-to-all-start = ((f32[128,48,128]{2,1,0:T(8,128)}), f32[128,48,128]{2,1,0:T(8,128)}, u32[]{:S(2)}, u32[]{:S(2)}) async-start(f32[128,48,128]{2,1,0:T(8,128)} %pack.1), calls=%async_computation | async-start | bytes 6291456 | tf_op jit(solution)/shard_map/all_to_all | solution.py:336
  18.3 38.2 %collective-permute-start.1 = (f32[6,128,128]{2,1,0:T(8,128)}, f32[6,128,128]{2,1,0:T(8,128)}, u32[]{:S(2)}, u32[]{:S(2)}) collective-permute-start(f32[6,128,128]{2,1,0:T(8,128)} %get-tuple-element.15), channel_id=1, source_target_pairs={{1,0},{2,1},{3,2},{4,3},{5,4},{6,5},{7,6},{8,7},{9,8},{10,9},{11,1... | collective-permute-start | bytes 1179656 | tf_op jit(solution)/shard_map/ppermute | solution.py:342
  21.3 35.2 %collective-permute-start = (f32[6,128,128]{2,1,0:T(8,128)}, f32[6,128,128]{2,1,0:T(8,128)}, u32[]{:S(2)}, u32[]{:S(2)}) collective-permute-start(f32[6,128,128]{2,1,0:T(8,128)} %get-tuple-element.16), channel_id=1, source_target_pairs={{0,1},{1,2},{2,3},{3,4},{4,5},{5,6},{6,7},{7,8},{8,9},{9,10},{10,1... | collective-permute-start | bytes 1179656 | tf_op jit(solution)/shard_map/ppermute | solution.py:341
  63.3 49.9 %all-to-all-start.1 = ((f32[128,48,128]{2,1,0:T(8,128)}), f32[128,48,128]{2,1,0:T(8,128)}, u32[]{:S(2)}, u32[]{:S(2)}) async-start(f32[128,48,128]{2,1,0:T(8,128)} %get-tuple-element.11), calls=%async_computation.1 | async-start | bytes 6291456 | tf_op jit(solution)/shard_map/all_to_all | solution.py:336
  71.7 38.5 %collective-permute-start.2 = (f32[6,128,128]{2,1,0:T(8,128)}, f32[6,128,128]{2,1,0:T(8,128)}, u32[]{:S(2)}, u32[]{:S(2)}) collective-permute-start(f32[6,128,128]{2,1,0:T(8,128)} %get-tuple-element.12), channel_id=1, source_target_pairs={{0,1},{1,2},{2,3},{3,4},{4,5},{5,6},{6,7},{7,8},{8,9},{9,10},{10,1... | collective-permute-start | bytes 1179656 | tf_op jit(solution)/shard_map/ppermute | solution.py:341
  75.4 36.6 %collective-permute-start.3 = (f32[6,128,128]{2,1,0:T(8,128)}, f32[6,128,128]{2,1,0:T(8,128)}, u32[]{:S(2)}, u32[]{:S(2)}) collective-permute-start(f32[6,128,128]{2,1,0:T(8,128)} %get-tuple-element.13), channel_id=1, source_target_pairs={{1,0},{2,1},{3,2},{4,3},{5,4},{6,5},{7,6},{8,7},{9,8},{10,9},{11,1... | collective-permute-start | bytes 1179656 | tf_op jit(solution)/shard_map/ppermute | solution.py:342

commit v5 on v4

--- a/solution.py
+++ b/solution.py
@@ -18,11 +18,12 @@
 PEERS = COMPS * BLOCKS
 OTHERS = COMPS - 1
 PACK = NVAR * CAP
-SPLIT = 2
+SPLIT = 4
 PIECES = OTHERS * SPLIT
 BAND = 32
 EDGE = 8
 BATCH = 4
+HALF = 3
 WHOLE_VMEM = 67_000_000
 VMEM_LIMIT = 63_500_000
 F32 = jnp.float32
@@ -102,7 +103,7 @@
             total[v] = both if j == 0 else total[v] + both
 
 
-def settle(field, coupling, rows, total, below, above, volume, scale):
+def add_halos(field, coupling, below, above, volume, scale):
     for side, halo, first in ((1, below, EDGE), (0, above, EDGE + ROWS - CY)):
 
         def band(i, carry):
@@ -118,16 +119,18 @@
 
         lax.fori_loop(0, CY // BAND, band, 0)
 
+
+def patch_rows(field, rows, total, scale, variables):
     def patch(i, carry):
         slots = [i * BATCH + k for k in range(BATCH)]
         spots = [rows[0, s] + EDGE for s in slots]
         sums = []
         for s, t in zip(slots, spots):
-            for v in range(NVAR):
+            for v in variables:
                 sums.append(field[v, pl.ds(t, 1), :] + (PENALTY * scale) * total[v, pl.ds(s, 1), :])
         for k, t in enumerate(spots):
-            for v in range(NVAR):
-                field[v, pl.ds(t, 1), :] = sums[k * NVAR + v]
+            for n, v in enumerate(variables):
+                field[v, pl.ds(t, 1), :] = sums[k * len(variables) + n]
         return carry
 
     lax.fori_loop(0, SLOTS // BATCH, patch, 0)
@@ -137,13 +140,18 @@
     return field.at[:, pl.ds(EDGE + first, size), :]
 
 
+def line(field, v):
+    return field.at[v, pl.ds(EDGE, ROWS), :]
+
+
 def copies_of(pairs, sems, first=0):
     return [pltpu.make_async_copy(a, b, sems.at[first + i]) for i, (a, b) in enumerate(pairs)]
 
 
 def pack_kernel(tile, count, weight, field, sent, tile_s, count_s, weight_s, field_v, buf, sems, sent_sems):
     scratch = (tile_s, count_s, weight_s)
-    copies = copies_of(list(zip((tile, count, weight), scratch)) + [(field, inner(field_v))], sems)
+    pairs = list(zip((tile, count, weight), scratch)) + [(field.at[v], line(field_v, v)) for v in range(NVAR)]
+    copies = copies_of(pairs, sems)
     start_all(copies)
     wait_all(copies)
     wait_all(gather_rows(field_v, scratch, buf, sent, sent_sems))
@@ -152,58 +160,69 @@
 def arrive(inputs, scratch, sems, field, scale):
     coupling, rows, slots, arrived, below, above, volume = inputs
     coupling_s, rows_s, slots_v, data, total, below_v, above_v, volume_v = scratch
-    loads = [(slots, slots_v)] + [(block_of(arrived, j), part_of(data, j)) for j in range(OTHERS)]
-    others = [(coupling, coupling_s), (rows, rows_s), (below, below_v), (above, above_v)]
-    others += [(volume.at[0], volume_v.at[0]), (volume.at[CX - 1], volume_v.at[1])]
-    loads = copies_of(loads, sems)
-    others = copies_of(others, sems, len(loads))
-    start_all(loads + others)
-    loads[0].wait()
-    reduce_rows(slots_v, loads[1:], data, total)
-    wait_all(others)
-    settle(field, coupling_s, rows_s, total, below_v, above_v, volume_v, scale)
+    first = [(coupling, coupling_s), (below, below_v), (above, above_v)]
+    first += [(volume.at[0], volume_v.at[0]), (volume.at[CX - 1], volume_v.at[1])]
+    first += [(slots, slots_v), (rows, rows_s)]
+    loads = [(block_of(arrived, j), part_of(data, j)) for j in range(OTHERS)]
+    first = copies_of(first, sems)
+    loads = copies_of(loads, sems, len(first))
+    start_all(first + loads)
+    wait_all(first)
+    add_halos(field, coupling_s, below_v, above_v, volume_v, scale)
+    reduce_rows(slots_v, loads, data, total)
 
 
 def middle_kernel(*refs):
     tables, inputs, refs = refs[:3], refs[4:11], refs[11:]
-    field, sent, mid, low, high, refs = *refs[:5], refs[5:]
+    field, sent, low, high, refs = *refs[:4], refs[4:]
     table_scratch, scratch, (sems, table_sems, sent_sems) = refs[:3], refs[3:11], refs[11:]
     table_copies = copies_of(list(zip(tables, table_scratch)), table_sems)
     start_all(table_copies)
     arrive(inputs, scratch, sems, field, TIME_STEP)
-    stores = copies_of([(inner(field), mid), (inner(field, 0, CY), low), (inner(field, ROWS - CY, CY), high)], sems)
+    patch_rows(field, scratch[1], scratch[4], TIME_STEP, range(NVAR))
+    stores = copies_of([(inner(field, 0, CY), low), (inner(field, ROWS - CY, CY), high)], sems)
     start_all(stores)
     wait_all(table_copies)
     wait_all(gather_rows(field, table_scratch, scratch[3], sent, sent_sems))
     wait_all(stores)
 
 
+def spill_kernel(field, held, mid, sem):
+    store = pltpu.make_async_copy(inner(held), mid, sem)
+    store.start()
+    store.wait()
+
+
 def finish_kernel(*refs):
     inputs, (field, end), scratch, sems = refs[1:8], refs[8:10], refs[10:18], refs[18]
     arrive(inputs, scratch, sems, field, 0.5 * TIME_STEP)
-    store = pltpu.make_async_copy(inner(field), end, sems.at[0])
-    store.start()
-    store.wait()
+    stores = copies_of([(line(field, v), end.at[v]) for v in range(NVAR)], sems)
+    for first in range(0, NVAR, HALF):
+        half = range(first, first + HALF)
+        patch_rows(field, scratch[1], scratch[4], 0.5 * TIME_STEP, half)
+        start_all([stores[v] for v in half])
+    wait_all(stores)
 
 
 def flux_kernel(second, coupling, rows, field, *refs):
     if second:
-        base, source, volume, out, ext, sem = refs
+        base, source, volume, out, ext, sems = refs
     else:
-        source, volume, out, ext, sem = refs
+        source, volume, out, ext, sems = refs
     x = pl.program_id(0)
 
     @pl.when(x == 0)
     def _():
-        copy = pltpu.make_async_copy(field, ext.at[:, pl.ds(1, CX), pl.ds(8, CY), :], sem)
-        copy.start()
+        planes = [(field.at[:, i], ext.at[:, i + 1, pl.ds(8, CY), :]) for i in range(CX)]
+        copies = copies_of(planes, sems)
+        start_all(copies)
         edge = jnp.zeros((NVAR, CX + 2, 8, CZ), F32)
         ext[:, :, 0:8, :] = edge
         ext[:, :, 8 + CY : 16 + CY, :] = edge
         plane = jnp.zeros((NVAR, CY, CZ), F32)
         ext[:, 0, 8 : 8 + CY, :] = plane
         ext[:, CX + 1, 8 : 8 + CY, :] = plane
-        copy.wait()
+        wait_all(copies)
 
     lane = lax.broadcasted_iota(jnp.int32, (BAND, CZ), 1)
 
@@ -298,7 +317,7 @@
 def pack(tables, field):
     (sent,) = call(
         pack_kernel, "pack", [*tables, field], [shape(PEERS, PACK, CZ)],
-        [*TABLES, FIELD_V, DATA_V, DMA((4,)), DMA((PIECES,))], 8 << 20, 10**6, WHOLE_VMEM,
+        [*TABLES, FIELD_V, DATA_V, DMA((3 + NVAR,)), DMA((PIECES,))], 8 << 20, 10**6, WHOLE_VMEM,
     )
     return sent
 
@@ -306,9 +325,14 @@
 def middle(tables, field, inputs):
     return call(
         middle_kernel, "middle", [*tables, field, *inputs],
-        [FIELD_V, shape(PEERS, PACK, CZ), shape(NVAR, ROWS, CZ), shape(NVAR, CY, CZ), shape(NVAR, CY, CZ)],
+        [FIELD_V, shape(PEERS, PACK, CZ), shape(NVAR, CY, CZ), shape(NVAR, CY, CZ)],
         [*TABLES, *ARRIVE, DMA((3,)), DMA((PIECES,))], 16 << 20, 10**8, VMEM_LIMIT, 3,
-    )[1:]
+    )
+
+
+def spill(field):
+    out_shape = [FIELD_V, shape(NVAR, ROWS, CZ)]
+    return call(spill_kernel, "spill", [field], out_shape, [DMA(())], 3 << 20, 10**6, VMEM_LIMIT, 0)[1]
 
 
 def finish(field, inputs):
@@ -325,7 +349,7 @@
         + [pl.BlockSpec((1, CY, CZ), lambda i: (i, 0, 0))],
         out_specs=VMEM,
         out_shape=FIELD_V,
-        scratch_shapes=[pltpu.VMEM((NVAR, CX + 2, CY + 16, CZ), F32), DMA(())],
+        scratch_shapes=[pltpu.VMEM((NVAR, CX + 2, CY + 16, CZ), F32), DMA((CX,))],
         compiler_params=pltpu.CompilerParams(dimension_semantics=("arbitrary",), vmem_limit_bytes=VMEM_LIMIT),
         cost_estimate=pl.CostEstimate(flops=60 * 10**6, bytes_accessed=40 << 20, transcendentals=0),
         name="advance_end" if second else "advance_mid",
@@ -356,8 +380,9 @@
     arrived = exchange(pack(tables, start.reshape(tiled)))
     below, above = halos(start[:, 0], start[:, -1])
     field = advance(False, matrices, fringe_row, start, [source], volume)
-    sent, mid, low, high = middle(tables, field, [matrices, fringe_row, slots, arrived, below, above, volume])
+    field, sent, low, high = middle(tables, field, [matrices, fringe_row, slots, arrived, below, above, volume])
     arrived = exchange(sent)
+    mid = spill(field)
     below, above = halos(low, high)
     field = advance(True, matrices, fringe_row, mid.reshape(NVAR, CX, CY, CZ), [start, source], volume)
     end = finish(field, [matrices, fringe_row, slots, arrived, below, above, volume])

time: 118 us -> 118 us (level)
  waiting for transfers between devices: 38.2 us -> 36.5 us
  Pallas kernels: 44.5 us -> 45.7 us
    ppermute x2, waiting for transfers between devices: 17.7 us -> 16 us  [halos(): below = lax.ppermute(high, 'blk', [(i, i + 1) for i in range(count - 1)])]
    pallas_call x3 -> x4, Pallas kernels: 14.4 us -> 15.6 us  [call(): pl.pallas_call(kernel, in_specs=specs, out_specs=out_specs, out_shape=out...]
  transfers between devices with their start and end apart: 6 -> 6, of which waited for: 5 -> 5; matrix products, arithmetic and copies ran while one was open for 3% -> 3% of each run, Pallas kernels for 26% -> 27%
where the time goes in v5:
time: 118 us; the launch traced here: 117 us
  Pallas kernels  45.7 us (39%)
  waiting for transfers between devices  36.5 us (31%)
  starting transfers between devices  31.4 us (27%)
  local copies, waits for them, and re-layouts  3.53 us (3%)
    pallas_call x2, Pallas kernels, advance(): pl.pallas_call(functools.partial(flux_kernel, second), grid=(CX,), in_spe...  30.1 us
    all_to_all x2, starting transfers between devices, exchange(): lax.all_to_all(sent, ('comp', 'blk'), split_axis=0, concat_axis=0, tiled=...  20.3 us
    ppermute x2, waiting for transfers between devices, halos(): above = lax.ppermute(low, 'blk', [(i + 1, i) for i in range(count - 1)])  18 us
    ppermute x2, waiting for transfers between devices, halos(): below = lax.ppermute(high, 'blk', [(i, i + 1) for i in range(count - 1)])  16 us
    pallas_call x4, Pallas kernels, call(): pl.pallas_call(kernel, in_specs=specs, out_specs=out_specs, out_shape=out...  15.6 us
    ppermute x2, starting transfers between devices, halos(): below = lax.ppermute(high, 'blk', [(i, i + 1) for i in range(count - 1)])  6.2 us
    ppermute x2, starting transfers between devices, halos(): above = lax.ppermute(low, 'blk', [(i + 1, i) for i in range(count - 1)])  4.95 us
    all_to_all x2, waiting for transfers between devices, exchange(): lax.all_to_all(sent, ('comp', 'blk'), split_axis=0, concat_axis=0, tiled=...  2.57 us
  transfers between devices with their start and end apart: 6, of which 5 were waited for; matrix products, arithmetic and copies ran while one was open for 3% of the time, Pallas kernels for 27%

profile of v5, /device:TPU:1, one launch (start us, length us, event | category | flops | bytes accessed | tf_op | source)
XLA Modules:
  0.0 117.3 jit_solution(17237167114476833294)
XLA Ops:
  0.0 4.3 %pack.1 = f32[128,48,128]{2,1,0:T(8,128)} custom-call(s32[8,128]{1,0:T(8,128)} %bitcast.27, s32[1,128]{1,0:T(1,128)} %refs_1_.1, f32[8,128]{1,0:T(8,128)} %bitcast.29, f32[6,1024,128]{2,1,0:T(8,128)} %bitcast.16), custom_call_target="tpu_custom_call" | custom-call | flops 1000000 | bytes 8388608 | tf_op jit(solution)/shard_map/pack/pallas_call | solution.py:304
  4.3 0.0 copy-start
  4.3 0.0 copy-start.1
  4.3 11.9 %all-to-all-start = ((f32[128,48,128]{2,1,0:T(8,128)}), f32[128,48,128]{2,1,0:T(8,128)}, u32[]{:S(2)}, u32[]{:S(2)}) async-start(f32[128,48,128]{2,1,0:T(8,128)} %pack.1), calls=%async_computation | async-start | bytes 6291456 | tf_op jit(solution)/shard_map/all_to_all | solution.py:360
  16.2 2.1 %slice_bitcast_fusion = (f32[6,128,128]{2,1,0:T(8,128)}, f32[6,128,128]{2,1,0:T(8,128)}) fusion(f32[6,8,128,128]{3,2,1,0:T(8,128)} %bitcast.17), kind=kLoop, calls=%fused_computation | loop fusion | bytes 1572864 | tf_op jit(solution)/shard_map/squeeze | solution.py:381
  18.3 3.0 %collective-permute-start.1 = (f32[6,128,128]{2,1,0:T(8,128)}, f32[6,128,128]{2,1,0:T(8,128)}, u32[]{:S(2)}, u32[]{:S(2)}) collective-permute-start(f32[6,128,128]{2,1,0:T(8,128)} %get-tuple-element.17), channel_id=1, source_target_pairs={{1,0},{2,1},{3,2},{4,3},{5,4},{6,5},{7,6},{8,7},{9,8},{10,9},{11,1... | collective-permute-start | bytes 1179656 | tf_op jit(solution)/shard_map/ppermute | solution.py:366
  21.3 2.5 %collective-permute-start = (f32[6,128,128]{2,1,0:T(8,128)}, f32[6,128,128]{2,1,0:T(8,128)}, u32[]{:S(2)}, u32[]{:S(2)}) collective-permute-start(f32[6,128,128]{2,1,0:T(8,128)} %get-tuple-element.18), channel_id=1, source_target_pairs={{0,1},{1,2},{2,3},{3,4},{4,5},{5,6},{6,7},{7,8},{8,9},{9,10},{10,1... | collective-permute-start | bytes 1179656 | tf_op jit(solution)/shard_map/ppermute | solution.py:365
  23.9 0.0 copy-done
  23.9 0.1 reduce
  23.9 0.7 reshape_squeeze.9.coupling.refs_4_.refs_1_
  24.6 0.0 copy-done.1
  24.6 0.1 copy.14
  24.7 0.7 reshape_squeeze.10.refs_6_.refs_3_
  25.4 14.8 %advance_mid.1.refs_3_ = f32[6,1040,128]{2,1,0:T(8,128)S(1)} custom-call(f32[6,36]{1,0:T(8,128)} %reshape_squeeze.9.coupling.refs_4_.refs_1_, s32[1,64]{1,0:T(1,128)} %refs_2_.1, f32[6,8,128,128]{3,2,1,0:T(8,128)} %bitcast.18, f32[6,8,128,128]{3,2,1,0:T(8,128)} %bitcast.20, f32[8,128,128]{2,1,0:T(8,128)} %bitcast.22), custom_call_target="tpu_custom_call" | custom-call | flops 60000000 | bytes 41943040 | tf_op jit(solution)/shard_map/advance_mid/pallas_call | solution.py:344
  40.2 16.3 %collective-permute-done.1.refs_9_ = f32[6,128,128]{2,1,0:T(8,128)} collective-permute-done((f32[6,128,128]{2,1,0:T(8,128)}, f32[6,128,128]{2,1,0:T(8,128)}, u32[]{:S(2)}, u32[]{:S(2)}) %collective-permute-start.1) | collective-permute-done | bytes 393248 | tf_op jit(solution)/shard_map/ppermute | solution.py:366
  56.5 0.0 collective-permute-done.refs_8_
  56.5 1.3 %all-to-all-done.refs_7_ = f32[128,48,128]{2,1,0:T(8,128)} async-done(((f32[128,48,128]{2,1,0:T(8,128)}), f32[128,48,128]{2,1,0:T(8,128)}, u32[]{:S(2)}, u32[]{:S(2)}) %all-to-all-start) | async-done | bytes 3145760 | tf_op jit(solution)/shard_map/all_to_all | solution.py:360
  57.8 5.3 %middle.1 = (f32[6,1040,128]{2,1,0:T(8,128)S(1)}, f32[128,48,128]{2,1,0:T(8,128)}, f32[6,128,128]{2,1,0:T(8,128)}, f32[6,128,128]{2,1,0:T(8,128)}) custom-call(s32[8,128]{1,0:T(8,128)} %bitcast.28, s32[1,128]{1,0:T(1,128)} %refs_1_.1, f32[8,128]{1,0:T(8,128)} %bitcast.30, f32[6,1040,128]{2,1,0:T(8,128)S(1)} %advance_mid.1.refs_3_, ...), custom_call_target="tpu_custom_call", output_to_operand_aliasing={{0}: (3, {})} | custom-call | flops 100000000 | bytes 16777216 | tf_op jit(solution)/shard_map/middle/pallas_call | solution.py:304
  63.1 8.3 %all-to-all-start.1 = ((f32[128,48,128]{2,1,0:T(8,128)}), f32[128,48,128]{2,1,0:T(8,128)}, u32[]{:S(2)}, u32[]{:S(2)}) async-start(f32[128,48,128]{2,1,0:T(8,128)} %get-tuple-element.13), calls=%async_computation.1 | async-start | bytes 6291456 | tf_op jit(solution)/shard_map/all_to_all | solution.py:360
  71.4 3.7 %collective-permute-start.2 = (f32[6,128,128]{2,1,0:T(8,128)}, f32[6,128,128]{2,1,0:T(8,128)}, u32[]{:S(2)}, u32[]{:S(2)}) collective-permute-start(f32[6,128,128]{2,1,0:T(8,128)} %get-tuple-element.14), channel_id=1, source_target_pairs={{0,1},{1,2},{2,3},{3,4},{4,5},{5,6},{6,7},{7,8},{8,9},{9,10},{10,1... | collective-permute-start | bytes 1179656 | tf_op jit(solution)/shard_map/ppermute | solution.py:365
  75.1 1.9 %collective-permute-start.3 = (f32[6,128,128]{2,1,0:T(8,128)}, f32[6,128,128]{2,1,0:T(8,128)}, u32[]{:S(2)}, u32[]{:S(2)}) collective-permute-start(f32[6,128,128]{2,1,0:T(8,128)} %get-tuple-element.15), channel_id=1, source_target_pairs={{1,0},{2,1},{3,2},{4,3},{5,4},{6,5},{7,6},{8,7},{9,8},{10,9},{11,1... | collective-permute-start | bytes 1179656 | tf_op jit(solution)/shard_map/ppermute | solution.py:366
  77.0 1.7 %spill.1 = (f32[6,1040,128]{2,1,0:T(8,128)S(1)}, f32[6,1024,128]{2,1,0:T(8,128)}) custom-call(f32[6,1040,128]{2,1,0:T(8,128)S(1)} %get-tuple-element.11.field), custom_call_target="tpu_custom_call", output_to_operand_aliasing={{0}: (0, {})} | custom-call | flops 1000000 | bytes 3145728 | tf_op jit(solution)/shard_map/spill/pallas_call | solution.py:304
  78.7 15.2 %advance_end.1.refs_0_ = f32[6,1040,128]{2,1,0:T(8,128)S(1)} custom-call(f32[6,36]{1,0:T(8,128)} %reshape_squeeze.9.coupling.refs_4_.refs_1_, s32[1,64]{1,0:T(1,128)} %refs_2_.1, f32[6,8,128,128]{3,2,1,0:T(8,128)} %bitcast.26, f32[6,8,128,128]{3,2,1,0:T(8,128)} %bitcast.19, f32[6,8,128,128]{3,2,1,0:T(8,128)} %bitcast.21, f32[8,128,128]{2,1,0:T(8,128)} %bitcast.24), custom_call_target="tpu_custom_call" | custom-call | flops 60000000 | bytes 41943040 | tf_op jit(solution)/shard_map/advance_end/pallas_call | solution.py:344
  94.0 16.0 %collective-permute-done.2.refs_5_ = f32[6,128,128]{2,1,0:T(8,128)} collective-permute-done((f32[6,128,128]{2,1,0:T(8,128)}, f32[6,128,128]{2,1,0:T(8,128)}, u32[]{:S(2)}, u32[]{:S(2)}) %collective-permute-start.2) | collective-permute-done | bytes 393248 | tf_op jit(solution)/shard_map/ppermute | solution.py:365
  109.9 1.7 %collective-permute-done.3.refs_6_ = f32[6,128,128]{2,1,0:T(8,128)} collective-permute-done((f32[6,128,128]{2,1,0:T(8,128)}, f32[6,128,128]{2,1,0:T(8,128)}, u32[]{:S(2)}, u32[]{:S(2)}) %collective-permute-start.3) | collective-permute-done | bytes 393248 | tf_op jit(solution)/shard_map/ppermute | solution.py:366
  111.7 1.3 %all-to-all-done.1.refs_4_ = f32[128,48,128]{2,1,0:T(8,128)} async-done(((f32[128,48,128]{2,1,0:T(8,128)}), f32[128,48,128]{2,1,0:T(8,128)}, u32[]{:S(2)}, u32[]{:S(2)}) %all-to-all-start.1) | async-done | bytes 3145760 | tf_op jit(solution)/shard_map/all_to_all | solution.py:360
  113.0 4.4 %finish.1 = (f32[6,1040,128]{2,1,0:T(8,128)S(1)}, f32[6,1024,128]{2,1,0:T(8,128)}) custom-call(f32[6,1040,128]{2,1,0:T(8,128)S(1)} %advance_end.1.refs_0_, f32[6,36]{1,0:T(8,128)} %reshape_squeeze.9.coupling.refs_4_.refs_1_, s32[1,64]{1,0:T(1,128)} %refs_2_.1, s32[4,256]{1,0:T(4,128)} %reshape_squeeze.10.refs_6_.refs_3_, ...), custom_call_target="tpu_custom_call", output_to_operand_aliasing={{0}: (0, {})} | custom-call | flops 100000000 | bytes 10485760 | tf_op jit(solution)/shard_map/finish/pallas_call | solution.py:304
Async XLA Ops:
  4.3 19.6 %copy-start = (f32[1,6,6,6]{3,0,2,1:T(1,128)S(1)}, f32[1,6,6,6]{3,0,2,1:T(1,128)}, u32[]{:S(2)}) copy-start(f32[1,6,6,6]{3,0,2,1:T(1,128)} %param.12) | copy-start | bytes 2596
  4.3 20.3 %copy-start.1 = (s32[1,128,8]{1,2,0:T(8,128)S(1)}, s32[1,128,8]{1,2,0:T(8,128)}, u32[]{:S(2)}) copy-start(s32[1,128,8]{1,2,0:T(8,128)} %param.16) | copy-start | bytes 12292
  4.3 53.5 %all-to-all-start = ((f32[128,48,128]{2,1,0:T(8,128)}), f32[128,48,128]{2,1,0:T(8,128)}, u32[]{:S(2)}, u32[]{:S(2)}) async-start(f32[128,48,128]{2,1,0:T(8,128)} %pack.1), calls=%async_computation | async-start | bytes 6291456 | tf_op jit(solution)/shard_map/all_to_all | solution.py:360
  18.3 38.2 %collective-permute-start.1 = (f32[6,128,128]{2,1,0:T(8,128)}, f32[6,128,128]{2,1,0:T(8,128)}, u32[]{:S(2)}, u32[]{:S(2)}) collective-permute-start(f32[6,128,128]{2,1,0:T(8,128)} %get-tuple-element.17), channel_id=1, source_target_pairs={{1,0},{2,1},{3,2},{4,3},{5,4},{6,5},{7,6},{8,7},{9,8},{10,9},{11,1... | collective-permute-start | bytes 1179656 | tf_op jit(solution)/shard_map/ppermute | solution.py:366
  21.3 35.2 %collective-permute-start = (f32[6,128,128]{2,1,0:T(8,128)}, f32[6,128,128]{2,1,0:T(8,128)}, u32[]{:S(2)}, u32[]{:S(2)}) collective-permute-start(f32[6,128,128]{2,1,0:T(8,128)} %get-tuple-element.18), channel_id=1, source_target_pairs={{0,1},{1,2},{2,3},{3,4},{4,5},{5,6},{6,7},{7,8},{8,9},{9,10},{10,1... | collective-permute-start | bytes 1179656 | tf_op jit(solution)/shard_map/ppermute | solution.py:365
  63.1 49.9 %all-to-all-start.1 = ((f32[128,48,128]{2,1,0:T(8,128)}), f32[128,48,128]{2,1,0:T(8,128)}, u32[]{:S(2)}, u32[]{:S(2)}) async-start(f32[128,48,128]{2,1,0:T(8,128)} %get-tuple-element.13), calls=%async_computation.1 | async-start | bytes 6291456 | tf_op jit(solution)/shard_map/all_to_all | solution.py:360
  71.4 38.5 %collective-permute-start.2 = (f32[6,128,128]{2,1,0:T(8,128)}, f32[6,128,128]{2,1,0:T(8,128)}, u32[]{:S(2)}, u32[]{:S(2)}) collective-permute-start(f32[6,128,128]{2,1,0:T(8,128)} %get-tuple-element.14), channel_id=1, source_target_pairs={{0,1},{1,2},{2,3},{3,4},{4,5},{5,6},{6,7},{7,8},{8,9},{9,10},{10,1... | collective-permute-start | bytes 1179656 | tf_op jit(solution)/shard_map/ppermute | solution.py:365
  75.1 36.6 %collective-permute-start.3 = (f32[6,128,128]{2,1,0:T(8,128)}, f32[6,128,128]{2,1,0:T(8,128)}, u32[]{:S(2)}, u32[]{:S(2)}) collective-permute-start(f32[6,128,128]{2,1,0:T(8,128)} %get-tuple-element.15), channel_id=1, source_target_pairs={{1,0},{2,1},{3,2},{4,3},{5,4},{6,5},{7,6},{8,7},{9,8},{10,9},{11,1... | collective-permute-start | bytes 1179656 | tf_op jit(solution)/shard_map/ppermute | solution.py:366

commit v6 on v5

--- a/solution.py
+++ b/solution.py
@@ -24,6 +24,7 @@
 EDGE = 8
 BATCH = 4
 HALF = 3
+LOADS = 4
 WHOLE_VMEM = 67_000_000
 VMEM_LIMIT = 63_500_000
 F32 = jnp.float32
@@ -93,7 +94,7 @@
     slot_ids = lax.broadcasted_iota(jnp.int32, (SLOTS, BLOCKS * CAP), 0)
     for j in range(OTHERS):
         onehot = (slots[pl.ds(other(j), 1), :] == slot_ids).astype(F32).astype(jnp.bfloat16)
-        loads[j].wait()
+        wait_all(loads[j * LOADS : (j + 1) * LOADS])
         for v in range(NVAR):
             part = data[j * BLOCKS : (j + 1) * BLOCKS, v * CAP : (v + 1) * CAP, :].reshape(BLOCKS * CAP, CZ)
             high = part.astype(jnp.bfloat16)
@@ -163,7 +164,12 @@
     first = [(coupling, coupling_s), (below, below_v), (above, above_v)]
     first += [(volume.at[0], volume_v.at[0]), (volume.at[CX - 1], volume_v.at[1])]
     first += [(slots, slots_v), (rows, rows_s)]
-    loads = [(block_of(arrived, j), part_of(data, j)) for j in range(OTHERS)]
+    size = BLOCKS // LOADS
+    loads = []
+    for j in range(OTHERS):
+        for i in range(LOADS):
+            span = pl.ds(i * size, size)
+            loads.append((block_of(arrived, j).at[span], part_of(data, j).at[span]))
     first = copies_of(first, sems)
     loads = copies_of(loads, sems, len(first))
     start_all(first + loads)
@@ -174,23 +180,21 @@
 
 def middle_kernel(*refs):
     tables, inputs, refs = refs[:3], refs[4:11], refs[11:]
-    field, sent, low, high, refs = *refs[:4], refs[4:]
+    field, sent, refs = *refs[:2], refs[2:]
     table_scratch, scratch, (sems, table_sems, sent_sems) = refs[:3], refs[3:11], refs[11:]
     table_copies = copies_of(list(zip(tables, table_scratch)), table_sems)
     start_all(table_copies)
     arrive(inputs, scratch, sems, field, TIME_STEP)
     patch_rows(field, scratch[1], scratch[4], TIME_STEP, range(NVAR))
-    stores = copies_of([(inner(field, 0, CY), low), (inner(field, ROWS - CY, CY), high)], sems)
-    start_all(stores)
     wait_all(table_copies)
     wait_all(gather_rows(field, table_scratch, scratch[3], sent, sent_sems))
+
+
+def spill_kernel(field, held, mid, low, high, sems):
+    pairs = [(inner(held, 0, CY), low), (inner(held, ROWS - CY, CY), high), (inner(held), mid)]
+    stores = copies_of(pairs, sems)
+    start_all(stores)
     wait_all(stores)
-
-
-def spill_kernel(field, held, mid, sem):
-    store = pltpu.make_async_copy(inner(held), mid, sem)
-    store.start()
-    store.wait()
 
 
 def finish_kernel(*refs):
@@ -290,7 +294,7 @@
     pltpu.VMEM((NVAR, CY, CZ), F32),
     pltpu.VMEM((NVAR, CY, CZ), F32),
     pltpu.VMEM((2, CY, CZ), F32),
-    DMA((10,)),
+    DMA((7 + OTHERS * LOADS,)),
 ]
 
 
@@ -325,14 +329,14 @@
 def middle(tables, field, inputs):
     return call(
         middle_kernel, "middle", [*tables, field, *inputs],
-        [FIELD_V, shape(PEERS, PACK, CZ), shape(NVAR, CY, CZ), shape(NVAR, CY, CZ)],
+        [FIELD_V, shape(PEERS, PACK, CZ)],
         [*TABLES, *ARRIVE, DMA((3,)), DMA((PIECES,))], 16 << 20, 10**8, VMEM_LIMIT, 3,
     )
 
 
 def spill(field):
-    out_shape = [FIELD_V, shape(NVAR, ROWS, CZ)]
-    return call(spill_kernel, "spill", [field], out_shape, [DMA(())], 3 << 20, 10**6, VMEM_LIMIT, 0)[1]
+    out_shape = [FIELD_V, shape(NVAR, ROWS, CZ), shape(NVAR, CY, CZ), shape(NVAR, CY, CZ)]
+    return call(spill_kernel, "spill", [field], out_shape, [DMA((3,))], 3 << 20, 10**6, VMEM_LIMIT, 0)[1:]
 
 
 def finish(field, inputs):
@@ -380,9 +384,9 @@
     arrived = exchange(pack(tables, start.reshape(tiled)))
     below, above = halos(start[:, 0], start[:, -1])
     field = advance(False, matrices, fringe_row, start, [source], volume)
-    field, sent, low, high = middle(tables, field, [matrices, fringe_row, slots, arrived, below, above, volume])
+    field, sent = middle(tables, field, [matrices, fringe_row, slots, arrived, below, above, volume])
     arrived = exchange(sent)
-    mid = spill(field)
+    mid, low, high = spill(field)
     below, above = halos(low, high)
     field = advance(True, matrices, fringe_row, mid.reshape(NVAR, CX, CY, CZ), [start, source], volume)
     end = finish(field, [matrices, fringe_row, slots, arrived, below, above, volume])

time: 118 us -> 118 us (level)
  no operation moved by 1% of the time
where the time goes in v6:
time: 118 us
  Pallas kernels  46.1 us (39%)
  waiting for transfers between devices  36.3 us (31%)
  starting transfers between devices  31.4 us (27%)
  local copies, waits for them, and re-layouts  3.53 us (3%)
    pallas_call x2, Pallas kernels, advance(): pl.pallas_call(functools.partial(flux_kernel, second), grid=(CX,), in_spe...  30.1 us
    all_to_all x2, starting transfers between devices, exchange(): lax.all_to_all(sent, ('comp', 'blk'), split_axis=0, concat_axis=0, tiled=...  20.3 us
    ppermute x2, waiting for transfers between devices, halos(): above = lax.ppermute(low, 'blk', [(i + 1, i) for i in range(count - 1)])  17.8 us
    pallas_call x4, Pallas kernels, call(): pl.pallas_call(kernel, in_specs=specs, out_specs=out_specs, out_shape=out...  16 us
    ppermute x2, waiting for transfers between devices, halos(): below = lax.ppermute(high, 'blk', [(i, i + 1) for i in range(count - 1)])  16 us
    ppermute x2, starting transfers between devices, halos(): below = lax.ppermute(high, 'blk', [(i, i + 1) for i in range(count - 1)])  6.2 us
    ppermute x2, starting transfers between devices, halos(): above = lax.ppermute(low, 'blk', [(i + 1, i) for i in range(count - 1)])  4.95 us
    all_to_all x2, waiting for transfers between devices, exchange(): lax.all_to_all(sent, ('comp', 'blk'), split_axis=0, concat_axis=0, tiled=...  2.57 us
  transfers between devices with their start and end apart: 6, of which 5 were waited for; matrix products, arithmetic and copies ran while one was open for 3% of the time, Pallas kernels for 27%

profile of v6, /device:TPU:1, one launch (start us, length us, event | category | flops | bytes accessed | tf_op | source)
XLA Modules:
  0.0 117.5 jit_solution(9560064219720222511)
XLA Ops:
  0.0 4.3 %pack.1 = f32[128,48,128]{2,1,0:T(8,128)} custom-call(s32[8,128]{1,0:T(8,128)} %bitcast.27, s32[1,128]{1,0:T(1,128)} %refs_1_.1, f32[8,128]{1,0:T(8,128)} %bitcast.29, f32[6,1024,128]{2,1,0:T(8,128)} %bitcast.16), custom_call_target="tpu_custom_call" | custom-call | flops 1000000 | bytes 8388608 | tf_op jit(solution)/shard_map/pack/pallas_call | solution.py:308
  4.3 0.0 copy-start
  4.3 0.0 copy-start.1
  4.3 11.9 %all-to-all-start = ((f32[128,48,128]{2,1,0:T(8,128)}), f32[128,48,128]{2,1,0:T(8,128)}, u32[]{:S(2)}, u32[]{:S(2)}) async-start(f32[128,48,128]{2,1,0:T(8,128)} %pack.1), calls=%async_computation | async-start | bytes 6291456 | tf_op jit(solution)/shard_map/all_to_all | solution.py:364
  16.2 2.1 %slice_bitcast_fusion = (f32[6,128,128]{2,1,0:T(8,128)}, f32[6,128,128]{2,1,0:T(8,128)}) fusion(f32[6,8,128,128]{3,2,1,0:T(8,128)} %bitcast.17), kind=kLoop, calls=%fused_computation | loop fusion | bytes 1572864 | tf_op jit(solution)/shard_map/squeeze | solution.py:385
  18.3 3.0 %collective-permute-start.1 = (f32[6,128,128]{2,1,0:T(8,128)}, f32[6,128,128]{2,1,0:T(8,128)}, u32[]{:S(2)}, u32[]{:S(2)}) collective-permute-start(f32[6,128,128]{2,1,0:T(8,128)} %get-tuple-element.17), channel_id=1, source_target_pairs={{1,0},{2,1},{3,2},{4,3},{5,4},{6,5},{7,6},{8,7},{9,8},{10,9},{11,1... | collective-permute-start | bytes 1179656 | tf_op jit(solution)/shard_map/ppermute | solution.py:370
  21.3 2.5 %collective-permute-start = (f32[6,128,128]{2,1,0:T(8,128)}, f32[6,128,128]{2,1,0:T(8,128)}, u32[]{:S(2)}, u32[]{:S(2)}) collective-permute-start(f32[6,128,128]{2,1,0:T(8,128)} %get-tuple-element.18), channel_id=1, source_target_pairs={{0,1},{1,2},{2,3},{3,4},{4,5},{5,6},{6,7},{7,8},{8,9},{9,10},{10,1... | collective-permute-start | bytes 1179656 | tf_op jit(solution)/shard_map/ppermute | solution.py:369
  23.9 0.0 copy-done
  23.9 0.1 reduce
  23.9 0.7 reshape_squeeze.9.coupling.refs_4_.refs_1_
  24.6 0.0 copy-done.1
  24.6 0.1 copy.14
  24.7 0.7 reshape_squeeze.10.refs_6_.refs_3_
  25.4 14.8 %advance_mid.1.refs_3_ = f32[6,1040,128]{2,1,0:T(8,128)S(1)} custom-call(f32[6,36]{1,0:T(8,128)} %reshape_squeeze.9.coupling.refs_4_.refs_1_, s32[1,64]{1,0:T(1,128)} %refs_2_.1, f32[6,8,128,128]{3,2,1,0:T(8,128)} %bitcast.18, f32[6,8,128,128]{3,2,1,0:T(8,128)} %bitcast.20, f32[8,128,128]{2,1,0:T(8,128)} %bitcast.22), custom_call_target="tpu_custom_call" | custom-call | flops 60000000 | bytes 41943040 | tf_op jit(solution)/shard_map/advance_mid/pallas_call | solution.py:348
  40.2 16.3 %collective-permute-done.1.refs_9_ = f32[6,128,128]{2,1,0:T(8,128)} collective-permute-done((f32[6,128,128]{2,1,0:T(8,128)}, f32[6,128,128]{2,1,0:T(8,128)}, u32[]{:S(2)}, u32[]{:S(2)}) %collective-permute-start.1) | collective-permute-done | bytes 393248 | tf_op jit(solution)/shard_map/ppermute | solution.py:370
  56.5 0.0 collective-permute-done.refs_8_
  56.5 1.3 %all-to-all-done.refs_7_ = f32[128,48,128]{2,1,0:T(8,128)} async-done(((f32[128,48,128]{2,1,0:T(8,128)}), f32[128,48,128]{2,1,0:T(8,128)}, u32[]{:S(2)}, u32[]{:S(2)}) %all-to-all-start) | async-done | bytes 3145760 | tf_op jit(solution)/shard_map/all_to_all | solution.py:364
  57.8 5.4 %middle.1 = (f32[6,1040,128]{2,1,0:T(8,128)S(1)}, f32[128,48,128]{2,1,0:T(8,128)}) custom-call(s32[8,128]{1,0:T(8,128)} %bitcast.28, s32[1,128]{1,0:T(1,128)} %refs_1_.1, f32[8,128]{1,0:T(8,128)} %bitcast.30, f32[6,1040,128]{2,1,0:T(8,128)S(1)} %advance_mid.1.refs_3_, ...), custom_call_target="tpu_custom_call", output_to_operand_aliasing={{0}: (3, {})} | custom-call | flops 100000000 | bytes 16777216 | tf_op jit(solution)/shard_map/middle/pallas_call | solution.py:308
  63.1 8.4 %all-to-all-start.1 = ((f32[128,48,128]{2,1,0:T(8,128)}), f32[128,48,128]{2,1,0:T(8,128)}, u32[]{:S(2)}, u32[]{:S(2)}) async-start(f32[128,48,128]{2,1,0:T(8,128)} %get-tuple-element.13), calls=%async_computation.1 | async-start | bytes 6291456 | tf_op jit(solution)/shard_map/all_to_all | solution.py:364
  71.5 1.9 %spill.1 = (f32[6,1040,128]{2,1,0:T(8,128)S(1)}, f32[6,1024,128]{2,1,0:T(8,128)}, f32[6,128,128]{2,1,0:T(8,128)}, f32[6,128,128]{2,1,0:T(8,128)}) custom-call(f32[6,1040,128]{2,1,0:T(8,128)S(1)} %get-tuple-element.11.field), custom_call_target="tpu_custom_call", output_to_operand_aliasing={{0}: (0, {})} | custom-call | flops 1000000 | bytes 3145728 | tf_op jit(solution)/shard_map/spill/pallas_call | solution.py:308
  73.5 3.7 %collective-permute-start.2 = (f32[6,128,128]{2,1,0:T(8,128)}, f32[6,128,128]{2,1,0:T(8,128)}, u32[]{:S(2)}, u32[]{:S(2)}) collective-permute-start(f32[6,128,128]{2,1,0:T(8,128)} %get-tuple-element.14), channel_id=1, source_target_pairs={{0,1},{1,2},{2,3},{3,4},{4,5},{5,6},{6,7},{7,8},{8,9},{9,10},{10,1... | collective-permute-start | bytes 1179656 | tf_op jit(solution)/shard_map/ppermute | solution.py:369
  77.1 1.9 %collective-permute-start.3 = (f32[6,128,128]{2,1,0:T(8,128)}, f32[6,128,128]{2,1,0:T(8,128)}, u32[]{:S(2)}, u32[]{:S(2)}) collective-permute-start(f32[6,128,128]{2,1,0:T(8,128)} %get-tuple-element.15), channel_id=1, source_target_pairs={{1,0},{2,1},{3,2},{4,3},{5,4},{6,5},{7,6},{8,7},{9,8},{10,9},{11,1... | collective-permute-start | bytes 1179656 | tf_op jit(solution)/shard_map/ppermute | solution.py:370
  79.0 15.2 %advance_end.1.refs_0_ = f32[6,1040,128]{2,1,0:T(8,128)S(1)} custom-call(f32[6,36]{1,0:T(8,128)} %reshape_squeeze.9.coupling.refs_4_.refs_1_, s32[1,64]{1,0:T(1,128)} %refs_2_.1, f32[6,8,128,128]{3,2,1,0:T(8,128)} %bitcast.26, f32[6,8,128,128]{3,2,1,0:T(8,128)} %bitcast.19, f32[6,8,128,128]{3,2,1,0:T(8,128)} %bitcast.21, f32[8,128,128]{2,1,0:T(8,128)} %bitcast.24), custom_call_target="tpu_custom_call" | custom-call | flops 60000000 | bytes 41943040 | tf_op jit(solution)/shard_map/advance_end/pallas_call | solution.py:348
  94.3 16.0 %collective-permute-done.2.refs_5_ = f32[6,128,128]{2,1,0:T(8,128)} collective-permute-done((f32[6,128,128]{2,1,0:T(8,128)}, f32[6,128,128]{2,1,0:T(8,128)}, u32[]{:S(2)}, u32[]{:S(2)}) %collective-permute-start.2) | collective-permute-done | bytes 393248 | tf_op jit(solution)/shard_map/ppermute | solution.py:369
  110.3 1.5 %collective-permute-done.3.refs_6_ = f32[6,128,128]{2,1,0:T(8,128)} collective-permute-done((f32[6,128,128]{2,1,0:T(8,128)}, f32[6,128,128]{2,1,0:T(8,128)}, u32[]{:S(2)}, u32[]{:S(2)}) %collective-permute-start.3) | collective-permute-done | bytes 393248 | tf_op jit(solution)/shard_map/ppermute | solution.py:370
  111.8 1.3 %all-to-all-done.1.refs_4_ = f32[128,48,128]{2,1,0:T(8,128)} async-done(((f32[128,48,128]{2,1,0:T(8,128)}), f32[128,48,128]{2,1,0:T(8,128)}, u32[]{:S(2)}, u32[]{:S(2)}) %all-to-all-start.1) | async-done | bytes 3145760 | tf_op jit(solution)/shard_map/all_to_all | solution.py:364
  113.0 4.5 %finish.1 = (f32[6,1040,128]{2,1,0:T(8,128)S(1)}, f32[6,1024,128]{2,1,0:T(8,128)}) custom-call(f32[6,1040,128]{2,1,0:T(8,128)S(1)} %advance_end.1.refs_0_, f32[6,36]{1,0:T(8,128)} %reshape_squeeze.9.coupling.refs_4_.refs_1_, s32[1,64]{1,0:T(1,128)} %refs_2_.1, s32[4,256]{1,0:T(4,128)} %reshape_squeeze.10.refs_6_.refs_3_, ...), custom_call_target="tpu_custom_call", output_to_operand_aliasing={{0}: (0, {})} | custom-call | flops 100000000 | bytes 10485760 | tf_op jit(solution)/shard_map/finish/pallas_call | solution.py:308
Async XLA Ops:
  4.3 19.6 %copy-start = (f32[1,6,6,6]{3,0,2,1:T(1,128)S(1)}, f32[1,6,6,6]{3,0,2,1:T(1,128)}, u32[]{:S(2)}) copy-start(f32[1,6,6,6]{3,0,2,1:T(1,128)} %param.12) | copy-start | bytes 2596
  4.3 20.3 %copy-start.1 = (s32[1,128,8]{1,2,0:T(8,128)S(1)}, s32[1,128,8]{1,2,0:T(8,128)}, u32[]{:S(2)}) copy-start(s32[1,128,8]{1,2,0:T(8,128)} %param.16) | copy-start | bytes 12292
  4.3 53.5 %all-to-all-start = ((f32[128,48,128]{2,1,0:T(8,128)}), f32[128,48,128]{2,1,0:T(8,128)}, u32[]{:S(2)}, u32[]{:S(2)}) async-start(f32[128,48,128]{2,1,0:T(8,128)} %pack.1), calls=%async_computation | async-start | bytes 6291456 | tf_op jit(solution)/shard_map/all_to_all | solution.py:364
  18.3 38.2 %collective-permute-start.1 = (f32[6,128,128]{2,1,0:T(8,128)}, f32[6,128,128]{2,1,0:T(8,128)}, u32[]{:S(2)}, u32[]{:S(2)}) collective-permute-start(f32[6,128,128]{2,1,0:T(8,128)} %get-tuple-element.17), channel_id=1, source_target_pairs={{1,0},{2,1},{3,2},{4,3},{5,4},{6,5},{7,6},{8,7},{9,8},{10,9},{11,1... | collective-permute-start | bytes 1179656 | tf_op jit(solution)/shard_map/ppermute | solution.py:370
  21.3 35.2 %collective-permute-start = (f32[6,128,128]{2,1,0:T(8,128)}, f32[6,128,128]{2,1,0:T(8,128)}, u32[]{:S(2)}, u32[]{:S(2)}) collective-permute-start(f32[6,128,128]{2,1,0:T(8,128)} %get-tuple-element.18), channel_id=1, source_target_pairs={{0,1},{1,2},{2,3},{3,4},{4,5},{5,6},{6,7},{7,8},{8,9},{9,10},{10,1... | collective-permute-start | bytes 1179656 | tf_op jit(solution)/shard_map/ppermute | solution.py:369
  63.1 49.9 %all-to-all-start.1 = ((f32[128,48,128]{2,1,0:T(8,128)}), f32[128,48,128]{2,1,0:T(8,128)}, u32[]{:S(2)}, u32[]{:S(2)}) async-start(f32[128,48,128]{2,1,0:T(8,128)} %get-tuple-element.13), calls=%async_computation.1 | async-start | bytes 6291456 | tf_op jit(solution)/shard_map/all_to_all | solution.py:364
  73.5 36.8 %collective-permute-start.2 = (f32[6,128,128]{2,1,0:T(8,128)}, f32[6,128,128]{2,1,0:T(8,128)}, u32[]{:S(2)}, u32[]{:S(2)}) collective-permute-start(f32[6,128,128]{2,1,0:T(8,128)} %get-tuple-element.14), channel_id=1, source_target_pairs={{0,1},{1,2},{2,3},{3,4},{4,5},{5,6},{6,7},{7,8},{8,9},{9,10},{10,1... | collective-permute-start | bytes 1179656 | tf_op jit(solution)/shard_map/ppermute | solution.py:369
  77.1 34.6 %collective-permute-start.3 = (f32[6,128,128]{2,1,0:T(8,128)}, f32[6,128,128]{2,1,0:T(8,128)}, u32[]{:S(2)}, u32[]{:S(2)}) collective-permute-start(f32[6,128,128]{2,1,0:T(8,128)} %get-tuple-element.15), channel_id=1, source_target_pairs={{1,0},{2,1},{3,2},{4,3},{5,4},{6,5},{7,6},{8,7},{9,8},{10,9},{11,1... | collective-permute-start | bytes 1179656 | tf_op jit(solution)/shard_map/ppermute | solution.py:370

commit v7 on v5

--- a/solution.py
+++ b/solution.py
@@ -22,7 +22,7 @@
 PIECES = OTHERS * SPLIT
 BAND = 32
 EDGE = 8
-BATCH = 4
+BATCH = 8
 HALF = 3
 WHOLE_VMEM = 67_000_000
 VMEM_LIMIT = 63_500_000
@@ -82,7 +82,7 @@
                 buf[piece * size + b, v * CAP : (v + 1) * CAP, :] = rows * scale
             return carry
 
-        lax.fori_loop(0, size, peer_rows, 0, unroll=4)
+        lax.fori_loop(0, size, peer_rows, 0, unroll=8)
         ready = buf.at[pl.ds(piece * size, size)]
         stores.append(pltpu.make_async_copy(ready, sent.at[pl.ds(first, size)], sems.at[piece]))
         stores[-1].start()
@@ -160,16 +160,16 @@
 def arrive(inputs, scratch, sems, field, scale):
     coupling, rows, slots, arrived, below, above, volume = inputs
     coupling_s, rows_s, slots_v, data, total, below_v, above_v, volume_v = scratch
-    first = [(coupling, coupling_s), (below, below_v), (above, above_v)]
-    first += [(volume.at[0], volume_v.at[0]), (volume.at[CX - 1], volume_v.at[1])]
-    first += [(slots, slots_v), (rows, rows_s)]
-    loads = [(block_of(arrived, j), part_of(data, j)) for j in range(OTHERS)]
-    first = copies_of(first, sems)
-    loads = copies_of(loads, sems, len(first))
-    start_all(first + loads)
-    wait_all(first)
+    loads = [(slots, slots_v)] + [(block_of(arrived, j), part_of(data, j)) for j in range(OTHERS)]
+    others = [(coupling, coupling_s), (rows, rows_s), (below, below_v), (above, above_v)]
+    others += [(volume.at[0], volume_v.at[0]), (volume.at[CX - 1], volume_v.at[1])]
+    loads = copies_of(loads, sems)
+    others = copies_of(others, sems, len(loads))
+    start_all(loads + others)
+    loads[0].wait()
+    reduce_rows(slots_v, loads[1:], data, total)
+    wait_all(others)
     add_halos(field, coupling_s, below_v, above_v, volume_v, scale)
-    reduce_rows(slots_v, loads, data, total)
 
 
 def middle_kernel(*refs):

time: 118 us -> 118 us (level)
  no operation moved by 1% of the time
where the time goes in v7:
time: 118 us; the launch traced here: 117 us
  Pallas kernels  45.4 us (38%)
  waiting for transfers between devices  36.5 us (31%)
  starting transfers between devices  31.4 us (27%)
  local copies, waits for them, and re-layouts  3.53 us (3%)
    pallas_call x2, Pallas kernels, advance(): pl.pallas_call(functools.partial(flux_kernel, second), grid=(CX,), in_spe...  30.1 us
    all_to_all x2, starting transfers between devices, exchange(): lax.all_to_all(sent, ('comp', 'blk'), split_axis=0, concat_axis=0, tiled=...  20.2 us
    ppermute x2, waiting for transfers between devices, halos(): above = lax.ppermute(low, 'blk', [(i + 1, i) for i in range(count - 1)])  18 us
    ppermute x2, waiting for transfers between devices, halos(): below = lax.ppermute(high, 'blk', [(i, i + 1) for i in range(count - 1)])  16 us
    pallas_call x4, Pallas kernels, call(): pl.pallas_call(kernel, in_specs=specs, out_specs=out_specs, out_shape=out...  15.4 us
    ppermute x2, starting transfers between devices, halos(): below = lax.ppermute(high, 'blk', [(i, i + 1) for i in range(count - 1)])  6.2 us
    ppermute x2, starting transfers between devices, halos(): above = lax.ppermute(low, 'blk', [(i + 1, i) for i in range(count - 1)])  4.95 us
    all_to_all x2, waiting for transfers between devices, exchange(): lax.all_to_all(sent, ('comp', 'blk'), split_axis=0, concat_axis=0, tiled=...  2.57 us
  transfers between devices with their start and end apart: 6, of which 5 were waited for; matrix products, arithmetic and copies ran while one was open for 3% of the time, Pallas kernels for 27%

profile of v7, /device:TPU:1, one launch (start us, length us, event | category | flops | bytes accessed | tf_op | source)
XLA Modules:
  0.0 117.1 jit_solution(15171987321029259794)
XLA Ops:
  0.0 4.0 %pack.1 = f32[128,48,128]{2,1,0:T(8,128)} custom-call(s32[8,128]{1,0:T(8,128)} %bitcast.27, s32[1,128]{1,0:T(1,128)} %refs_1_.1, f32[8,128]{1,0:T(8,128)} %bitcast.29, f32[6,1024,128]{2,1,0:T(8,128)} %bitcast.16), custom_call_target="tpu_custom_call" | custom-call | flops 1000000 | bytes 8388608 | tf_op jit(solution)/shard_map/pack/pallas_call | solution.py:304
  4.0 0.0 copy-start
  4.0 0.0 copy-start.1
  4.0 11.9 %all-to-all-start = ((f32[128,48,128]{2,1,0:T(8,128)}), f32[128,48,128]{2,1,0:T(8,128)}, u32[]{:S(2)}, u32[]{:S(2)}) async-start(f32[128,48,128]{2,1,0:T(8,128)} %pack.1), calls=%async_computation | async-start | bytes 6291456 | tf_op jit(solution)/shard_map/all_to_all | solution.py:360
  15.9 2.1 %slice_bitcast_fusion = (f32[6,128,128]{2,1,0:T(8,128)}, f32[6,128,128]{2,1,0:T(8,128)}) fusion(f32[6,8,128,128]{3,2,1,0:T(8,128)} %bitcast.17), kind=kLoop, calls=%fused_computation | loop fusion | bytes 1572864 | tf_op jit(solution)/shard_map/squeeze | solution.py:381
  18.0 3.0 %collective-permute-start.1 = (f32[6,128,128]{2,1,0:T(8,128)}, f32[6,128,128]{2,1,0:T(8,128)}, u32[]{:S(2)}, u32[]{:S(2)}) collective-permute-start(f32[6,128,128]{2,1,0:T(8,128)} %get-tuple-element.17), channel_id=1, source_target_pairs={{1,0},{2,1},{3,2},{4,3},{5,4},{6,5},{7,6},{8,7},{9,8},{10,9},{11,1... | collective-permute-start | bytes 1179656 | tf_op jit(solution)/shard_map/ppermute | solution.py:366
  21.0 2.5 %collective-permute-start = (f32[6,128,128]{2,1,0:T(8,128)}, f32[6,128,128]{2,1,0:T(8,128)}, u32[]{:S(2)}, u32[]{:S(2)}) collective-permute-start(f32[6,128,128]{2,1,0:T(8,128)} %get-tuple-element.18), channel_id=1, source_target_pairs={{0,1},{1,2},{2,3},{3,4},{4,5},{5,6},{6,7},{7,8},{8,9},{9,10},{10,1... | collective-permute-start | bytes 1179656 | tf_op jit(solution)/shard_map/ppermute | solution.py:365
  23.6 0.0 copy-done
  23.6 0.1 reduce
  23.6 0.7 reshape_squeeze.9.coupling.refs_4_.refs_1_
  24.3 0.0 copy-done.1
  24.3 0.1 copy.14
  24.4 0.7 reshape_squeeze.10.refs_6_.refs_3_
  25.1 14.8 %advance_mid.1.refs_3_ = f32[6,1040,128]{2,1,0:T(8,128)S(1)} custom-call(f32[6,36]{1,0:T(8,128)} %reshape_squeeze.9.coupling.refs_4_.refs_1_, s32[1,64]{1,0:T(1,128)} %refs_2_.1, f32[6,8,128,128]{3,2,1,0:T(8,128)} %bitcast.18, f32[6,8,128,128]{3,2,1,0:T(8,128)} %bitcast.20, f32[8,128,128]{2,1,0:T(8,128)} %bitcast.22), custom_call_target="tpu_custom_call" | custom-call | flops 60000000 | bytes 41943040 | tf_op jit(solution)/shard_map/advance_mid/pallas_call | solution.py:344
  39.9 16.3 %collective-permute-done.1.refs_9_ = f32[6,128,128]{2,1,0:T(8,128)} collective-permute-done((f32[6,128,128]{2,1,0:T(8,128)}, f32[6,128,128]{2,1,0:T(8,128)}, u32[]{:S(2)}, u32[]{:S(2)}) %collective-permute-start.1) | collective-permute-done | bytes 393248 | tf_op jit(solution)/shard_map/ppermute | solution.py:366
  56.2 0.0 collective-permute-done.refs_8_
  56.2 1.3 %all-to-all-done.refs_7_ = f32[128,48,128]{2,1,0:T(8,128)} async-done(((f32[128,48,128]{2,1,0:T(8,128)}), f32[128,48,128]{2,1,0:T(8,128)}, u32[]{:S(2)}, u32[]{:S(2)}) %all-to-all-start) | async-done | bytes 3145760 | tf_op jit(solution)/shard_map/all_to_all | solution.py:360
  57.5 5.4 %middle.1 = (f32[6,1040,128]{2,1,0:T(8,128)S(1)}, f32[128,48,128]{2,1,0:T(8,128)}, f32[6,128,128]{2,1,0:T(8,128)}, f32[6,128,128]{2,1,0:T(8,128)}) custom-call(s32[8,128]{1,0:T(8,128)} %bitcast.28, s32[1,128]{1,0:T(1,128)} %refs_1_.1, f32[8,128]{1,0:T(8,128)} %bitcast.30, f32[6,1040,128]{2,1,0:T(8,128)S(1)} %advance_mid.1.refs_3_, ...), custom_call_target="tpu_custom_call", output_to_operand_aliasing={{0}: (3, {})} | custom-call | flops 100000000 | bytes 16777216 | tf_op jit(solution)/shard_map/middle/pallas_call | solution.py:304
  62.8 8.3 %all-to-all-start.1 = ((f32[128,48,128]{2,1,0:T(8,128)}), f32[128,48,128]{2,1,0:T(8,128)}, u32[]{:S(2)}, u32[]{:S(2)}) async-start(f32[128,48,128]{2,1,0:T(8,128)} %get-tuple-element.13), calls=%async_computation.1 | async-start | bytes 6291456 | tf_op jit(solution)/shard_map/all_to_all | solution.py:360
  71.2 3.7 %collective-permute-start.2 = (f32[6,128,128]{2,1,0:T(8,128)}, f32[6,128,128]{2,1,0:T(8,128)}, u32[]{:S(2)}, u32[]{:S(2)}) collective-permute-start(f32[6,128,128]{2,1,0:T(8,128)} %get-tuple-element.14), channel_id=1, source_target_pairs={{0,1},{1,2},{2,3},{3,4},{4,5},{5,6},{6,7},{7,8},{8,9},{9,10},{10,1... | collective-permute-start | bytes 1179656 | tf_op jit(solution)/shard_map/ppermute | solution.py:365
  74.8 1.9 %collective-permute-start.3 = (f32[6,128,128]{2,1,0:T(8,128)}, f32[6,128,128]{2,1,0:T(8,128)}, u32[]{:S(2)}, u32[]{:S(2)}) collective-permute-start(f32[6,128,128]{2,1,0:T(8,128)} %get-tuple-element.15), channel_id=1, source_target_pairs={{1,0},{2,1},{3,2},{4,3},{5,4},{6,5},{7,6},{8,7},{9,8},{10,9},{11,1... | collective-permute-start | bytes 1179656 | tf_op jit(solution)/shard_map/ppermute | solution.py:366
  76.8 1.7 %spill.1 = (f32[6,1040,128]{2,1,0:T(8,128)S(1)}, f32[6,1024,128]{2,1,0:T(8,128)}) custom-call(f32[6,1040,128]{2,1,0:T(8,128)S(1)} %get-tuple-element.11.field), custom_call_target="tpu_custom_call", output_to_operand_aliasing={{0}: (0, {})} | custom-call | flops 1000000 | bytes 3145728 | tf_op jit(solution)/shard_map/spill/pallas_call | solution.py:304
  78.5 15.2 %advance_end.1.refs_0_ = f32[6,1040,128]{2,1,0:T(8,128)S(1)} custom-call(f32[6,36]{1,0:T(8,128)} %reshape_squeeze.9.coupling.refs_4_.refs_1_, s32[1,64]{1,0:T(1,128)} %refs_2_.1, f32[6,8,128,128]{3,2,1,0:T(8,128)} %bitcast.26, f32[6,8,128,128]{3,2,1,0:T(8,128)} %bitcast.19, f32[6,8,128,128]{3,2,1,0:T(8,128)} %bitcast.21, f32[8,128,128]{2,1,0:T(8,128)} %bitcast.24), custom_call_target="tpu_custom_call" | custom-call | flops 60000000 | bytes 41943040 | tf_op jit(solution)/shard_map/advance_end/pallas_call | solution.py:344
  93.7 16.0 %collective-permute-done.2.refs_5_ = f32[6,128,128]{2,1,0:T(8,128)} collective-permute-done((f32[6,128,128]{2,1,0:T(8,128)}, f32[6,128,128]{2,1,0:T(8,128)}, u32[]{:S(2)}, u32[]{:S(2)}) %collective-permute-start.2) | collective-permute-done | bytes 393248 | tf_op jit(solution)/shard_map/ppermute | solution.py:365
  109.7 1.7 %collective-permute-done.3.refs_6_ = f32[6,128,128]{2,1,0:T(8,128)} collective-permute-done((f32[6,128,128]{2,1,0:T(8,128)}, f32[6,128,128]{2,1,0:T(8,128)}, u32[]{:S(2)}, u32[]{:S(2)}) %collective-permute-start.3) | collective-permute-done | bytes 393248 | tf_op jit(solution)/shard_map/ppermute | solution.py:366
  111.4 1.3 %all-to-all-done.1.refs_4_ = f32[128,48,128]{2,1,0:T(8,128)} async-done(((f32[128,48,128]{2,1,0:T(8,128)}), f32[128,48,128]{2,1,0:T(8,128)}, u32[]{:S(2)}, u32[]{:S(2)}) %all-to-all-start.1) | async-done | bytes 3145760 | tf_op jit(solution)/shard_map/all_to_all | solution.py:360
  112.7 4.4 %finish.1 = (f32[6,1040,128]{2,1,0:T(8,128)S(1)}, f32[6,1024,128]{2,1,0:T(8,128)}) custom-call(f32[6,1040,128]{2,1,0:T(8,128)S(1)} %advance_end.1.refs_0_, f32[6,36]{1,0:T(8,128)} %reshape_squeeze.9.coupling.refs_4_.refs_1_, s32[1,64]{1,0:T(1,128)} %refs_2_.1, s32[4,256]{1,0:T(4,128)} %reshape_squeeze.10.refs_6_.refs_3_, ...), custom_call_target="tpu_custom_call", output_to_operand_aliasing={{0}: (0, {})} | custom-call | flops 100000000 | bytes 10485760 | tf_op jit(solution)/shard_map/finish/pallas_call | solution.py:304
Async XLA Ops:
  4.0 19.6 %copy-start = (f32[1,6,6,6]{3,0,2,1:T(1,128)S(1)}, f32[1,6,6,6]{3,0,2,1:T(1,128)}, u32[]{:S(2)}) copy-start(f32[1,6,6,6]{3,0,2,1:T(1,128)} %param.12) | copy-start | bytes 2596
  4.0 20.3 %copy-start.1 = (s32[1,128,8]{1,2,0:T(8,128)S(1)}, s32[1,128,8]{1,2,0:T(8,128)}, u32[]{:S(2)}) copy-start(s32[1,128,8]{1,2,0:T(8,128)} %param.16) | copy-start | bytes 12292
  4.0 53.5 %all-to-all-start = ((f32[128,48,128]{2,1,0:T(8,128)}), f32[128,48,128]{2,1,0:T(8,128)}, u32[]{:S(2)}, u32[]{:S(2)}) async-start(f32[128,48,128]{2,1,0:T(8,128)} %pack.1), calls=%async_computation | async-start | bytes 6291456 | tf_op jit(solution)/shard_map/all_to_all | solution.py:360
  18.0 38.2 %collective-permute-start.1 = (f32[6,128,128]{2,1,0:T(8,128)}, f32[6,128,128]{2,1,0:T(8,128)}, u32[]{:S(2)}, u32[]{:S(2)}) collective-permute-start(f32[6,128,128]{2,1,0:T(8,128)} %get-tuple-element.17), channel_id=1, source_target_pairs={{1,0},{2,1},{3,2},{4,3},{5,4},{6,5},{7,6},{8,7},{9,8},{10,9},{11,1... | collective-permute-start | bytes 1179656 | tf_op jit(solution)/shard_map/ppermute | solution.py:366
  21.0 35.2 %collective-permute-start = (f32[6,128,128]{2,1,0:T(8,128)}, f32[6,128,128]{2,1,0:T(8,128)}, u32[]{:S(2)}, u32[]{:S(2)}) collective-permute-start(f32[6,128,128]{2,1,0:T(8,128)} %get-tuple-element.18), channel_id=1, source_target_pairs={{0,1},{1,2},{2,3},{3,4},{4,5},{5,6},{6,7},{7,8},{8,9},{9,10},{10,1... | collective-permute-start | bytes 1179656 | tf_op jit(solution)/shard_map/ppermute | solution.py:365
  62.8 49.9 %all-to-all-start.1 = ((f32[128,48,128]{2,1,0:T(8,128)}), f32[128,48,128]{2,1,0:T(8,128)}, u32[]{:S(2)}, u32[]{:S(2)}) async-start(f32[128,48,128]{2,1,0:T(8,128)} %get-tuple-element.13), calls=%async_computation.1 | async-start | bytes 6291456 | tf_op jit(solution)/shard_map/all_to_all | solution.py:360
  71.2 38.5 %collective-permute-start.2 = (f32[6,128,128]{2,1,0:T(8,128)}, f32[6,128,128]{2,1,0:T(8,128)}, u32[]{:S(2)}, u32[]{:S(2)}) collective-permute-start(f32[6,128,128]{2,1,0:T(8,128)} %get-tuple-element.14), channel_id=1, source_target_pairs={{0,1},{1,2},{2,3},{3,4},{4,5},{5,6},{6,7},{7,8},{8,9},{9,10},{10,1... | collective-permute-start | bytes 1179656 | tf_op jit(solution)/shard_map/ppermute | solution.py:365
  74.8 36.6 %collective-permute-start.3 = (f32[6,128,128]{2,1,0:T(8,128)}, f32[6,128,128]{2,1,0:T(8,128)}, u32[]{:S(2)}, u32[]{:S(2)}) collective-permute-start(f32[6,128,128]{2,1,0:T(8,128)} %get-tuple-element.15), channel_id=1, source_target_pairs={{1,0},{2,1},{3,2},{4,3},{5,4},{6,5},{7,6},{8,7},{9,8},{10,9},{11,1... | collective-permute-start | bytes 1179656 | tf_op jit(solution)/shard_map/ppermute | solution.py:366
